TPU v7x, 128 devices: a whole 4x4x4 slice. The times are simulated.
128 devices in a mesh: filt: 8 (over z, x_hi), space: 16 (over x_lo, y, core).
Axes of the slice: x: 4 (x_hi: 2, x_lo: 2; x = x_hi * 2 + x_lo), y: 4, z: 4, core: 2. Of those that a mesh axis runs over, the one named last changes fastest.
Arguments:
- inputs: bfloat16 [16, 256, 2048], P('space', 'filt'), may hold values from -6 to 6
- weight: bfloat16 [3, 3, 3, 256, 256], P(None, None, None, 'filt'), may hold values from -0.078125 to 0.078125
- bias: bfloat16 [256], P('filt'), may hold values from -4 to 4
- cotangent: bfloat16 [16, 256, 2048], P('space', 'filt'), may hold values from -6 to 6
Outputs:
- output: float32 [16, 256, 2048], P('space', 'filt')
- grad_inputs: float32 [16, 256, 2048], P('space', 'filt')
- grad_weight: float32 [3, 3, 3, 256, 256], P(None, None, None, 'filt')
- grad_bias: float32 [256], P('filt')
All inputs are finite; a program needn't handle non-finite values.
Results may differ from a plain program's by a relative error of at most 0.0003.
Values may be sent and summed in bfloat16 or wider, within the bound.
No kernel may reach another device: no remote copies, remote signals or barrier semaphores. Data moves between devices by JAX's collectives and lax.ppermute only.
A program may use at most 64 MiB of HBM per device.

v0:
```python
import jax
import jax.numpy as jnp
from jax import lax
from jax.sharding import PartitionSpec as P

ROWS = 32
WIDE = 64


def extended(cells, sides, width):
    for axis, dim in sides:
        count = lax.axis_size(axis)
        ends = count - 1
        head = lax.slice_in_dim(cells, 0, width, axis=dim)
        tail = lax.slice_in_dim(cells, cells.shape[dim] - width, cells.shape[dim], axis=dim)
        cells = jnp.concatenate(
            [
                lax.ppermute(tail, axis, [(i, (i + 1) % count) for i in range(ends)]),
                cells,
                lax.ppermute(head, axis, [((i + 1) % count, i) for i in range(ends)]),
            ],
            axis=dim,
        )
    return cells


def convolve_padded(padded, kernel):
    volume = padded.reshape(padded.shape[0], padded.shape[1], ROWS, WIDE)
    result = lax.conv_general_dilated(
        volume[None],
        kernel,
        (1, 1, 1),
        [(0, 0), (1, 1), (1, 1)],
        dimension_numbers=("NDCHW", "DHWIO", "NDCHW"),
        preferred_element_type=jnp.float32,
    )
    return result[0].reshape(result.shape[1], result.shape[2], ROWS * WIDE)


def body(inputs, weight, bias, cotangent):
    planes = inputs.shape[0]
    own_channels = inputs.shape[1]
    padded_in = extended(inputs, (("space", 0),), 1)
    partial_out = convolve_padded(padded_in, weight)
    summed = lax.psum_scatter(partial_out, "filt", scatter_dimension=1, tiled=True)
    output = summed + bias.astype(jnp.float32)[None, :, None]
    all_grad = lax.all_gather(cotangent, "filt", axis=1, tiled=True)
    padded_grad = extended(all_grad, (("space", 0),), 1)
    back_kernel = jnp.swapaxes(jnp.flip(weight, (0, 1, 2)), 3, 4)
    grad_inputs = convolve_padded(padded_grad, back_kernel)
    shaped_in = padded_in.reshape(planes + 2, own_channels, ROWS, WIDE)
    framed = jnp.pad(shaped_in, ((0, 0), (0, 0), (1, 1), (1, 1)))
    grad_vol = all_grad.reshape(planes, all_grad.shape[1], ROWS, WIDE)
    terms = []
    for depth_off in range(3):
        for row_off in range(3):
            for col_off in range(3):
                window = framed[
                    depth_off : depth_off + planes,
                    :,
                    row_off : row_off + ROWS,
                    col_off : col_off + WIDE,
                ]
                terms.append(
                    lax.dot_general(
                        window,
                        grad_vol,
                        (((0, 2, 3), (0, 2, 3)), ((), ())),
                        preferred_element_type=jnp.float32,
                    )
                )
    kernel_part = jnp.stack(terms).reshape(3, 3, 3, own_channels, grad_vol.shape[1])
    bias_part = jnp.sum(cotangent.astype(jnp.float32), axis=(0, 2))
    kernel_total, bias_total = lax.psum((kernel_part, bias_part), "space")
    factor = 1.0 / jnp.sqrt(jnp.float32(planes * lax.axis_size("space") * ROWS * WIDE))
    return (output, grad_inputs, kernel_total * factor, bias_total * factor)


def solution(mesh):
    placed = (
        P("space", "filt", None),
        P(None, None, None, "filt", None),
        P("filt"),
        P("space", "filt", None),
    )
    return jax.shard_map(
        body,
        mesh=mesh,
        in_specs=placed,
        out_specs=(
            P("space", "filt", None),
            P("space", "filt", None),
            P(None, None, None, "filt", None),
            P("filt"),
        ),
        check_vma=False,
    )
```

profile of v0, /device:TPU:1, one launch (start us, length us, event | category | flops | bytes accessed | tf_op | source)
XLA Modules:
  0.0 326.3 jit_solution(3926293909356311096)
XLA Ops:
  7.2 4.7 %collective-permute-start = (bf16[1,32,2048]{2,1,0:T(8,128)(2,1)}, bf16[1,32,2048]{2,1,0:T(8,128)(2,1)S(1)}, u32[]{:S(2)}, u32[]{:S(2)}) collective-permute-start(bf16[1,32,2048]{2,1,0:T(8,128)(2,1)} %param.4), channel_id=1, source_target_pairs={{0,1},{1,2},{2,3},{3,4},{4,5},{5,6},{6,7},{7,8},{8,9},{9,10},{10,1... | collective-permute-start | bytes 393224 | tf_op jit(solution)/shard_map/ppermute | solution.py:18
  12.0 1.9 collective-permute-start.1
  14.2 1.0 constant_dynamic-update-slice_fusion.1
  15.2 3.4 %collective-permute-done.1 = bf16[1,32,2048]{2,1,0:T(8,128)(2,1)S(1)} collective-permute-done((bf16[1,32,2048]{2,1,0:T(8,128)(2,1)}, bf16[1,32,2048]{2,1,0:T(8,128)(2,1)S(1)}, u32[]{:S(2)}, u32[]{:S(2)}) %collective-permute-start.1) | collective-permute-done | bytes 131104 | tf_op jit(solution)/shard_map/ppermute | solution.py:20
  18.5 0.8 reshape.169
  19.3 0.8 reshape.214
  20.5 2.1 copy.50
  22.6 3.0 pad.5.clone
  25.6 3.9 %copy.35 = bf16[3,32,32,1,8,9]{1,4,5,2,0,3:T(8,128)(2,1)} copy(bf16[3,32,32,1,8,9]{2,1,5,4,0,3:T(8,128)(2,1)} %bitcast.299) | data formatting | bytes 884736 | tf_op jit(solution)/shard_map/conv_general_dilated | solution.py:29
  29.5 1.1 slice.109
  30.7 3.9 %fusion.17 = f32[1,32,8,9,256]{4,2,3,1,0:T(8,128)S(1)} fusion(bf16[3,3,3,32,256]{4,3,2,1,0:T(8,128)(2,1)S(1)} %copy-done, bf16[3,32,32,1,7,2]{1,4,5,2,0,3:T(8,128)(2,1)S(1)} %slice.109, bf16[3,32,32,1,8,9]{1,4,5,2,0,3:T(8,128)(2,1)} %copy.35, pred[8,9]{0,1:T(8,128)(4,1)S(1)} %copy-done.9), kind=kOutput, calls=%fused_computation.19 | convolution fusion | flops 1000194048 | bytes 3330120 | tf_op jit(solution)/shard_map/conv_general_dilated | solution.py:29
  34.6 0.8 copy.36
  35.6 2.5 copy.37
  38.1 6.1 %copy.38 = f32[1,256,2048]{2,0,1:T(1,128)} copy(f32[1,256,2048]{1,2,0:T(8,128)} %bitcast.298) | data formatting | bytes 4194304 | tf_op jit(solution)/shard_map/reshape;squeeze | solution.py:37
  44.5 14.0 %all-gather.2.cloned.1.call-done = bf16[1,256,2048]{2,1,0:T(8,128)(2,1)} async-done(((bf16[1,32,2048]{2,1,0:T(8,128)(2,1)}), bf16[1,256,2048]{2,1,0:T(8,128)(2,1)}) %all-gather.2.cloned.1.call-update) | async-done | bytes 1048592 | tf_op jit(solution)/shard_map/all_gather | solution.py:47
  58.5 1.5 copy.39
  70.9 0.9 copy-done.2
  71.9 0.6 dynamic-slice
  73.1 4.2 %collective-permute-start.3 = (bf16[1,256,2048]{1,2,0:T(8,128)(2,1)S(1)}, bf16[1,256,2048]{1,2,0:T(8,128)(2,1)S(1)}, u32[]{:S(2)}, u32[]{:S(2)}) collective-permute-start(bf16[1,256,2048]{1,2,0:T(8,128)(2,1)S(1)} %copy.39), channel_id=1, source_target_pairs={{1,0},{2,1},{3,2},{4,3},{5,4},{6,5},{7,6},{8,7},{9,8},{10,9},{11,1... | collective-permute-start | bytes 3145736 | tf_op jit(solution)/shard_map/ppermute | solution.py:20
  77.3 3.0 collective-permute-start.2
  80.5 45.1 %psum.15 = f32[32]{0:T(128)S(1)} all-reduce(f32[32]{0:T(128)S(1)} %convert_reduce_fusion), channel_id=1, replica_groups=mesh['filt'=8,'space'=16] {'space'}, use_global_device_ids=true, to_apply=%region_3.4 | all-reduce | flops 32 | bytes 256 | tf_op jit(solution)/shard_map/psum | solution.py:74
  126.1 52.8 %all-reduce.7.cloned.1.call-done = f32[1,256,2048]{2,0,1:T(1,128)} async-done(((f32[1,256,2048]{2,0,1:T(1,128)}), f32[1,256,2048]{2,0,1:T(1,128)}) %all-reduce.7.cloned.1.call-update) | async-done | bytes 2097168
  178.9 1.2 dynamic-slice_add_fusion
  180.1 0.8 copy.49
  180.8 119.8 %all-reduce.5.cloned.1.call-done = f32[3,3,3,32,256]{4,3,2,1,0:T(8,128)} async-done(((f32[3,3,3,32,256]{4,3,2,1,0:T(8,128)}), f32[3,3,3,32,256]{4,3,2,1,0:T(8,128)}) %all-reduce.5.cloned.1.call-update) | async-done | bytes 884752 | tf_op jit(solution)/shard_map/psum | solution.py:74
  300.6 2.2 broadcast_multiply_fusion
  302.8 1.6 pad_maximum_fusion
  304.4 1.8 copy.51
  306.6 2.1 copy.44
  308.9 8.9 %fusion.20 = f32[1,32,8,9,32]{4,2,3,1,0:T(8,128)S(1)} fusion(bf16[3,3,3,32,256]{4,3,2,1,0:T(8,128)(2,1)S(1)} %copy-done, bf16[3,256,32,1,7,2]{1,4,5,2,0,3:T(8,128)(2,1)S(1)} %slice.111, bf16[3,256,32,1,8,9]{1,4,5,2,0,3:T(8,128)(2,1)S(1)} %copy.44, pred[8,9]{0,1:T(8,128)(4,1)S(1)} %copy-done.10), kind=kOutput, calls=%fused_computation.20 | convolution fusion | flops 1011032064 | bytes 4964424 | tf_op jit(solution)/shard_map/conv_general_dilated | solution.py:29
  318.1 0.8 copy.46
  318.8 0.9 reshape_squeeze.7
  (68 shorter events, 13.5 us)
Async XLA Ops:
  7.2 23.5 %copy-start = (bf16[3,3,3,32,256]{4,3,2,1,0:T(8,128)(2,1)S(1)}, bf16[3,3,3,32,256]{4,3,2,1,0:T(8,128)(2,1)}, u32[]{:S(2)}) copy-start(bf16[3,3,3,32,256]{4,3,2,1,0:T(8,128)(2,1)} %param.5) | copy-start | bytes 1327108
  7.2 51.4 %all-gather.2.cloned.1.call-start = ((), (), s32[]{:S(2)}) async-start(), calls=%async_computation | async-start | bytes 1179648 | tf_op jit(solution)/shard_map/all_gather | solution.py:47
  7.2 7.0 %collective-permute-start = (bf16[1,32,2048]{2,1,0:T(8,128)(2,1)}, bf16[1,32,2048]{2,1,0:T(8,128)(2,1)S(1)}, u32[]{:S(2)}, u32[]{:S(2)}) collective-permute-start(bf16[1,32,2048]{2,1,0:T(8,128)(2,1)} %param.4), channel_id=1, source_target_pairs={{0,1},{1,2},{2,3},{3,4},{4,5},{5,6},{6,7},{7,8},{8,9},{9,10},{10,1... | collective-permute-start | bytes 393224 | tf_op jit(solution)/shard_map/ppermute | solution.py:18
  12.0 166.9 %all-reduce.7.cloned.1.call-start = ((), (), s32[]{:S(2)}) async-start(), calls=%async_computation.2 | async-start | bytes 4194304
  12.0 6.5 %collective-permute-start.1 = (bf16[1,32,2048]{2,1,0:T(8,128)(2,1)}, bf16[1,32,2048]{2,1,0:T(8,128)(2,1)S(1)}, u32[]{:S(2)}, u32[]{:S(2)}) collective-permute-start(bf16[1,32,2048]{2,1,0:T(8,128)(2,1)} %param.4), channel_id=1, source_target_pairs={{1,0},{2,1},{3,2},{4,3},{5,4},{6,5},{7,6},{8,7},{9,8},{10,9},{11,1... | collective-permute-start | bytes 393224 | tf_op jit(solution)/shard_map/ppermute | solution.py:20
  14.2 4.3 %copy-start.4 = (bf16[1,32,2048]{2,1,0:T(8,128)(2,1)}, bf16[1,32,2048]{2,1,0:T(8,128)(2,1)S(1)}, u32[]{:S(2)}) copy-start(bf16[1,32,2048]{2,1,0:T(8,128)(2,1)S(1)} %collective-permute-done) | copy-start | bytes 393220
  25.6 5.1 %copy-start.9 = (pred[8,9]{0,1:T(8,128)(4,1)S(1)}, pred[8,9]{0,1:T(8,128)(4,1)}, u32[]{:S(2)}) copy-start(pred[8,9]{0,1:T(8,128)(4,1)} %constant.20) | copy-start | bytes 220
  44.3 256.4 %all-reduce.5.cloned.1.call-start = ((), (), s32[]{:S(2)}) async-start(), calls=%async_computation.1 | async-start | bytes 1769472 | tf_op jit(solution)/shard_map/psum | solution.py:74
  60.4 1.2 copy-start.1
  60.5 1.2 copy-start.5
  64.1 1.2 copy-start.3
  70.1 1.7 copy-start.7
  70.2 1.7 copy-start.8
  70.2 10.2 %copy-start.6 = (bf16[1,32,2048]{2,1,0:T(8,128)(2,1)S(1)}, bf16[1,32,2048]{2,1,0:T(8,128)(2,1)}, u32[]{:S(2)}) copy-start(bf16[1,32,2048]{2,1,0:T(8,128)(2,1)} %param.7) | copy-start | bytes 393220
  70.9 0.9 copy-start.2
  73.1 229.7 %collective-permute-start.3 = (bf16[1,256,2048]{1,2,0:T(8,128)(2,1)S(1)}, bf16[1,256,2048]{1,2,0:T(8,128)(2,1)S(1)}, u32[]{:S(2)}, u32[]{:S(2)}) collective-permute-start(bf16[1,256,2048]{1,2,0:T(8,128)(2,1)S(1)} %copy.39), channel_id=1, source_target_pairs={{1,0},{2,1},{3,2},{4,3},{5,4},{6,5},{7,6},{8,7},{9,8},{10,9},{11,1... | collective-permute-start | bytes 3145736 | tf_op jit(solution)/shard_map/ppermute | solution.py:20
  77.3 225.5 %collective-permute-start.2 = (bf16[1,256,2048]{1,2,0:T(8,128)(2,1)S(1)}, bf16[1,256,2048]{1,2,0:T(8,128)(2,1)}, u32[]{:S(2)}, u32[]{:S(2)}) collective-permute-start(bf16[1,256,2048]{1,2,0:T(8,128)(2,1)S(1)} %copy.39), channel_id=1, source_target_pairs={{0,1},{1,2},{2,3},{3,4},{4,5},{5,6},{6,7},{7,8},{8,9},{9,10},{10,1... | collective-permute-start | bytes 3145736 | tf_op jit(solution)/shard_map/ppermute | solution.py:18
  306.6 2.3 copy-start.10
Sparse Core Ops, SparseCore 0:
  12.1 46.3 all-gather.1
  61.1 117.7 all-reduce.6
  181.9 118.6 all-reduce.4
where the time goes:
time: 327 us; the launch traced here: 326 us
  waiting for transfers between devices  190 us (58%)
  blocking collectives  45.1 us (14%)
  local copies, waits for them, and re-layouts  33 us (10%)
  matrix products  23.5 us (7%)
  between operations  14.8 us (5%)
  starting transfers between devices  14.1 us (4%)
  other arithmetic  5.6 us (2%)
    psum x1, waiting for transfers between devices, body(): kernel_total, bias_total = lax.psum((kernel_part, bias_part), 'space')  120 us
    unnamed x4, waiting for transfers between devices  52.8 us
    psum x1, blocking collectives, body(): kernel_total, bias_total = lax.psum((kernel_part, bias_part), 'space')  45.1 us
    all_gather x1, waiting for transfers between devices, body(): all_grad = lax.all_gather(cotangent, 'filt', axis=1, tiled=True)  14 us
    conv_general_dilated x2, matrix products, convolve_padded(): lax.conv_general_dilated(volume[None], kernel, (1, 1, 1), [(0, 0), (1, 1)...  12.8 us
    conv_general_dilated x10, local copies, waits for them, and re-layouts, convolve_padded(): lax.conv_general_dilated(volume[None], kernel, (1, 1, 1), [(0, 0), (1, 1)...  11.9 us
    dot_general x27, matrix products, body(): lax.dot_general(window, grad_vol, (((0, 2, 3), (0, 2, 3)), ((), ())), pre...  10.7 us
    ppermute x2, starting transfers between devices, extended(): lax.ppermute(tail, axis, [(i, (i + 1) % count) for i in range(ends)])  7.73 us
  transfers between devices with their start and end apart: 7, of which 5 were waited for; matrix products, arithmetic and copies ran while one was open for 14% of the time, Pallas kernels for 0%

commit v1 on v0

v1 whole, which is shorter than its diff:
```python
import jax
import jax.numpy as jnp
from jax import lax
from jax.experimental import pallas as pl
from jax.experimental.pallas import tpu as pltpu
from jax.sharding import PartitionSpec as P

ROWS = 32
WIDE = 64
PLANE = ROWS * WIDE
OWN = 32
TAPS = 9 * OWN
HALF = 896
PIECE = HALF // 8
BF = jnp.bfloat16
F32 = jnp.float32

VM = pl.BlockSpec(memory_space=pltpu.VMEM)
PARAMS = pltpu.CompilerParams(vmem_limit_bytes=48 * 1024 * 1024)


def along_z(step):
    return [(f, ((f // 2 + step) % 4) * 2 + f % 2) for f in range(8)]


ACROSS = [(f, f ^ 1) for f in range(8)]
UP = [(s, (s + 1) % 16) for s in range(16)]
DOWN = [((s + 1) % 16, s) for s in range(16)]
CORE = [(s, s ^ 1) for s in range(16)]
XLO = [(s, s ^ 8) for s in range(16)]


def along_y(step):
    return [(s, (s & 9) | ((((s >> 1) + step) & 3) << 1)) for s in range(16)]


def swapped(flip):
    pairs = []
    for f in range(8):
        for s in range(16):
            if s & 1:
                pairs.append((f * 16 + s, (f ^ 1) * 16 + (s ^ flip)))
            else:
                pairs.append((f * 16 + s, f * 16 + (s ^ 8)))
    return pairs


def columns(shape):
    return lax.broadcasted_iota(jnp.int32, shape, 1) & (WIDE - 1)


def lanes(shape):
    return lax.broadcasted_iota(jnp.int32, shape, 1)


def select_kernel(w_ref, mine_ref, theirs_ref):
    filt = lax.axis_index("filt")
    z, xh = filt // 2, filt % 2
    src = lax.broadcasted_iota(jnp.int32, (256, 256), 0)
    lane = lax.broadcasted_iota(jnp.int32, (256, 256), 1)
    side, turn, chan = lane >> 7, (lane >> 5) & 3, lane & 31
    want = ((z + turn) & 3) * 64 + ((xh + side) & 1) * 32 + chan
    pick = jnp.where(src == want, 1.0, 0.0).astype(BF)
    got = jnp.dot(w_ref[...], pick, preferred_element_type=F32).astype(BF)
    mine_ref[...] = got[:, :128]
    theirs_ref[...] = got[:, 128:]


def forward_kernel(prev_ref, here_ref, next_ref, wa_ref, wb_ref, xs_ref, o0, o1, o2, o3):
    space = lax.axis_index("space")
    col = columns((64, PLANE))
    has_prev = (space > 0).astype(F32)
    has_next = (space < 15).astype(F32)
    for kd, ref in enumerate((prev_ref, here_ref, next_ref)):
        wide = ref[...].astype(F32)
        if kd == 0:
            wide = wide * has_prev
        if kd == 2:
            wide = wide * has_next
        left = jnp.where(col == 0, 0.0, pltpu.roll(wide, 1, 1))
        right = jnp.where(col == WIDE - 1, 0.0, pltpu.roll(wide, PLANE - 1, 1))
        for kw, part in enumerate((left, wide, right)):
            at = (kd * 3 + kw) * OWN
            narrow = part.astype(BF)
            xs_ref[0, at : at + OWN, :] = narrow[:OWN]
            xs_ref[1, at : at + OWN, :] = narrow[OWN:]
    xs_ref[:, TAPS:, :] = jnp.ones((2, 16, PLANE), BF)
    rhs = jnp.concatenate([xs_ref[0, :TAPS, :], xs_ref[1, :TAPS, :]], axis=0)
    parts = []
    for kh in range(3):
        lhs = jnp.concatenate(
            [w[(kd * 3 + kh) * 96 : (kd * 3 + kh) * 96 + 96, :] for w in (wa_ref, wb_ref) for kd in range(3)],
            axis=0,
        )
        parts.append(
            lax.dot_general(lhs, rhs, (((0,), (0,)), ((), ())), preferred_element_type=F32)
        )
    lane = lanes((128, PLANE))
    total = (
        parts[1]
        + jnp.where(lane < WIDE, 0.0, pltpu.roll(parts[0], WIDE, 1))
        + jnp.where(lane >= PLANE - WIDE, 0.0, pltpu.roll(parts[2], PLANE - WIDE, 1))
    )
    for r, ref in enumerate((o0, o1, o2, o3)):
        ref[...] = total[r * 32 : r * 32 + 32]


def row_shifts(wide):
    lane = lanes(wide.shape)
    turned = pltpu.roll(wide, PLANE - WIDE, 1)
    up = jnp.where(lane >= PLANE - WIDE, 0.0, turned)
    down = jnp.where(lane < WIDE, 0.0, pltpu.roll(wide, WIDE, 1))
    return up.astype(BF), wide.astype(BF), down.astype(BF)


def kernel_grad_kernel(xs_ref, c0, c1, c2, c3, keep_ref, send_ref, cs_ref):
    core = lax.axis_index("space") & 1
    for r, ref in enumerate((c0, c1, c2, c3)):
        for kh, part in enumerate(row_shifts(ref[...].astype(F32))):
            cs_ref[kh * 128 + r * 32 : kh * 128 + r * 32 + 32, :] = part
    for slot, ref in enumerate((keep_ref, send_ref)):
        got = lax.dot_general(
            xs_ref[core ^ slot], cs_ref[...], (((1,), (1,)), ((), ())), preferred_element_type=F32
        )
        for kh in range(3):
            ref[kh * TAPS : (kh + 1) * TAPS, :] = got[:TAPS, kh * 128 : kh * 128 + 128]
        ref[3 * TAPS : 3 * TAPS + 16, :] = got[TAPS:, 128:256]
        ref[3 * TAPS + 16 :, :] = got[TAPS:, 128:256]


def input_grad_kernel(prev_ref, next_ref, c0, c1, c2, c3, wa_ref, wb_ref, mine_ref, theirs_ref, cs_ref):
    space = lax.axis_index("space")
    has_prev = (space > 0).astype(F32)
    has_next = (space < 15).astype(F32)
    for r, ref in enumerate((c0, c1, c2, c3)):
        rows = slice(r * 32, r * 32 + 32)
        planes = (
            next_ref[rows, :].astype(F32) * has_next,
            ref[...].astype(F32),
            prev_ref[rows, :].astype(F32) * has_prev,
        )
        for kd, wide in enumerate(planes):
            for kh, part in enumerate(row_shifts(wide)):
                at = (kd * 3 + kh) * 128 + r * 32
                cs_ref[at : at + 32, :] = part
    lhs = jnp.concatenate(
        [
            jnp.concatenate([w[t * 96 : t * 96 + 96, :] for t in range(9)], axis=1)
            for w in (wa_ref, wb_ref)
        ],
        axis=0,
    )
    got = jnp.dot(lhs, cs_ref[...], preferred_element_type=F32)
    col = columns((OWN, PLANE))
    for h, ref in enumerate((mine_ref, theirs_ref)):
        base = h * 96
        ref[...] = (
            got[base + 32 : base + 64]
            + jnp.where(col == WIDE - 1, 0.0, pltpu.roll(got[base : base + 32], PLANE - 1, 1))
            + jnp.where(col == 0, 0.0, pltpu.roll(got[base + 64 : base + 96], 1, 1))
        )


def assemble_kernel(own_ref, other_ref, grad_ref, bias_ref, both_ref, *, factor):
    filt, space = lax.axis_index("filt"), lax.axis_index("space")
    z, xh = filt // 2, filt % 2
    xlo, y, core = space // 8, (space // 2) & 3, space & 1
    for side, ref in enumerate((own_ref, other_ref)):
        for ry in range(4):
            for rx in range(2):
                at = (ry * 2 + rx) * PIECE
                to = pl.multiple_of(((xlo ^ rx) * 4 + ((y + ry) & 3)) * PIECE, 8)
                both_ref[pl.ds(to, PIECE), side * 128 : side * 128 + 128] = ref[at : at + PIECE, :]
    src = lax.broadcasted_iota(jnp.int32, (256, 256), 0)
    lane = lax.broadcasted_iota(jnp.int32, (256, 256), 1)
    side, turn, chan = src >> 7, (src >> 5) & 3, src & 31
    want = ((z + turn) & 3) * 64 + ((xh + core + side) & 1) * 32 + chan
    pick = jnp.where(lane == want, 1.0, 0.0)
    got = jnp.dot(both_ref[: 3 * TAPS, :], pick, precision=lax.Precision.HIGHEST, preferred_element_type=F32)
    got = got * factor
    for kd in range(3):
        for kh in range(3):
            grad_ref[(kd * 3 + kh) * 96 : (kd * 3 + kh) * 96 + 96, :] = got[
                kh * TAPS + kd * 96 : kh * TAPS + kd * 96 + 96
            ]
    tail = both_ref[3 * TAPS : 3 * TAPS + 8, :]
    bias_ref[...] = jnp.where(core == 0, tail[:, :128], tail[:, 128:]) * factor


def call(kernel, outs, *args, scratch=()):
    return pl.pallas_call(
        kernel,
        out_shape=[jax.ShapeDtypeStruct(s, d) for s, d in outs],
        in_specs=[VM] * len(args),
        out_specs=[VM] * len(outs),
        scratch_shapes=list(scratch),
        compiler_params=PARAMS,
    )(*args)


def body(inputs, weight, bias, cotangent):
    space = lax.axis_index("space")
    xlo, y = space // 8, (space // 2) & 3
    x_own = inputs[0]
    c_own = cotangent[0]

    cots = [c_own] + [lax.ppermute(c_own, "filt", along_z(-r)) for r in (1, 2, 3)]
    x_other = lax.ppermute(x_own, "filt", ACROSS)
    w_mine, w_theirs = call(
        select_kernel, [((864, 128), BF), ((864, 128), BF)], weight.reshape(864, 256)
    )
    w_other = lax.ppermute(w_theirs, "filt", ACROSS)

    x_here = jnp.concatenate([x_own, x_other], axis=0)
    x_prev = lax.ppermute(x_here, "space", UP)
    x_next = lax.ppermute(x_here, "space", DOWN)
    c_here = jnp.concatenate(cots, axis=0)
    c_prev = lax.ppermute(c_here, "space", UP)
    c_next = lax.ppermute(c_here, "space", DOWN)

    xs, *outs = call(
        forward_kernel,
        [((2, TAPS + 16, PLANE), BF)] + [((32, PLANE), F32)] * 4,
        x_prev,
        x_here,
        x_next,
        w_mine,
        w_other,
    )
    keep, send = call(
        kernel_grad_kernel,
        [((HALF, 128), F32)] * 2,
        xs,
        *cots,
        scratch=[pltpu.VMEM((384, PLANE), BF)],
    )
    r_core = keep + lax.ppermute(send, "space", CORE)
    half = HALF // 2
    r_send = lax.dynamic_slice_in_dim(r_core, (1 - xlo) * half, half, 0)
    r_keep = lax.dynamic_slice_in_dim(r_core, xlo * half, half, 0)
    r_xlo = r_keep + lax.ppermute(r_send, "space", XLO)

    def part(r):
        return lax.dynamic_slice_in_dim(r_xlo, ((y + r) & 3) * PIECE, PIECE, 0)

    piece = part(0)
    for r in (1, 2, 3):
        piece = piece + lax.ppermute(part(r), "space", along_y(r))

    summed = outs[0]
    for r in (1, 2, 3):
        summed = summed + lax.ppermute(outs[r], "filt", along_z(r))
    output = summed + bias.astype(F32)[:, None]

    g_mine, g_theirs = call(
        input_grad_kernel,
        [((OWN, PLANE), F32)] * 2,
        c_prev,
        c_next,
        *cots,
        w_mine,
        w_other,
        scratch=[pltpu.VMEM((9 * 128, PLANE), BF)],
    )
    grad_inputs = g_mine + lax.ppermute(g_theirs, "filt", ACROSS)

    first = lax.ppermute(piece, ("filt", "space"), swapped(0))
    second = lax.ppermute(piece, ("filt", "space"), swapped(8))
    even = (space & 1) == 0
    pair = jnp.concatenate(
        [jnp.where(even, piece, first), jnp.where(even, first, second)], axis=0
    )
    mine = jnp.concatenate(
        [pair] + [lax.ppermute(pair, "space", along_y(-r)) for r in (1, 2, 3)], axis=0
    )
    other = lax.ppermute(mine, "space", CORE)
    factor = float((16 * PLANE) ** -0.5)
    grad_weight, grad_bias = call(
        lambda *refs: assemble_kernel(*refs, factor=factor),
        [((864, 256), F32), ((8, 128), F32)],
        mine,
        other,
        scratch=[pltpu.VMEM((HALF, 256), F32)],
    )
    return (
        output[None],
        grad_inputs[None],
        grad_weight.reshape(3, 3, 3, OWN, 256),
        grad_bias[0, :OWN],
    )


def solution(mesh):
    placed = (
        P("space", "filt", None),
        P(None, None, None, "filt", None),
        P("filt"),
        P("space", "filt", None),
    )
    return jax.shard_map(
        body,
        mesh=mesh,
        in_specs=placed,
        out_specs=(
            P("space", "filt", None),
            P("space", "filt", None),
            P(None, None, None, "filt", None),
            P("filt"),
        ),
        check_vma=False,
    )
```

time: 327 us -> 80.6 us (0.25)
  waiting for transfers between devices: 190 us -> 28.8 us
  blocking collectives: 45.1 us -> 0 us
  local copies, waits for them, and re-layouts: 33 us -> 3.14 us
  matrix products: 23.5 us -> 0 us
  starting transfers between devices: 14.1 us -> 36.2 us
  between operations: 14.8 us -> 0.75 us
  Pallas kernels: 0 us -> 7.2 us
    psum x1 -> x0, waiting for transfers between devices: 120 us -> none  [body(): kernel_total, bias_total = lax.psum((kernel_part, bias_part), 'space')]
    unnamed x4 -> x0, waiting for transfers between devices: 52.8 us -> none
    psum x1 -> x0, blocking collectives: 45.1 us -> none  [body(): kernel_total, bias_total = lax.psum((kernel_part, bias_part), 'space')]
    ppermute x4 -> x24, waiting for transfers between devices: 3.59 us -> 28.8 us  [the longest x1 8 us: body(): second = lax.ppermute(piece, ('filt', 'space'), swapped(8))]
    ppermute x4 -> x24, starting transfers between devices: 13.8 us -> 36.2 us  [the longest x3 5.67 us: body(): lax.ppermute(pair, 'space', along_y(-r))]
    all_gather x1 -> x0, waiting for transfers between devices: 14 us -> none  [body(): all_grad = lax.all_gather(cotangent, 'filt', axis=1, tiled=True)]
    conv_general_dilated x2 -> x0, matrix products: 12.8 us -> none  [convolve_padded(): lax.conv_general_dilated(volume[None], kernel, (1, 1, 1), [(0, 0), (1, 1)...]
    conv_general_dilated x10 -> x0, local copies, waits for them, and re-layouts: 11.9 us -> none  [convolve_padded(): lax.conv_general_dilated(volume[None], kernel, (1, 1, 1), [(0, 0), (1, 1)...]
  transfers between devices with their start and end apart: 7 -> 24, of which waited for: 5 -> 12; matrix products, arithmetic and copies ran while one was open for 14% -> 6% of each run, Pallas kernels for 0% -> 5%
where the time goes in v1:
time: 80.6 us; the launch traced here: 80.3 us
  starting transfers between devices  36.2 us (45%)
  waiting for transfers between devices  28.8 us (36%)
  Pallas kernels  7.2 us (9%)
  other arithmetic  4.23 us (5%)
  local copies, waits for them, and re-layouts  3.14 us (4%)
    ppermute x1, waiting for transfers between devices, body(): second = lax.ppermute(piece, ('filt', 'space'), swapped(8))  8 us
    pallas_call x5, Pallas kernels, call(): pl.pallas_call(kernel, out_shape=[jax.ShapeDtypeStruct(s, d) for s, d in...  7.2 us
    ppermute x3, starting transfers between devices, body(): lax.ppermute(pair, 'space', along_y(-r))  5.67 us
    ppermute x3, starting transfers between devices, body(): lax.ppermute(c_own, 'filt', along_z(-r))  5.67 us
    ppermute x3, waiting for transfers between devices, body(): lax.ppermute(pair, 'space', along_y(-r))  5.58 us
    ppermute x3, waiting for transfers between devices, body(): piece = piece + lax.ppermute(part(r), 'space', along_y(r))  5.36 us
    ppermute x1, waiting for transfers between devices, body(): r_xlo = r_keep + lax.ppermute(r_send, 'space', XLO)  4.13 us
    ppermute x1, starting transfers between devices, body(): r_core = keep + lax.ppermute(send, 'space', CORE)  3.82 us
  transfers between devices with their start and end apart: 24, of which 12 were waited for; matrix products, arithmetic and copies ran while one was open for 6% of the time, Pallas kernels for 5%

profile of v1, /device:TPU:1, one launch (start us, length us, event | category | flops | bytes accessed | tf_op | source)
XLA Modules:
  0.0 80.3 jit_solution(3622032925217112749)
XLA Ops:
  0.6 3.6 %collective-permute-start = (bf16[32,2048]{1,0:T(8,128)(2,1)}, bf16[32,2048]{1,0:T(8,128)(2,1)S(1)}, u32[]{:S(2)}, u32[]{:S(2)}) collective-permute-start(bf16[32,2048]{1,0:T(8,128)(2,1)} %bitcast.17), channel_id=1, source_target_pairs={{0,16},{16,0},{32,48},{48,32},{64,80},{80,64},{96,112},{112,96},{1... | collective-permute-start | bytes 393224 | tf_op jit(solution)/shard_map/ppermute | solution.py:208
  4.3 1.0 %copy-done.2 = bf16[3,3,3,32,256]{4,3,2,1,0:T(8,128)(2,1)S(1)} copy-done((bf16[3,3,3,32,256]{4,3,2,1,0:T(8,128)(2,1)S(1)}, bf16[3,3,3,32,256]{4,3,2,1,0:T(8,128)(2,1)}, u32[]{:S(2)}) %copy-start.2) | copy-done | bytes 442392
  5.7 1.6 %collective-permute-done = bf16[32,2048]{1,0:T(8,128)(2,1)S(1)} collective-permute-done((bf16[32,2048]{1,0:T(8,128)(2,1)}, bf16[32,2048]{1,0:T(8,128)(2,1)S(1)}, u32[]{:S(2)}, u32[]{:S(2)}) %collective-permute-start) | collective-permute-done | bytes 131104 | tf_op jit(solution)/shard_map/ppermute | solution.py:208
  7.3 0.9 %pad_maximum_fusion.1.here_ref = bf16[64,2048]{1,0:T(8,128)(2,1)S(1)} fusion(bf16[32,2048]{1,0:T(8,128)(2,1)S(1)} %collective-permute-done, bf16[32,2048]{1,0:T(8,128)(2,1)} %bitcast.18), kind=kLoop, calls=%fused_computation.1 | loop fusion | flops 524288 | bytes 524288 | tf_op jit(solution)/shard_map/concatenate | solution.py:214
  8.2 3.4 %collective-permute-start.1 = (bf16[64,2048]{1,0:T(8,128)(2,1)S(1)}, bf16[64,2048]{1,0:T(8,128)(2,1)S(1)}, u32[]{:S(2)}, u32[]{:S(2)}) collective-permute-start(bf16[64,2048]{1,0:T(8,128)(2,1)S(1)} %pad_maximum_fusion.1.here_ref), channel_id=1, source_target_pairs={{0,1},{1,2},{2,3},{3,4},{4,5},{5,6},{6,7},{7,8},{8,9},{9,10},{10,1... | collective-permute-start | bytes 786440 | tf_op jit(solution)/shard_map/ppermute | solution.py:215
  11.6 1.6 %collective-permute-start.9 = (bf16[32,2048]{1,0:T(8,128)(2,1)}, bf16[32,2048]{1,0:T(8,128)(2,1)S(1)}, u32[]{:S(2)}, u32[]{:S(2)}) collective-permute-start(bf16[32,2048]{1,0:T(8,128)(2,1)} %bitcast.10), channel_id=1, source_target_pairs={{0,32},{16,48},{32,64},{48,80},{64,96},{80,112},{96,0},{112,16},{1... | collective-permute-start | bytes 393224 | tf_op jit(solution)/shard_map/ppermute | solution.py:207
  13.2 3.3 %collective-permute-start.8 = (bf16[32,2048]{1,0:T(8,128)(2,1)}, bf16[32,2048]{1,0:T(8,128)(2,1)S(1)}, u32[]{:S(2)}, u32[]{:S(2)}) collective-permute-start(bf16[32,2048]{1,0:T(8,128)(2,1)} %bitcast.11), channel_id=1, source_target_pairs={{0,64},{16,80},{32,96},{48,112},{64,0},{80,16},{96,32},{112,48},{1... | collective-permute-start | bytes 393224 | tf_op jit(solution)/shard_map/ppermute | solution.py:207
  17.7 2.0 %shard_map.76 = (bf16[2,304,2048]{2,1,0:T(8,128)(2,1)S(1)}, f32[32,2048]{1,0:T(8,128)S(1)}, f32[32,2048]{1,0:T(8,128)S(1)}, f32[32,2048]{1,0:T(8,128)S(1)}, f32[32,2048]{1,0:T(8,128)S(1)}) custom-call(bf16[64,2048]{1,0:T(8,128)(2,1)S(1)} %collective-permute-done.1.prev_ref, bf16[64,2048]{1,0:T(8,128)(2,1)S(1)} %pad_maximum_fusion.1.here_ref, ...), custom_call_target="tpu_custom_call" | custom-call | tf_op jit(solution)/shard_map/pallas_call | solution.py:191
  19.7 0.9 %collective-permute-done.8.c2 = bf16[32,2048]{1,0:T(8,128)(2,1)S(1)} collective-permute-done((bf16[32,2048]{1,0:T(8,128)(2,1)}, bf16[32,2048]{1,0:T(8,128)(2,1)S(1)}, u32[]{:S(2)}, u32[]{:S(2)}) %collective-permute-start.8) | collective-permute-done | bytes 131104 | tf_op jit(solution)/shard_map/ppermute | solution.py:207
  21.2 0.9 %copy-done = bf16[1,32,2048]{2,1,0:T(8,128)(2,1)S(1)} copy-done((bf16[1,32,2048]{2,1,0:T(8,128)(2,1)S(1)}, bf16[1,32,2048]{2,1,0:T(8,128)(2,1)}, u32[]{:S(2)}) %copy-start) | copy-done | bytes 131096
  22.1 1.5 %shard_map.78 = (f32[896,128]{1,0:T(8,128)S(1)}, f32[896,128]{1,0:T(8,128)S(1)}) custom-call(bf16[2,304,2048]{2,1,0:T(8,128)(2,1)S(1)} %get-tuple-element.25.xs_ref, bf16[32,2048]{1,0:T(8,128)(2,1)S(1)} %bitcast.13, bf16[32,2048]{1,0:T(8,128)(2,1)S(1)} %collective-permute-done.7.c1, bf16[32,2048]{1,0:T(8,128)(2,1)S(1)} %collective-permute-done.8.c2, ...), custom_call_target="tpu_custom_call" | custom-call | tf_op jit(solution)/shard_map/pallas_call | solution.py:191
  23.7 3.8 %collective-permute-start.13 = (f32[896,128]{1,0:T(8,128)S(1)}, f32[896,128]{1,0:T(8,128)S(1)}, u32[]{:S(2)}, u32[]{:S(2)}) collective-permute-start(f32[896,128]{1,0:T(8,128)S(1)} %get-tuple-element.27), channel_id=1, source_target_pairs={{0,1},{1,0},{2,3},{3,2},{4,5},{5,4},{6,7},{7,6},{8,9},{9,8},{10,11... | collective-permute-start | bytes 1376264 | tf_op jit(solution)/shard_map/ppermute | solution.py:237
  27.5 1.4 %collective-permute-done.13 = f32[896,128]{1,0:T(8,128)S(1)} collective-permute-done((f32[896,128]{1,0:T(8,128)S(1)}, f32[896,128]{1,0:T(8,128)S(1)}, u32[]{:S(2)}, u32[]{:S(2)}) %collective-permute-start.13) | collective-permute-done | bytes 458784 | tf_op jit(solution)/shard_map/ppermute | solution.py:237
  29.0 1.0 %collective-permute-start.14 = (f32[448,128]{1,0:T(8,128)S(1)}, f32[448,128]{1,0:T(8,128)S(1)}, u32[]{:S(2)}, u32[]{:S(2)}) collective-permute-start(f32[448,128]{1,0:T(8,128)S(1)} %constant_dynamic-slice_fusion.3), channel_id=1, source_target_pairs={{0,8},{1,9},{2,10},{3,11},{4,12},{5,13},{6,14},{7,15},{8,0},{9,1},... | collective-permute-start | bytes 688136 | tf_op jit(solution)/shard_map/ppermute | solution.py:241
  30.1 0.8 %pad_maximum_fusion = bf16[128,2048]{1,0:T(8,128)(2,1)} fusion(bf16[32,2048]{1,0:T(8,128)(2,1)S(1)} %collective-permute-done.9.c3, bf16[32,2048]{1,0:T(8,128)(2,1)S(1)} %collective-permute-done.8.c2, bf16[32,2048]{1,0:T(8,128)(2,1)S(1)} %collective-permute-done.7.c1, bf16[32,2048]{1,0:T(8,128)(2,1)S(1)} %bitcast.14), kind=kLoop, calls=%fused_computation | loop fusion | flops 2097152 | bytes 1048576 | tf_op jit(solution)/shard_map/concatenate | solution.py:217
  30.9 0.9 %collective-permute-start.10 = (bf16[128,2048]{1,0:T(8,128)(2,1)}, bf16[128,2048]{1,0:T(8,128)(2,1)S(1)}, u32[]{:S(2)}, u32[]{:S(2)}) collective-permute-start(bf16[128,2048]{1,0:T(8,128)(2,1)} %pad_maximum_fusion), channel_id=1, source_target_pairs={{0,1},{1,2},{2,3},{3,4},{4,5},{5,6},{6,7},{7,8},{8,9},{9,10},{10,1... | collective-permute-start | bytes 1572872 | tf_op jit(solution)/shard_map/ppermute | solution.py:218
  31.8 4.1 %collective-permute-done.14 = f32[448,128]{1,0:T(8,128)S(1)} collective-permute-done((f32[448,128]{1,0:T(8,128)S(1)}, f32[448,128]{1,0:T(8,128)S(1)}, u32[]{:S(2)}, u32[]{:S(2)}) %collective-permute-start.14) | collective-permute-done | bytes 229408 | tf_op jit(solution)/shard_map/ppermute | solution.py:241
  36.6 1.1 %collective-permute-start.17 = (f32[112,128]{1,0:T(8,128)}, f32[112,128]{1,0:T(8,128)S(1)}, u32[]{:S(2)}, u32[]{:S(2)}) collective-permute-start(f32[112,128]{1,0:T(8,128)} %get-tuple-element.35), channel_id=1, source_target_pairs={{0,6},{1,7},{2,0},{3,1},{4,2},{5,3},{6,4},{7,5},{8,14},{9,15},{10,... | collective-permute-start | bytes 172040 | tf_op jit(solution)/shard_map/ppermute | solution.py:248
  37.7 1.1 %collective-permute-start.16 = (f32[112,128]{1,0:T(8,128)S(1)}, f32[112,128]{1,0:T(8,128)S(1)}, u32[]{:S(2)}, u32[]{:S(2)}) collective-permute-start(f32[112,128]{1,0:T(8,128)S(1)} %get-tuple-element.36), channel_id=1, source_target_pairs={{0,4},{1,5},{2,6},{3,7},{4,0},{5,1},{6,2},{7,3},{8,12},{9,13},{10,... | collective-permute-start | bytes 172040 | tf_op jit(solution)/shard_map/ppermute | solution.py:248
  39.1 5.4 %collective-permute-done.17 = f32[112,128]{1,0:T(8,128)S(1)} collective-permute-done((f32[112,128]{1,0:T(8,128)}, f32[112,128]{1,0:T(8,128)S(1)}, u32[]{:S(2)}, u32[]{:S(2)}) %collective-permute-start.17) | collective-permute-done | bytes 57376 | tf_op jit(solution)/shard_map/ppermute | solution.py:248
  44.5 0.8 %add_add_fusion = f32[112,128]{1,0:T(8,128)S(1)} fusion(f32[112,128]{1,0:T(8,128)S(1)} %collective-permute-done.17, f32[112,128]{1,0:T(8,128)S(1)} %collective-permute-done.16, f32[112,128]{1,0:T(8,128)} %collective-permute-done.15, f32[448,128]{1,0:T(8,128)S(1)} %dynamic-slice_add_fusion, s32[]{:T(128)S(6)} %select_n.43), kind=kLoop, calls=%fused_computation.6 | loop fusion | flops 43008 | bytes 286724 | tf_op jit(solution)/shard_map/add | solution.py:248
  45.3 3.7 %collective-permute-start.18 = (f32[112,128]{1,0:T(8,128)S(1)}, f32[112,128]{1,0:T(8,128)S(1)}, u32[]{:S(2)}, u32[]{:S(2)}) collective-permute-start(f32[112,128]{1,0:T(8,128)S(1)} %add_add_fusion), channel_id=1, source_target_pairs={{0,8},{1,17},{2,10},{3,19},{4,12},{5,21},{6,14},{7,23},{8,0},{9,25... | collective-permute-start | bytes 172040 | tf_op jit(solution)/shard_map/ppermute | solution.py:267
  49.0 1.9 %collective-permute-start.6 = (f32[32,2048]{1,0:T(8,128)S(1)}, f32[32,2048]{1,0:T(8,128)S(1)}, u32[]{:S(2)}, u32[]{:S(2)}) collective-permute-start(f32[32,2048]{1,0:T(8,128)S(1)} %get-tuple-element.22), channel_id=1, source_target_pairs={{0,96},{16,112},{32,0},{48,16},{64,32},{80,48},{96,64},{112,80},{1... | collective-permute-start | bytes 786440 | tf_op jit(solution)/shard_map/ppermute | solution.py:252
  51.6 1.5 %shard_map.77 = (f32[32,2048]{1,0:T(8,128)S(1)}, f32[32,2048]{1,0:T(8,128)S(1)}) custom-call(bf16[128,2048]{1,0:T(8,128)(2,1)S(1)} %collective-permute-done.10.prev_ref, bf16[128,2048]{1,0:T(8,128)(2,1)S(1)} %collective-permute-done.11.next_ref, bf16[32,2048]{1,0:T(8,128)(2,1)S(1)} %bitcast.15, bf16[32,2048]{1,0:T(8,128)(2,1)S(1)} %collective-permute-done.7.c1, ...), custom_call_target="tpu_custom_call" | custom-call | tf_op jit(solution)/shard_map/pallas_call | solution.py:191
  53.3 2.1 %collective-permute-start.19 = (f32[112,128]{1,0:T(8,128)S(1)}, f32[112,128]{1,0:T(8,128)S(1)}, u32[]{:S(2)}, u32[]{:S(2)}) collective-permute-start(f32[112,128]{1,0:T(8,128)S(1)} %add_add_fusion), channel_id=1, source_target_pairs={{0,8},{1,25},{2,10},{3,27},{4,12},{5,29},{6,14},{7,31},{8,0},{9,17... | collective-permute-start | bytes 172040 | tf_op jit(solution)/shard_map/ppermute | solution.py:268
  55.4 8.0 %collective-permute-done.19 = f32[112,128]{1,0:T(8,128)S(1)} collective-permute-done((f32[112,128]{1,0:T(8,128)S(1)}, f32[112,128]{1,0:T(8,128)S(1)}, u32[]{:S(2)}, u32[]{:S(2)}) %collective-permute-start.19) | collective-permute-done | bytes 57376 | tf_op jit(solution)/shard_map/ppermute | solution.py:268
  63.5 2.8 %collective-permute-start.20 = (f32[224,128]{1,0:T(8,128)S(1)}, f32[224,128]{1,0:T(8,128)S(1)}, u32[]{:S(2)}, u32[]{:S(2)}) collective-permute-start(f32[224,128]{1,0:T(8,128)S(1)} %pad_maximum_fusion.2), channel_id=1, source_target_pairs={{0,6},{1,7},{2,0},{3,1},{4,2},{5,3},{6,4},{7,5},{8,14},{9,15},{10,... | collective-permute-start | bytes 344072 | tf_op jit(solution)/shard_map/ppermute | solution.py:274
  67.1 2.8 %collective-permute-start.22 = (f32[224,128]{1,0:T(8,128)S(1)}, f32[224,128]{1,0:T(8,128)S(1)}, u32[]{:S(2)}, u32[]{:S(2)}) collective-permute-start(f32[224,128]{1,0:T(8,128)S(1)} %pad_maximum_fusion.2), channel_id=1, source_target_pairs={{0,2},{1,3},{2,4},{3,5},{4,6},{5,7},{6,0},{7,1},{8,10},{9,11},{10,... | collective-permute-start | bytes 344072 | tf_op jit(solution)/shard_map/ppermute | solution.py:274
  70.0 2.9 %collective-permute-done.21 = f32[224,128]{1,0:T(8,128)S(1)} collective-permute-done((f32[224,128]{1,0:T(8,128)S(1)}, f32[224,128]{1,0:T(8,128)S(1)}, u32[]{:S(2)}, u32[]{:S(2)}) %collective-permute-start.21) | collective-permute-done | bytes 114720 | tf_op jit(solution)/shard_map/ppermute | solution.py:274
  73.0 2.6 %collective-permute-done.22 = f32[224,128]{1,0:T(8,128)S(1)} collective-permute-done((f32[224,128]{1,0:T(8,128)S(1)}, f32[224,128]{1,0:T(8,128)S(1)}, u32[]{:S(2)}, u32[]{:S(2)}) %collective-permute-start.22) | collective-permute-done | bytes 114720 | tf_op jit(solution)/shard_map/ppermute | solution.py:274
  75.6 0.9 %collective-permute-start.23 = (f32[896,128]{1,0:T(8,128)S(1)}, f32[896,128]{1,0:T(8,128)S(1)}, u32[]{:S(2)}, u32[]{:S(2)}) collective-permute-start(f32[896,128]{1,0:T(8,128)S(1)} %constant_dynamic-update-slice_fusion.refs_0_), channel_id=1, source_target_pairs={{0,1},{1,0},{2,3},{3,2},{4,5},{5,4},{6,7},{7,6},{8,9},{9,8},{10,11... | collective-permute-start | bytes 1376264 | tf_op jit(solution)/shard_map/ppermute | solution.py:276
  77.9 1.9 %shard_map.79 = (f32[864,256]{1,0:T(8,128)}, f32[8,128]{1,0:T(8,128)S(1)}) custom-call(f32[896,128]{1,0:T(8,128)S(1)} %constant_dynamic-update-slice_fusion.refs_0_, f32[896,128]{1,0:T(8,128)S(1)} %collective-permute-done.23.refs_1_), custom_call_target="tpu_custom_call" | custom-call | tf_op jit(solution)/shard_map/pallas_call | solution.py:191
  (46 shorter events, 7.0 us)
Async XLA Ops:
  0.6 6.7 %collective-permute-start = (bf16[32,2048]{1,0:T(8,128)(2,1)}, bf16[32,2048]{1,0:T(8,128)(2,1)S(1)}, u32[]{:S(2)}, u32[]{:S(2)}) collective-permute-start(bf16[32,2048]{1,0:T(8,128)(2,1)} %bitcast.17), channel_id=1, source_target_pairs={{0,16},{16,0},{32,48},{48,32},{64,80},{80,64},{96,112},{112,96},{1... | collective-permute-start | bytes 393224 | tf_op jit(solution)/shard_map/ppermute | solution.py:208
  4.3 1.0 %copy-start.2 = (bf16[3,3,3,32,256]{4,3,2,1,0:T(8,128)(2,1)S(1)}, bf16[3,3,3,32,256]{4,3,2,1,0:T(8,128)(2,1)}, u32[]{:S(2)}) copy-start(bf16[3,3,3,32,256]{4,3,2,1,0:T(8,128)(2,1)} %param.5) | copy-start | bytes 1327108
  5.6 11.0 %collective-permute-start.3 = (bf16[864,128]{1,0:T(8,128)(2,1)S(1)}, bf16[864,128]{1,0:T(8,128)(2,1)S(1)}, u32[]{:S(2)}, u32[]{:S(2)}) collective-permute-start(bf16[864,128]{1,0:T(8,128)(2,1)S(1)} %get-tuple-element.18), channel_id=1, source_target_pairs={{0,16},{16,0},{32,48},{48,32},{64,80},{80,64},{96,112},{112,96},{1... | collective-permute-start | bytes 663560 | tf_op jit(solution)/shard_map/ppermute | solution.py:212
  8.2 9.1 %collective-permute-start.1 = (bf16[64,2048]{1,0:T(8,128)(2,1)S(1)}, bf16[64,2048]{1,0:T(8,128)(2,1)S(1)}, u32[]{:S(2)}, u32[]{:S(2)}) collective-permute-start(bf16[64,2048]{1,0:T(8,128)(2,1)S(1)} %pad_maximum_fusion.1.here_ref), channel_id=1, source_target_pairs={{0,1},{1,2},{2,3},{3,4},{4,5},{5,6},{6,7},{7,8},{8,9},{9,10},{10,1... | collective-permute-start | bytes 786440 | tf_op jit(solution)/shard_map/ppermute | solution.py:215
  11.6 6.1 %collective-permute-start.2 = (bf16[64,2048]{1,0:T(8,128)(2,1)S(1)}, bf16[64,2048]{1,0:T(8,128)(2,1)S(1)}, u32[]{:S(2)}, u32[]{:S(2)}) collective-permute-start(bf16[64,2048]{1,0:T(8,128)(2,1)S(1)} %pad_maximum_fusion.1.here_ref), channel_id=1, source_target_pairs={{1,0},{2,1},{3,2},{4,3},{5,4},{6,5},{7,6},{8,7},{9,8},{10,9},{11,1... | collective-permute-start | bytes 786440 | tf_op jit(solution)/shard_map/ppermute | solution.py:216
  11.6 8.1 %collective-permute-start.9 = (bf16[32,2048]{1,0:T(8,128)(2,1)}, bf16[32,2048]{1,0:T(8,128)(2,1)S(1)}, u32[]{:S(2)}, u32[]{:S(2)}) collective-permute-start(bf16[32,2048]{1,0:T(8,128)(2,1)} %bitcast.10), channel_id=1, source_target_pairs={{0,32},{16,48},{32,64},{48,80},{64,96},{80,112},{96,0},{112,16},{1... | collective-permute-start | bytes 393224 | tf_op jit(solution)/shard_map/ppermute | solution.py:207
  13.2 7.4 %collective-permute-start.8 = (bf16[32,2048]{1,0:T(8,128)(2,1)}, bf16[32,2048]{1,0:T(8,128)(2,1)S(1)}, u32[]{:S(2)}, u32[]{:S(2)}) collective-permute-start(bf16[32,2048]{1,0:T(8,128)(2,1)} %bitcast.11), channel_id=1, source_target_pairs={{0,64},{16,80},{32,96},{48,112},{64,0},{80,16},{96,32},{112,48},{1... | collective-permute-start | bytes 393224 | tf_op jit(solution)/shard_map/ppermute | solution.py:207
  16.6 4.7 %collective-permute-start.7 = (bf16[32,2048]{1,0:T(8,128)(2,1)}, bf16[32,2048]{1,0:T(8,128)(2,1)S(1)}, u32[]{:S(2)}, u32[]{:S(2)}) collective-permute-start(bf16[32,2048]{1,0:T(8,128)(2,1)} %bitcast.12), channel_id=1, source_target_pairs={{0,96},{16,112},{32,0},{48,16},{64,32},{80,48},{96,64},{112,80},{1... | collective-permute-start | bytes 393224 | tf_op jit(solution)/shard_map/ppermute | solution.py:207
  17.7 12.4 %copy-start.1 = (bf16[1,32,2048]{2,1,0:T(8,128)(2,1)S(1)}, bf16[1,32,2048]{2,1,0:T(8,128)(2,1)}, u32[]{:S(2)}) copy-start(bf16[1,32,2048]{2,1,0:T(8,128)(2,1)} %param.7) | copy-start | bytes 393220
  21.2 0.9 %copy-start = (bf16[1,32,2048]{2,1,0:T(8,128)(2,1)S(1)}, bf16[1,32,2048]{2,1,0:T(8,128)(2,1)}, u32[]{:S(2)}) copy-start(bf16[1,32,2048]{2,1,0:T(8,128)(2,1)} %param.7) | copy-start | bytes 393220
  23.7 25.3 %copy-start.3 = (bf16[32]{0:T(256)(128)(2,1)S(1)}, bf16[32]{0:T(256)(128)(2,1)}, u32[]{:S(2)}) copy-start(bf16[32]{0:T(256)(128)(2,1)} %param.6) | copy-start | bytes 196
  23.7 5.3 %collective-permute-start.13 = (f32[896,128]{1,0:T(8,128)S(1)}, f32[896,128]{1,0:T(8,128)S(1)}, u32[]{:S(2)}, u32[]{:S(2)}) collective-permute-start(f32[896,128]{1,0:T(8,128)S(1)} %get-tuple-element.27), channel_id=1, source_target_pairs={{0,1},{1,0},{2,3},{3,2},{4,5},{5,4},{6,7},{7,6},{8,9},{9,8},{10,11... | collective-permute-start | bytes 1376264 | tf_op jit(solution)/shard_map/ppermute | solution.py:237
  29.0 6.9 %collective-permute-start.14 = (f32[448,128]{1,0:T(8,128)S(1)}, f32[448,128]{1,0:T(8,128)S(1)}, u32[]{:S(2)}, u32[]{:S(2)}) collective-permute-start(f32[448,128]{1,0:T(8,128)S(1)} %constant_dynamic-slice_fusion.3), channel_id=1, source_target_pairs={{0,8},{1,9},{2,10},{3,11},{4,12},{5,13},{6,14},{7,15},{8,0},{9,1},... | collective-permute-start | bytes 688136 | tf_op jit(solution)/shard_map/ppermute | solution.py:241
  30.9 20.4 %collective-permute-start.10 = (bf16[128,2048]{1,0:T(8,128)(2,1)}, bf16[128,2048]{1,0:T(8,128)(2,1)S(1)}, u32[]{:S(2)}, u32[]{:S(2)}) collective-permute-start(bf16[128,2048]{1,0:T(8,128)(2,1)} %pad_maximum_fusion), channel_id=1, source_target_pairs={{0,1},{1,2},{2,3},{3,4},{4,5},{5,6},{6,7},{7,8},{8,9},{9,10},{10,1... | collective-permute-start | bytes 1572872 | tf_op jit(solution)/shard_map/ppermute | solution.py:218
  31.8 19.8 %collective-permute-start.11 = (bf16[128,2048]{1,0:T(8,128)(2,1)}, bf16[128,2048]{1,0:T(8,128)(2,1)S(1)}, u32[]{:S(2)}, u32[]{:S(2)}) collective-permute-start(bf16[128,2048]{1,0:T(8,128)(2,1)} %pad_maximum_fusion), channel_id=1, source_target_pairs={{1,0},{2,1},{3,2},{4,3},{5,4},{6,5},{7,6},{8,7},{9,8},{10,9},{11,1... | collective-permute-start | bytes 1572872 | tf_op jit(solution)/shard_map/ppermute | solution.py:219
  36.6 7.9 %collective-permute-start.17 = (f32[112,128]{1,0:T(8,128)}, f32[112,128]{1,0:T(8,128)S(1)}, u32[]{:S(2)}, u32[]{:S(2)}) collective-permute-start(f32[112,128]{1,0:T(8,128)} %get-tuple-element.35), channel_id=1, source_target_pairs={{0,6},{1,7},{2,0},{3,1},{4,2},{5,3},{6,4},{7,5},{8,14},{9,15},{10,... | collective-permute-start | bytes 172040 | tf_op jit(solution)/shard_map/ppermute | solution.py:248
  37.7 6.8 %collective-permute-start.16 = (f32[112,128]{1,0:T(8,128)S(1)}, f32[112,128]{1,0:T(8,128)S(1)}, u32[]{:S(2)}, u32[]{:S(2)}) collective-permute-start(f32[112,128]{1,0:T(8,128)S(1)} %get-tuple-element.36), channel_id=1, source_target_pairs={{0,4},{1,5},{2,6},{3,7},{4,0},{5,1},{6,2},{7,3},{8,12},{9,13},{10,... | collective-permute-start | bytes 172040 | tf_op jit(solution)/shard_map/ppermute | solution.py:248
  38.7 5.8 %collective-permute-start.15 = (f32[112,128]{1,0:T(8,128)S(1)}, f32[112,128]{1,0:T(8,128)}, u32[]{:S(2)}, u32[]{:S(2)}) collective-permute-start(f32[112,128]{1,0:T(8,128)S(1)} %get-tuple-element.34), channel_id=1, source_target_pairs={{0,2},{1,3},{2,4},{3,5},{4,6},{5,7},{6,0},{7,1},{8,10},{9,11},{10,... | collective-permute-start | bytes 172040 | tf_op jit(solution)/shard_map/ppermute | solution.py:248
  45.3 7.9 %collective-permute-start.18 = (f32[112,128]{1,0:T(8,128)S(1)}, f32[112,128]{1,0:T(8,128)S(1)}, u32[]{:S(2)}, u32[]{:S(2)}) collective-permute-start(f32[112,128]{1,0:T(8,128)S(1)} %add_add_fusion), channel_id=1, source_target_pairs={{0,8},{1,17},{2,10},{3,19},{4,12},{5,21},{6,14},{7,23},{8,0},{9,25... | collective-permute-start | bytes 172040 | tf_op jit(solution)/shard_map/ppermute | solution.py:267
  49.0 17.3 %collective-permute-start.6 = (f32[32,2048]{1,0:T(8,128)S(1)}, f32[32,2048]{1,0:T(8,128)S(1)}, u32[]{:S(2)}, u32[]{:S(2)}) collective-permute-start(f32[32,2048]{1,0:T(8,128)S(1)} %get-tuple-element.22), channel_id=1, source_target_pairs={{0,96},{16,112},{32,0},{48,16},{64,32},{80,48},{96,64},{112,80},{1... | collective-permute-start | bytes 786440 | tf_op jit(solution)/shard_map/ppermute | solution.py:252
  50.9 15.3 %collective-permute-start.5 = (f32[32,2048]{1,0:T(8,128)S(1)}, f32[32,2048]{1,0:T(8,128)S(1)}, u32[]{:S(2)}, u32[]{:S(2)}) collective-permute-start(f32[32,2048]{1,0:T(8,128)S(1)} %get-tuple-element.21), channel_id=1, source_target_pairs={{0,64},{16,80},{32,96},{48,112},{64,0},{80,16},{96,32},{112,48},{1... | collective-permute-start | bytes 786440 | tf_op jit(solution)/shard_map/ppermute | solution.py:252
  51.3 15.0 %collective-permute-start.4 = (f32[32,2048]{1,0:T(8,128)S(1)}, f32[32,2048]{1,0:T(8,128)S(1)}, u32[]{:S(2)}, u32[]{:S(2)}) collective-permute-start(f32[32,2048]{1,0:T(8,128)S(1)} %get-tuple-element.20), channel_id=1, source_target_pairs={{0,32},{16,48},{32,64},{48,80},{64,96},{80,112},{96,0},{112,16},{1... | collective-permute-start | bytes 786440 | tf_op jit(solution)/shard_map/ppermute | solution.py:252
  53.1 23.4 %collective-permute-start.12 = (f32[32,2048]{1,0:T(8,128)S(1)}, f32[32,2048]{1,0:T(8,128)S(1)}, u32[]{:S(2)}, u32[]{:S(2)}) collective-permute-start(f32[32,2048]{1,0:T(8,128)S(1)} %get-tuple-element.24), channel_id=1, source_target_pairs={{0,16},{16,0},{32,48},{48,32},{64,80},{80,64},{96,112},{112,96},{1... | collective-permute-start | bytes 786440 | tf_op jit(solution)/shard_map/ppermute | solution.py:265
  53.3 10.2 %collective-permute-start.19 = (f32[112,128]{1,0:T(8,128)S(1)}, f32[112,128]{1,0:T(8,128)S(1)}, u32[]{:S(2)}, u32[]{:S(2)}) collective-permute-start(f32[112,128]{1,0:T(8,128)S(1)} %add_add_fusion), channel_id=1, source_target_pairs={{0,8},{1,25},{2,10},{3,27},{4,12},{5,29},{6,14},{7,31},{8,0},{9,17... | collective-permute-start | bytes 172040 | tf_op jit(solution)/shard_map/ppermute | solution.py:268
  63.5 6.5 %collective-permute-start.20 = (f32[224,128]{1,0:T(8,128)S(1)}, f32[224,128]{1,0:T(8,128)S(1)}, u32[]{:S(2)}, u32[]{:S(2)}) collective-permute-start(f32[224,128]{1,0:T(8,128)S(1)} %pad_maximum_fusion.2), channel_id=1, source_target_pairs={{0,6},{1,7},{2,0},{3,1},{4,2},{5,3},{6,4},{7,5},{8,14},{9,15},{10,... | collective-permute-start | bytes 344072 | tf_op jit(solution)/shard_map/ppermute | solution.py:274
  67.1 5.8 %collective-permute-start.21 = (f32[224,128]{1,0:T(8,128)S(1)}, f32[224,128]{1,0:T(8,128)S(1)}, u32[]{:S(2)}, u32[]{:S(2)}) collective-permute-start(f32[224,128]{1,0:T(8,128)S(1)} %pad_maximum_fusion.2), channel_id=1, source_target_pairs={{0,4},{1,5},{2,6},{3,7},{4,0},{5,1},{6,2},{7,3},{8,12},{9,13},{10,... | collective-permute-start | bytes 344072 | tf_op jit(solution)/shard_map/ppermute | solution.py:274
  67.1 8.4 %collective-permute-start.22 = (f32[224,128]{1,0:T(8,128)S(1)}, f32[224,128]{1,0:T(8,128)S(1)}, u32[]{:S(2)}, u32[]{:S(2)}) collective-permute-start(f32[224,128]{1,0:T(8,128)S(1)} %pad_maximum_fusion.2), channel_id=1, source_target_pairs={{0,2},{1,3},{2,4},{3,5},{4,6},{5,7},{6,0},{7,1},{8,10},{9,11},{10,... | collective-permute-start | bytes 344072 | tf_op jit(solution)/shard_map/ppermute | solution.py:274
  75.6 2.3 %collective-permute-start.23 = (f32[896,128]{1,0:T(8,128)S(1)}, f32[896,128]{1,0:T(8,128)S(1)}, u32[]{:S(2)}, u32[]{:S(2)}) collective-permute-start(f32[896,128]{1,0:T(8,128)S(1)} %constant_dynamic-update-slice_fusion.refs_0_), channel_id=1, source_target_pairs={{0,1},{1,0},{2,3},{3,2},{4,5},{5,4},{6,7},{7,6},{8,9},{9,8},{10,11... | collective-permute-start | bytes 1376264 | tf_op jit(solution)/shard_map/ppermute | solution.py:276

commit v2 on v1

--- a/solution.py
+++ b/solution.py
@@ -4,6 +4,7 @@
 from jax.experimental import pallas as pl
 from jax.experimental.pallas import tpu as pltpu
 from jax.sharding import PartitionSpec as P
+
 
 ROWS = 32
 WIDE = 64
@@ -53,7 +54,9 @@
     return lax.broadcasted_iota(jnp.int32, shape, 1)
 
 
-def select_kernel(w_ref, mine_ref, theirs_ref):
+def select_kernel(w_ref, x_ref, c_ref, mine_ref, theirs_ref, x_out, c_out):
+    x_out[...] = x_ref[...]
+    c_out[...] = c_ref[...]
     filt = lax.axis_index("filt")
     z, xh = filt // 2, filt % 2
     src = lax.broadcasted_iota(jnp.int32, (256, 256), 0)
@@ -66,8 +69,46 @@
     theirs_ref[...] = got[:, 128:]
 
 
-def forward_kernel(prev_ref, here_ref, next_ref, wa_ref, wb_ref, xs_ref, o0, o1, o2, o3):
+def join_kernel(*refs):
+    *parts, out_ref = refs
+    at = 0
+    for ref in parts:
+        out_ref[at : at + ref.shape[0], :] = ref[...]
+        at += ref.shape[0]
+
+
+def forward_kernel(xs_ref, wa_ref, wb_ref, o0, o1, o2, o3):
+    rhs = jnp.concatenate([xs_ref[0, :TAPS, :], xs_ref[1, :TAPS, :]], axis=0)
+    parts = []
+    for kh in range(3):
+        lhs = jnp.concatenate(
+            [w[(kd * 3 + kh) * 96 : (kd * 3 + kh) * 96 + 96, :] for w in (wa_ref, wb_ref) for kd in range(3)],
+            axis=0,
+        )
+        parts.append(
+            lax.dot_general(lhs, rhs, (((0,), (0,)), ((), ())), preferred_element_type=F32)
+        )
+    lane = lanes((128, PLANE))
+    total = (
+        parts[1]
+        + jnp.where(lane < WIDE, 0.0, pltpu.roll(parts[0], WIDE, 1))
+        + jnp.where(lane >= PLANE - WIDE, 0.0, pltpu.roll(parts[2], PLANE - WIDE, 1))
+    )
+    for r, ref in enumerate((o0, o1, o2, o3)):
+        ref[...] = total[r * 32 : r * 32 + 32]
+
+
+def row_shifts(wide):
+    lane = lanes(wide.shape)
+    turned = pltpu.roll(wide, PLANE - WIDE, 1)
+    up = jnp.where(lane >= PLANE - WIDE, 0.0, turned)
+    down = jnp.where(lane < WIDE, 0.0, pltpu.roll(wide, WIDE, 1))
+    return up.astype(BF), wide.astype(BF), down.astype(BF)
+
+
+def kernel_grad_kernel(prev_ref, here_ref, next_ref, c0, c1, c2, c3, xs_ref, keep_ref, send_ref, cs_ref):
     space = lax.axis_index("space")
+    core = space & 1
     col = columns((64, PLANE))
     has_prev = (space > 0).astype(F32)
     has_next = (space < 15).astype(F32)
@@ -85,36 +126,6 @@
             xs_ref[0, at : at + OWN, :] = narrow[:OWN]
             xs_ref[1, at : at + OWN, :] = narrow[OWN:]
     xs_ref[:, TAPS:, :] = jnp.ones((2, 16, PLANE), BF)
-    rhs = jnp.concatenate([xs_ref[0, :TAPS, :], xs_ref[1, :TAPS, :]], axis=0)
-    parts = []
-    for kh in range(3):
-        lhs = jnp.concatenate(
-            [w[(kd * 3 + kh) * 96 : (kd * 3 + kh) * 96 + 96, :] for w in (wa_ref, wb_ref) for kd in range(3)],
-            axis=0,
-        )
-        parts.append(
-            lax.dot_general(lhs, rhs, (((0,), (0,)), ((), ())), preferred_element_type=F32)
-        )
-    lane = lanes((128, PLANE))
-    total = (
-        parts[1]
-        + jnp.where(lane < WIDE, 0.0, pltpu.roll(parts[0], WIDE, 1))
-        + jnp.where(lane >= PLANE - WIDE, 0.0, pltpu.roll(parts[2], PLANE - WIDE, 1))
-    )
-    for r, ref in enumerate((o0, o1, o2, o3)):
-        ref[...] = total[r * 32 : r * 32 + 32]
-
-
-def row_shifts(wide):
-    lane = lanes(wide.shape)
-    turned = pltpu.roll(wide, PLANE - WIDE, 1)
-    up = jnp.where(lane >= PLANE - WIDE, 0.0, turned)
-    down = jnp.where(lane < WIDE, 0.0, pltpu.roll(wide, WIDE, 1))
-    return up.astype(BF), wide.astype(BF), down.astype(BF)
-
-
-def kernel_grad_kernel(xs_ref, c0, c1, c2, c3, keep_ref, send_ref, cs_ref):
-    core = lax.axis_index("space") & 1
     for r, ref in enumerate((c0, c1, c2, c3)):
         for kh, part in enumerate(row_shifts(ref[...].astype(F32))):
             cs_ref[kh * 128 + r * 32 : kh * 128 + r * 32 + 32, :] = part
@@ -183,8 +194,33 @@
             grad_ref[(kd * 3 + kh) * 96 : (kd * 3 + kh) * 96 + 96, :] = got[
                 kh * TAPS + kd * 96 : kh * TAPS + kd * 96 + 96
             ]
-    tail = both_ref[3 * TAPS : 3 * TAPS + 8, :]
-    bias_ref[...] = jnp.where(core == 0, tail[:, :128], tail[:, 128:]) * factor
+    tail = both_ref[3 * TAPS : 3 * TAPS + 1, :]
+    bias_ref[...] = jnp.where(core == 0, tail[:, :OWN], tail[:, 128 : 128 + OWN]) * factor
+
+
+def split_xlo_kernel(keep_ref, got_ref, send_out, keep_out):
+    half = HALF // 2
+    xlo = lax.axis_index("space") // 8
+    for out, at in ((send_out, (1 - xlo) * half), (keep_out, xlo * half)):
+        rows = pl.ds(pl.multiple_of(at, 8), half)
+        out[...] = keep_ref[rows, :] + got_ref[rows, :]
+
+
+def split_y_kernel(keep_ref, got_ref, *outs):
+    y = (lax.axis_index("space") // 2) & 3
+    for r, out in enumerate(outs):
+        rows = pl.ds(pl.multiple_of(((y + r) & 3) * PIECE, 8), PIECE)
+        out[...] = keep_ref[rows, :] + got_ref[rows, :]
+
+
+def add4_kernel(a, b, c, d, out):
+    out[...] = (a[...] + b[...]) + (c[...] + d[...])
+
+
+def pair_kernel(piece_ref, first_ref, second_ref, out_ref):
+    even = (lax.axis_index("space") & 1) == 0
+    out_ref[:PIECE, :] = jnp.where(even, piece_ref[...], first_ref[...])
+    out_ref[PIECE:, :] = jnp.where(even, first_ref[...], second_ref[...])
 
 
 def call(kernel, outs, *args, scratch=()):
@@ -198,60 +234,56 @@
     )(*args)
 
 
-def body(inputs, weight, bias, cotangent):
-    space = lax.axis_index("space")
-    xlo, y = space // 8, (space // 2) & 3
+def step(inputs, weight, bias, cotangent):
     x_own = inputs[0]
     c_own = cotangent[0]
 
-    cots = [c_own] + [lax.ppermute(c_own, "filt", along_z(-r)) for r in (1, 2, 3)]
     x_other = lax.ppermute(x_own, "filt", ACROSS)
-    w_mine, w_theirs = call(
-        select_kernel, [((864, 128), BF), ((864, 128), BF)], weight.reshape(864, 256)
+    c1, c3, c2 = (lax.ppermute(c_own, "filt", along_z(-r)) for r in (1, 3, 2))
+    w_mine, w_theirs, x_near, c_near = call(
+        select_kernel,
+        [((864, 128), BF), ((864, 128), BF), ((OWN, PLANE), BF), ((OWN, PLANE), BF)],
+        weight.reshape(864, 256),
+        x_own,
+        c_own,
     )
     w_other = lax.ppermute(w_theirs, "filt", ACROSS)
-
-    x_here = jnp.concatenate([x_own, x_other], axis=0)
+    cots = [c_near, c1, c2, c3]
+
+    (x_here,) = call(join_kernel, [((64, PLANE), BF)], x_near, x_other)
     x_prev = lax.ppermute(x_here, "space", UP)
     x_next = lax.ppermute(x_here, "space", DOWN)
-    c_here = jnp.concatenate(cots, axis=0)
-    c_prev = lax.ppermute(c_here, "space", UP)
-    c_next = lax.ppermute(c_here, "space", DOWN)
-
-    xs, *outs = call(
-        forward_kernel,
-        [((2, TAPS + 16, PLANE), BF)] + [((32, PLANE), F32)] * 4,
+
+    xs, keep, send = call(
+        kernel_grad_kernel,
+        [((2, TAPS + 16, PLANE), BF)] + [((HALF, 128), F32)] * 2,
         x_prev,
         x_here,
         x_next,
-        w_mine,
-        w_other,
-    )
-    keep, send = call(
-        kernel_grad_kernel,
-        [((HALF, 128), F32)] * 2,
-        xs,
         *cots,
         scratch=[pltpu.VMEM((384, PLANE), BF)],
     )
-    r_core = keep + lax.ppermute(send, "space", CORE)
+    r_core = lax.ppermute(send, "space", CORE)
+    outs = call(forward_kernel, [((32, PLANE), F32)] * 4, xs, w_mine, w_other)
+    (c_here,) = call(join_kernel, [((128, PLANE), BF)], *cots)
+
     half = HALF // 2
-    r_send = lax.dynamic_slice_in_dim(r_core, (1 - xlo) * half, half, 0)
-    r_keep = lax.dynamic_slice_in_dim(r_core, xlo * half, half, 0)
-    r_xlo = r_keep + lax.ppermute(r_send, "space", XLO)
-
-    def part(r):
-        return lax.dynamic_slice_in_dim(r_xlo, ((y + r) & 3) * PIECE, PIECE, 0)
-
-    piece = part(0)
-    for r in (1, 2, 3):
-        piece = piece + lax.ppermute(part(r), "space", along_y(r))
+    r_send, r_keep = call(split_xlo_kernel, [((half, 128), F32)] * 2, keep, r_core)
+    r_xlo = lax.ppermute(r_send, "space", XLO)
+    c_prev = lax.ppermute(c_here, "space", UP)
+    c_next = lax.ppermute(c_here, "space", DOWN)
+
+    parts = call(split_y_kernel, [((PIECE, 128), F32)] * 4, r_keep, r_xlo)
+    got = [lax.ppermute(parts[r], "space", along_y(r)) for r in (1, 3, 2)]
+    (piece,) = call(add4_kernel, [((PIECE, 128), F32)], parts[0], *got)
 
     summed = outs[0]
-    for r in (1, 2, 3):
+    for r in (1, 3, 2):
         summed = summed + lax.ppermute(outs[r], "filt", along_z(r))
     output = summed + bias.astype(F32)[:, None]
 
+    first = lax.ppermute(piece, ("filt", "space"), swapped(0))
+    second = lax.ppermute(piece, ("filt", "space"), swapped(8))
     g_mine, g_theirs = call(
         input_grad_kernel,
         [((OWN, PLANE), F32)] * 2,
@@ -264,20 +296,14 @@
     )
     grad_inputs = g_mine + lax.ppermute(g_theirs, "filt", ACROSS)
 
-    first = lax.ppermute(piece, ("filt", "space"), swapped(0))
-    second = lax.ppermute(piece, ("filt", "space"), swapped(8))
-    even = (space & 1) == 0
-    pair = jnp.concatenate(
-        [jnp.where(even, piece, first), jnp.where(even, first, second)], axis=0
-    )
-    mine = jnp.concatenate(
-        [pair] + [lax.ppermute(pair, "space", along_y(-r)) for r in (1, 2, 3)], axis=0
-    )
+    (pair,) = call(pair_kernel, [((2 * PIECE, 128), F32)], piece, first, second)
+    turned = {r: lax.ppermute(pair, "space", along_y(-r)) for r in (1, 3, 2)}
+    (mine,) = call(join_kernel, [((HALF, 128), F32)], pair, turned[1], turned[2], turned[3])
     other = lax.ppermute(mine, "space", CORE)
     factor = float((16 * PLANE) ** -0.5)
     grad_weight, grad_bias = call(
         lambda *refs: assemble_kernel(*refs, factor=factor),
-        [((864, 256), F32), ((8, 128), F32)],
+        [((864, 256), F32), ((1, OWN), F32)],
         mine,
         other,
         scratch=[pltpu.VMEM((HALF, 256), F32)],
@@ -286,7 +312,7 @@
         output[None],
         grad_inputs[None],
         grad_weight.reshape(3, 3, 3, OWN, 256),
-        grad_bias[0, :OWN],
+        grad_bias.reshape(OWN),
     )
 
 
@@ -298,7 +324,7 @@
         P("space", "filt", None),
     )
     return jax.shard_map(
-        body,
+        step,
         mesh=mesh,
         in_specs=placed,
         out_specs=(

time: 80.6 us -> 74 us (0.918)
  waiting for transfers between devices: 28.8 us -> 12.1 us
  starting transfers between devices: 36.2 us -> 49.6 us
  other arithmetic: 4.23 us -> 1.52 us
    ppermute x24, waiting for transfers between devices: 28.8 us -> 12.1 us  [the longest x3 5.73 us: step(): c1, c3, c2 = (lax.ppermute(c_own, 'filt', along_z(-r)) for r in (1, 3, 2))]
    ppermute x24, starting transfers between devices: 36.2 us -> 49.6 us  [the longest x3 12.4 us: step(): got = [lax.ppermute(parts[r], 'space', along_y(r)) for r in (1, 3, 2)]]
    concatenate x3 -> x0, other arithmetic: 1.76 us -> none  [the longest x1 0.92 us: body(): x_here = jnp.concatenate([x_own, x_other], axis=0)]
    add x3 -> x0, other arithmetic: 0.91 us -> none  [the longest x1 0.84 us: body(): piece = piece + lax.ppermute(part(r), 'space', along_y(r))]
    unnamed x10 -> x8, local copies, waits for them, and re-layouts: 1.94 us -> 2.83 us
    pallas_call x5 -> x12, Pallas kernels: 7.2 us -> 7.09 us  [call(): pl.pallas_call(kernel, out_shape=[jax.ShapeDtypeStruct(s, d) for s, d in...]
  transfers between devices with their start and end apart: 24 -> 24, of which waited for: 12 -> 8; matrix products, arithmetic and copies ran while one was open for 6% -> 2% of each run, Pallas kernels for 5% -> 5%
where the time goes in v2:
time: 74 us; the launch traced here: 73.8 us
  starting transfers between devices  49.6 us (67%)
  waiting for transfers between devices  12.1 us (16%)
  Pallas kernels  7.09 us (10%)
  local copies, waits for them, and re-layouts  2.83 us (4%)
  other arithmetic  1.52 us (2%)
  between operations  0.75 us (1%)
    ppermute x3, starting transfers between devices, step(): got = [lax.ppermute(parts[r], 'space', along_y(r)) for r in (1, 3, 2)]  12.4 us
    ppermute x3, starting transfers between devices, step(): turned = {r: lax.ppermute(pair, 'space', along_y(-r)) for r in (1, 3, 2)}  7.13 us
    pallas_call x12, Pallas kernels, call(): pl.pallas_call(kernel, out_shape=[jax.ShapeDtypeStruct(s, d) for s, d in...  7.09 us
    ppermute x3, waiting for transfers between devices, step(): c1, c3, c2 = (lax.ppermute(c_own, 'filt', along_z(-r)) for r in (1, 3, 2))  5.73 us
    ppermute x3, starting transfers between devices, step(): c1, c3, c2 = (lax.ppermute(c_own, 'filt', along_z(-r)) for r in (1, 3, 2))  4.46 us
    ppermute x1, starting transfers between devices, step(): r_core = lax.ppermute(send, 'space', CORE)  4.19 us
    ppermute x1, starting transfers between devices, step(): x_other = lax.ppermute(x_own, 'filt', ACROSS)  3.64 us
    ppermute x1, starting transfers between devices, step(): other = lax.ppermute(mine, 'space', CORE)  3.64 us
  transfers between devices with their start and end apart: 24, of which 8 were waited for; matrix products, arithmetic and copies ran while one was open for 2% of the time, Pallas kernels for 5%

profile of v2, /device:TPU:1, one launch (start us, length us, event | category | flops | bytes accessed | tf_op | source)
XLA Modules:
  0.0 73.8 jit_solution(4289352240385597140)
XLA Ops:
  0.6 3.6 %collective-permute-start = (bf16[32,2048]{1,0:T(8,128)(2,1)}, bf16[32,2048]{1,0:T(8,128)(2,1)S(1)}, u32[]{:S(2)}, u32[]{:S(2)}) collective-permute-start(bf16[32,2048]{1,0:T(8,128)(2,1)} %bitcast.10), channel_id=1, source_target_pairs={{0,16},{16,0},{32,48},{48,32},{64,80},{80,64},{96,112},{112,96},{1... | collective-permute-start | bytes 393224 | tf_op jit(solution)/shard_map/ppermute | solution.py:241
  4.3 1.0 %copy-done = bf16[3,3,3,32,256]{4,3,2,1,0:T(8,128)(2,1)S(1)} copy-done((bf16[3,3,3,32,256]{4,3,2,1,0:T(8,128)(2,1)S(1)}, bf16[3,3,3,32,256]{4,3,2,1,0:T(8,128)(2,1)}, u32[]{:S(2)}) %copy-start) | copy-done | bytes 442392
  5.3 0.9 %copy-done.1 = bf16[1,32,2048]{2,1,0:T(8,128)(2,1)S(1)} copy-done((bf16[1,32,2048]{2,1,0:T(8,128)(2,1)S(1)}, bf16[1,32,2048]{2,1,0:T(8,128)(2,1)}, u32[]{:S(2)}) %copy-start.1) | copy-done | bytes 131096
  6.2 0.9 %copy-done.2 = bf16[1,32,2048]{2,1,0:T(8,128)(2,1)S(1)} copy-done((bf16[1,32,2048]{2,1,0:T(8,128)(2,1)S(1)}, bf16[1,32,2048]{2,1,0:T(8,128)(2,1)}, u32[]{:S(2)}) %copy-start.2) | copy-done | bytes 131096
  7.4 3.0 %collective-permute-start.1 = (bf16[64,2048]{1,0:T(8,128)(2,1)S(1)}, bf16[64,2048]{1,0:T(8,128)(2,1)S(1)}, u32[]{:S(2)}, u32[]{:S(2)}) collective-permute-start(bf16[64,2048]{1,0:T(8,128)(2,1)S(1)} %shard_map.76.here_ref), channel_id=1, source_target_pairs={{0,1},{1,2},{2,3},{3,4},{4,5},{5,6},{6,7},{7,8},{8,9},{9,10},{10,1... | collective-permute-start | bytes 786440 | tf_op jit(solution)/shard_map/ppermute | solution.py:254
  10.4 3.8 %collective-permute-start.3 = (bf16[32,2048]{1,0:T(8,128)(2,1)S(1)}, bf16[32,2048]{1,0:T(8,128)(2,1)S(1)}, u32[]{:S(2)}, u32[]{:S(2)}) collective-permute-start(bf16[32,2048]{1,0:T(8,128)(2,1)S(1)} %bitcast.13), channel_id=1, source_target_pairs={{0,96},{16,112},{32,0},{48,16},{64,32},{80,48},{96,64},{112,80},{1... | collective-permute-start | bytes 393224 | tf_op jit(solution)/shard_map/ppermute | solution.py:242
  14.9 2.1 %collective-permute-done.3.c1.refs_1_ = bf16[32,2048]{1,0:T(8,128)(2,1)S(1)} collective-permute-done((bf16[32,2048]{1,0:T(8,128)(2,1)S(1)}, bf16[32,2048]{1,0:T(8,128)(2,1)S(1)}, u32[]{:S(2)}, u32[]{:S(2)}) %collective-permute-start.3) | collective-permute-done | bytes 131104 | tf_op jit(solution)/shard_map/ppermute | solution.py:242
  17.0 2.6 %collective-permute-done.4.c2.refs_2_ = bf16[32,2048]{1,0:T(8,128)(2,1)S(1)} collective-permute-done((bf16[32,2048]{1,0:T(8,128)(2,1)S(1)}, bf16[32,2048]{1,0:T(8,128)(2,1)S(1)}, u32[]{:S(2)}, u32[]{:S(2)}) %collective-permute-start.4) | collective-permute-done | bytes 131104 | tf_op jit(solution)/shard_map/ppermute | solution.py:242
  19.6 1.0 %collective-permute-done.5.c3.refs_3_ = bf16[32,2048]{1,0:T(8,128)(2,1)S(1)} collective-permute-done((bf16[32,2048]{1,0:T(8,128)(2,1)S(1)}, bf16[32,2048]{1,0:T(8,128)(2,1)S(1)}, u32[]{:S(2)}, u32[]{:S(2)}) %collective-permute-start.5) | collective-permute-done | bytes 131104 | tf_op jit(solution)/shard_map/ppermute | solution.py:242
  20.6 1.8 %shard_map.77 = (bf16[2,304,2048]{2,1,0:T(8,128)(2,1)S(1)}, f32[896,128]{1,0:T(8,128)S(1)}, f32[896,128]{1,0:T(8,128)S(1)}) custom-call(bf16[64,2048]{1,0:T(8,128)(2,1)S(1)} %collective-permute-done.1.prev_ref, bf16[64,2048]{1,0:T(8,128)(2,1)S(1)} %shard_map.76.here_ref, bf16[64,2048]{1,0:T(8,128)(2,1)S(1)} %collective-permute-done.2.next_ref, ...), custom_call_target="tpu_custom_call" | custom-call | tf_op jit(solution)/shard_map/pallas_call | solution.py:227
  22.5 4.2 %collective-permute-start.13 = (f32[896,128]{1,0:T(8,128)S(1)}, f32[896,128]{1,0:T(8,128)S(1)}, u32[]{:S(2)}, u32[]{:S(2)}) collective-permute-start(f32[896,128]{1,0:T(8,128)S(1)} %get-tuple-element.37), channel_id=1, source_target_pairs={{0,1},{1,0},{2,3},{3,2},{4,5},{5,4},{6,7},{7,6},{8,9},{9,8},{10,11... | collective-permute-start | bytes 1376264 | tf_op jit(solution)/shard_map/ppermute | solution.py:266
  27.4 0.7 collective-permute-done.13.got_ref
  28.2 1.3 %collective-permute-start.14 = (f32[448,128]{1,0:T(8,128)S(1)}, f32[448,128]{1,0:T(8,128)S(1)}, u32[]{:S(2)}, u32[]{:S(2)}) collective-permute-start(f32[448,128]{1,0:T(8,128)S(1)} %get-tuple-element.39), channel_id=1, source_target_pairs={{0,8},{1,9},{2,10},{3,11},{4,12},{5,13},{6,14},{7,15},{8,0},{9,1},... | collective-permute-start | bytes 688136 | tf_op jit(solution)/shard_map/ppermute | solution.py:272
  29.5 2.5 %collective-permute-start.6 = (bf16[864,128]{1,0:T(8,128)(2,1)S(1)}, bf16[864,128]{1,0:T(8,128)(2,1)S(1)}, u32[]{:S(2)}, u32[]{:S(2)}) collective-permute-start(bf16[864,128]{1,0:T(8,128)(2,1)S(1)} %get-tuple-element.29), channel_id=1, source_target_pairs={{0,16},{16,0},{32,48},{48,32},{64,80},{80,64},{96,112},{112,96},{1... | collective-permute-start | bytes 663560 | tf_op jit(solution)/shard_map/ppermute | solution.py:250
  31.9 1.6 %collective-permute-done.14.got_ref = f32[448,128]{1,0:T(8,128)S(1)} collective-permute-done((f32[448,128]{1,0:T(8,128)S(1)}, f32[448,128]{1,0:T(8,128)S(1)}, u32[]{:S(2)}, u32[]{:S(2)}) %collective-permute-start.14) | collective-permute-done | bytes 229408 | tf_op jit(solution)/shard_map/ppermute | solution.py:272
  33.5 2.2 %collective-permute-start.15 = (f32[112,128]{1,0:T(8,128)S(1)}, f32[112,128]{1,0:T(8,128)S(1)}, u32[]{:S(2)}, u32[]{:S(2)}) collective-permute-start(f32[112,128]{1,0:T(8,128)S(1)} %get-tuple-element.41), channel_id=1, source_target_pairs={{0,2},{1,3},{2,4},{3,5},{4,6},{5,7},{6,0},{7,1},{8,10},{9,11},{10,... | collective-permute-start | bytes 172040 | tf_op jit(solution)/shard_map/ppermute | solution.py:277
  35.7 9.1 %collective-permute-start.16 = (f32[112,128]{1,0:T(8,128)S(1)}, f32[112,128]{1,0:T(8,128)S(1)}, u32[]{:S(2)}, u32[]{:S(2)}) collective-permute-start(f32[112,128]{1,0:T(8,128)S(1)} %get-tuple-element.42), channel_id=1, source_target_pairs={{0,6},{1,7},{2,0},{3,1},{4,2},{5,3},{6,4},{7,5},{8,14},{9,15},{10,... | collective-permute-start | bytes 172040 | tf_op jit(solution)/shard_map/ppermute | solution.py:277
  44.9 1.1 %collective-permute-start.17 = (f32[112,128]{1,0:T(8,128)S(1)}, f32[112,128]{1,0:T(8,128)S(1)}, u32[]{:S(2)}, u32[]{:S(2)}) collective-permute-start(f32[112,128]{1,0:T(8,128)S(1)} %get-tuple-element.43), channel_id=1, source_target_pairs={{0,4},{1,5},{2,6},{3,7},{4,0},{5,1},{6,2},{7,3},{8,12},{9,13},{10,... | collective-permute-start | bytes 172040 | tf_op jit(solution)/shard_map/ppermute | solution.py:277
  46.0 1.4 %shard_map.78 = (f32[32,2048]{1,0:T(8,128)S(1)}, f32[32,2048]{1,0:T(8,128)S(1)}, f32[32,2048]{1,0:T(8,128)S(1)}, f32[32,2048]{1,0:T(8,128)S(1)}) custom-call(bf16[2,304,2048]{2,1,0:T(8,128)(2,1)S(1)} %get-tuple-element.27.xs_ref, bf16[864,128]{1,0:T(8,128)(2,1)S(1)} %get-tuple-element.28.wa_ref, bf16[864,128]{1,0:T(8,128)(2,1)S(1)} %collective-permute-done.6.wb_ref), custom_call_target="tpu_custom_call" | custom-call | tf_op jit(solution)/shard_map/pallas_call | solution.py:227
  48.4 1.1 %collective-permute-done.17.d = f32[112,128]{1,0:T(8,128)S(1)} collective-permute-done((f32[112,128]{1,0:T(8,128)S(1)}, f32[112,128]{1,0:T(8,128)S(1)}, u32[]{:S(2)}, u32[]{:S(2)}) %collective-permute-start.17) | collective-permute-done | bytes 57376 | tf_op jit(solution)/shard_map/ppermute | solution.py:277
  49.5 2.6 %collective-permute-start.18 = (f32[112,128]{1,0:T(8,128)S(1)}, f32[112,128]{1,0:T(8,128)S(1)}, u32[]{:S(2)}, u32[]{:S(2)}) collective-permute-start(f32[112,128]{1,0:T(8,128)S(1)} %shard_map.83.piece_ref), channel_id=1, source_target_pairs={{0,8},{1,17},{2,10},{3,19},{4,12},{5,21},{6,14},{7,23},{8,0},{9,25... | collective-permute-start | bytes 172040 | tf_op jit(solution)/shard_map/ppermute | solution.py:285
  52.2 0.9 %collective-permute-start.19 = (f32[112,128]{1,0:T(8,128)S(1)}, f32[112,128]{1,0:T(8,128)S(1)}, u32[]{:S(2)}, u32[]{:S(2)}) collective-permute-start(f32[112,128]{1,0:T(8,128)S(1)} %shard_map.83.piece_ref), channel_id=1, source_target_pairs={{0,8},{1,25},{2,10},{3,27},{4,12},{5,29},{6,14},{7,31},{8,0},{9,17... | collective-permute-start | bytes 172040 | tf_op jit(solution)/shard_map/ppermute | solution.py:286
  53.1 1.5 %shard_map.80 = (f32[32,2048]{1,0:T(8,128)S(1)}, f32[32,2048]{1,0:T(8,128)S(1)}) custom-call(bf16[128,2048]{1,0:T(8,128)(2,1)S(1)} %collective-permute-done.10.prev_ref, bf16[128,2048]{1,0:T(8,128)(2,1)S(1)} %collective-permute-done.11.next_ref, bf16[32,2048]{1,0:T(8,128)(2,1)S(1)} %get-tuple-element.26.c0.refs_0_, ...), custom_call_target="tpu_custom_call" | custom-call | tf_op jit(solution)/shard_map/pallas_call | solution.py:227
  54.5 2.2 %collective-permute-start.12 = (f32[32,2048]{1,0:T(8,128)S(1)}, f32[32,2048]{1,0:T(8,128)S(1)}, u32[]{:S(2)}, u32[]{:S(2)}) collective-permute-start(f32[32,2048]{1,0:T(8,128)S(1)} %get-tuple-element.35), channel_id=1, source_target_pairs={{0,16},{16,0},{32,48},{48,32},{64,80},{80,64},{96,112},{112,96},{1... | collective-permute-start | bytes 786440 | tf_op jit(solution)/shard_map/ppermute | solution.py:297
  56.7 2.4 %collective-permute-start.20 = (f32[224,128]{1,0:T(8,128)S(1)}, f32[224,128]{1,0:T(8,128)S(1)}, u32[]{:S(2)}, u32[]{:S(2)}) collective-permute-start(f32[224,128]{1,0:T(8,128)S(1)} %shard_map.84.refs_0_), channel_id=1, source_target_pairs={{0,6},{1,7},{2,0},{3,1},{4,2},{5,3},{6,4},{7,5},{8,14},{9,15},{10,... | collective-permute-start | bytes 344072 | tf_op jit(solution)/shard_map/ppermute | solution.py:300
  59.1 1.5 %collective-permute-start.21 = (f32[224,128]{1,0:T(8,128)S(1)}, f32[224,128]{1,0:T(8,128)S(1)}, u32[]{:S(2)}, u32[]{:S(2)}) collective-permute-start(f32[224,128]{1,0:T(8,128)S(1)} %shard_map.84.refs_0_), channel_id=1, source_target_pairs={{0,4},{1,5},{2,6},{3,7},{4,0},{5,1},{6,2},{7,3},{8,12},{9,13},{10,... | collective-permute-start | bytes 344072 | tf_op jit(solution)/shard_map/ppermute | solution.py:300
  60.6 3.3 %collective-permute-start.22 = (f32[224,128]{1,0:T(8,128)S(1)}, f32[224,128]{1,0:T(8,128)S(1)}, u32[]{:S(2)}, u32[]{:S(2)}) collective-permute-start(f32[224,128]{1,0:T(8,128)S(1)} %shard_map.84.refs_0_), channel_id=1, source_target_pairs={{0,2},{1,3},{2,4},{3,5},{4,6},{5,7},{6,0},{7,1},{8,10},{9,11},{10,... | collective-permute-start | bytes 344072 | tf_op jit(solution)/shard_map/ppermute | solution.py:300
  63.9 0.8 %add_bitcast_fusion.1 = f32[1,32,2048]{2,1,0:T(8,128)} fusion(f32[32,2048]{1,0:T(8,128)S(1)} %collective-permute-done.9, f32[32,2048]{1,0:T(8,128)S(1)} %collective-permute-done.8, f32[32,2048]{1,0:T(8,128)S(1)} %get-tuple-element.30, f32[32,2048]{1,0:T(8,128)S(1)} %collective-permute-done.7, f32[32]{0:T(128)S(1)} %convert_element_type.3), kind=kLoop, calls=%fused_computation.1 | loop fusion | flops 262144 | bytes 1310848 | tf_op jit(solution)/shard_map/broadcast_in_dim | solution.py:312
  64.7 2.2 %collective-permute-done.22.refs_3_ = f32[224,128]{1,0:T(8,128)S(1)} collective-permute-done((f32[224,128]{1,0:T(8,128)S(1)}, f32[224,128]{1,0:T(8,128)S(1)}, u32[]{:S(2)}, u32[]{:S(2)}) %collective-permute-start.22) | collective-permute-done | bytes 114720 | tf_op jit(solution)/shard_map/ppermute | solution.py:300
  66.9 3.6 %collective-permute-start.23 = (f32[896,128]{1,0:T(8,128)S(1)}, f32[896,128]{1,0:T(8,128)S(1)}, u32[]{:S(2)}, u32[]{:S(2)}) collective-permute-start(f32[896,128]{1,0:T(8,128)S(1)} %shard_map.85.refs_0_), channel_id=1, source_target_pairs={{0,1},{1,0},{2,3},{3,2},{4,5},{5,4},{6,7},{7,6},{8,9},{9,8},{10,11... | collective-permute-start | bytes 1376264 | tf_op jit(solution)/shard_map/ppermute | solution.py:302
  70.5 0.7 add_bitcast_fusion
  72.0 1.9 %shard_map.86 = (f32[864,256]{1,0:T(8,128)}, f32[1,32]{1,0:T(1,128)}) custom-call(f32[896,128]{1,0:T(8,128)S(1)} %shard_map.85.refs_0_, f32[896,128]{1,0:T(8,128)S(1)} %collective-permute-done.23.refs_1_), custom_call_target="tpu_custom_call" | custom-call | tf_op jit(solution)/shard_map/pallas_call | solution.py:227
  (39 shorter events, 3.6 us)
Async XLA Ops:
  0.6 6.8 %collective-permute-start = (bf16[32,2048]{1,0:T(8,128)(2,1)}, bf16[32,2048]{1,0:T(8,128)(2,1)S(1)}, u32[]{:S(2)}, u32[]{:S(2)}) collective-permute-start(bf16[32,2048]{1,0:T(8,128)(2,1)} %bitcast.10), channel_id=1, source_target_pairs={{0,16},{16,0},{32,48},{48,32},{64,80},{80,64},{96,112},{112,96},{1... | collective-permute-start | bytes 393224 | tf_op jit(solution)/shard_map/ppermute | solution.py:241
  4.3 1.0 %copy-start = (bf16[3,3,3,32,256]{4,3,2,1,0:T(8,128)(2,1)S(1)}, bf16[3,3,3,32,256]{4,3,2,1,0:T(8,128)(2,1)}, u32[]{:S(2)}) copy-start(bf16[3,3,3,32,256]{4,3,2,1,0:T(8,128)(2,1)} %param.5) | copy-start | bytes 1327108
  5.3 0.9 %copy-start.1 = (bf16[1,32,2048]{2,1,0:T(8,128)(2,1)S(1)}, bf16[1,32,2048]{2,1,0:T(8,128)(2,1)}, u32[]{:S(2)}) copy-start(bf16[1,32,2048]{2,1,0:T(8,128)(2,1)} %param.4) | copy-start | bytes 393220
  6.2 0.9 %copy-start.2 = (bf16[1,32,2048]{2,1,0:T(8,128)(2,1)S(1)}, bf16[1,32,2048]{2,1,0:T(8,128)(2,1)}, u32[]{:S(2)}) copy-start(bf16[1,32,2048]{2,1,0:T(8,128)(2,1)} %param.7) | copy-start | bytes 393220
  7.4 13.2 %collective-permute-start.1 = (bf16[64,2048]{1,0:T(8,128)(2,1)S(1)}, bf16[64,2048]{1,0:T(8,128)(2,1)S(1)}, u32[]{:S(2)}, u32[]{:S(2)}) collective-permute-start(bf16[64,2048]{1,0:T(8,128)(2,1)S(1)} %shard_map.76.here_ref), channel_id=1, source_target_pairs={{0,1},{1,2},{2,3},{3,4},{4,5},{5,6},{6,7},{7,8},{8,9},{9,10},{10,1... | collective-permute-start | bytes 786440 | tf_op jit(solution)/shard_map/ppermute | solution.py:254
  10.4 10.2 %collective-permute-start.2 = (bf16[64,2048]{1,0:T(8,128)(2,1)S(1)}, bf16[64,2048]{1,0:T(8,128)(2,1)S(1)}, u32[]{:S(2)}, u32[]{:S(2)}) collective-permute-start(bf16[64,2048]{1,0:T(8,128)(2,1)S(1)} %shard_map.76.here_ref), channel_id=1, source_target_pairs={{1,0},{2,1},{3,2},{4,3},{5,4},{6,5},{7,6},{8,7},{9,8},{10,9},{11,1... | collective-permute-start | bytes 786440 | tf_op jit(solution)/shard_map/ppermute | solution.py:255
  10.4 6.5 %collective-permute-start.3 = (bf16[32,2048]{1,0:T(8,128)(2,1)S(1)}, bf16[32,2048]{1,0:T(8,128)(2,1)S(1)}, u32[]{:S(2)}, u32[]{:S(2)}) collective-permute-start(bf16[32,2048]{1,0:T(8,128)(2,1)S(1)} %bitcast.13), channel_id=1, source_target_pairs={{0,96},{16,112},{32,0},{48,16},{64,32},{80,48},{96,64},{112,80},{1... | collective-permute-start | bytes 393224 | tf_op jit(solution)/shard_map/ppermute | solution.py:242
  14.2 5.4 %collective-permute-start.4 = (bf16[32,2048]{1,0:T(8,128)(2,1)S(1)}, bf16[32,2048]{1,0:T(8,128)(2,1)S(1)}, u32[]{:S(2)}, u32[]{:S(2)}) collective-permute-start(bf16[32,2048]{1,0:T(8,128)(2,1)S(1)} %bitcast.14), channel_id=1, source_target_pairs={{0,64},{16,80},{32,96},{48,112},{64,0},{80,16},{96,32},{112,48},{1... | collective-permute-start | bytes 393224 | tf_op jit(solution)/shard_map/ppermute | solution.py:242
  14.2 6.4 %collective-permute-start.5 = (bf16[32,2048]{1,0:T(8,128)(2,1)S(1)}, bf16[32,2048]{1,0:T(8,128)(2,1)S(1)}, u32[]{:S(2)}, u32[]{:S(2)}) collective-permute-start(bf16[32,2048]{1,0:T(8,128)(2,1)S(1)} %bitcast.15), channel_id=1, source_target_pairs={{0,32},{16,48},{32,64},{48,80},{64,96},{80,112},{96,0},{112,16},{1... | collective-permute-start | bytes 393224 | tf_op jit(solution)/shard_map/ppermute | solution.py:242
  22.5 5.6 %collective-permute-start.13 = (f32[896,128]{1,0:T(8,128)S(1)}, f32[896,128]{1,0:T(8,128)S(1)}, u32[]{:S(2)}, u32[]{:S(2)}) collective-permute-start(f32[896,128]{1,0:T(8,128)S(1)} %get-tuple-element.37), channel_id=1, source_target_pairs={{0,1},{1,0},{2,3},{3,2},{4,5},{5,4},{6,7},{7,6},{8,9},{9,8},{10,11... | collective-permute-start | bytes 1376264 | tf_op jit(solution)/shard_map/ppermute | solution.py:266
  26.7 26.3 %copy-start.3 = (bf16[32]{0:T(256)(128)(2,1)S(1)}, bf16[32]{0:T(256)(128)(2,1)}, u32[]{:S(2)}) copy-start(bf16[32]{0:T(256)(128)(2,1)} %param.6) | copy-start | bytes 196
  26.7 22.8 %collective-permute-start.10 = (bf16[128,2048]{1,0:T(8,128)(2,1)S(1)}, bf16[128,2048]{1,0:T(8,128)(2,1)S(1)}, u32[]{:S(2)}, u32[]{:S(2)}) collective-permute-start(bf16[128,2048]{1,0:T(8,128)(2,1)S(1)} %shard_map.79), channel_id=1, source_target_pairs={{0,1},{1,2},{2,3},{3,4},{4,5},{5,6},{6,7},{7,8},{8,9},{9,10},{10,1... | collective-permute-start | bytes 1572872 | tf_op jit(solution)/shard_map/ppermute | solution.py:273
  27.4 24.8 %collective-permute-start.11 = (bf16[128,2048]{1,0:T(8,128)(2,1)S(1)}, bf16[128,2048]{1,0:T(8,128)(2,1)S(1)}, u32[]{:S(2)}, u32[]{:S(2)}) collective-permute-start(bf16[128,2048]{1,0:T(8,128)(2,1)S(1)} %shard_map.79), channel_id=1, source_target_pairs={{1,0},{2,1},{3,2},{4,3},{5,4},{6,5},{7,6},{8,7},{9,8},{10,9},{11,1... | collective-permute-start | bytes 1572872 | tf_op jit(solution)/shard_map/ppermute | solution.py:274
  28.2 5.4 %collective-permute-start.14 = (f32[448,128]{1,0:T(8,128)S(1)}, f32[448,128]{1,0:T(8,128)S(1)}, u32[]{:S(2)}, u32[]{:S(2)}) collective-permute-start(f32[448,128]{1,0:T(8,128)S(1)} %get-tuple-element.39), channel_id=1, source_target_pairs={{0,8},{1,9},{2,10},{3,11},{4,12},{5,13},{6,14},{7,15},{8,0},{9,1},... | collective-permute-start | bytes 688136 | tf_op jit(solution)/shard_map/ppermute | solution.py:272
  29.5 15.4 %collective-permute-start.6 = (bf16[864,128]{1,0:T(8,128)(2,1)S(1)}, bf16[864,128]{1,0:T(8,128)(2,1)S(1)}, u32[]{:S(2)}, u32[]{:S(2)}) collective-permute-start(bf16[864,128]{1,0:T(8,128)(2,1)S(1)} %get-tuple-element.29), channel_id=1, source_target_pairs={{0,16},{16,0},{32,48},{48,32},{64,80},{80,64},{96,112},{112,96},{1... | collective-permute-start | bytes 663560 | tf_op jit(solution)/shard_map/ppermute | solution.py:250
  33.5 13.9 %collective-permute-start.15 = (f32[112,128]{1,0:T(8,128)S(1)}, f32[112,128]{1,0:T(8,128)S(1)}, u32[]{:S(2)}, u32[]{:S(2)}) collective-permute-start(f32[112,128]{1,0:T(8,128)S(1)} %get-tuple-element.41), channel_id=1, source_target_pairs={{0,2},{1,3},{2,4},{3,5},{4,6},{5,7},{6,0},{7,1},{8,10},{9,11},{10,... | collective-permute-start | bytes 172040 | tf_op jit(solution)/shard_map/ppermute | solution.py:277
  35.7 12.2 %collective-permute-start.16 = (f32[112,128]{1,0:T(8,128)S(1)}, f32[112,128]{1,0:T(8,128)S(1)}, u32[]{:S(2)}, u32[]{:S(2)}) collective-permute-start(f32[112,128]{1,0:T(8,128)S(1)} %get-tuple-element.42), channel_id=1, source_target_pairs={{0,6},{1,7},{2,0},{3,1},{4,2},{5,3},{6,4},{7,5},{8,14},{9,15},{10,... | collective-permute-start | bytes 172040 | tf_op jit(solution)/shard_map/ppermute | solution.py:277
  44.9 4.6 %collective-permute-start.17 = (f32[112,128]{1,0:T(8,128)S(1)}, f32[112,128]{1,0:T(8,128)S(1)}, u32[]{:S(2)}, u32[]{:S(2)}) collective-permute-start(f32[112,128]{1,0:T(8,128)S(1)} %get-tuple-element.43), channel_id=1, source_target_pairs={{0,4},{1,5},{2,6},{3,7},{4,0},{5,1},{6,2},{7,3},{8,12},{9,13},{10,... | collective-permute-start | bytes 172040 | tf_op jit(solution)/shard_map/ppermute | solution.py:277
  47.4 11.7 %collective-permute-start.9 = (f32[32,2048]{1,0:T(8,128)S(1)}, f32[32,2048]{1,0:T(8,128)S(1)}, u32[]{:S(2)}, u32[]{:S(2)}) collective-permute-start(f32[32,2048]{1,0:T(8,128)S(1)} %get-tuple-element.33), channel_id=1, source_target_pairs={{0,64},{16,80},{32,96},{48,112},{64,0},{80,16},{96,32},{112,48},{1... | collective-permute-start | bytes 786440 | tf_op jit(solution)/shard_map/ppermute | solution.py:282
  47.9 12.7 %collective-permute-start.8 = (f32[32,2048]{1,0:T(8,128)S(1)}, f32[32,2048]{1,0:T(8,128)S(1)}, u32[]{:S(2)}, u32[]{:S(2)}) collective-permute-start(f32[32,2048]{1,0:T(8,128)S(1)} %get-tuple-element.32), channel_id=1, source_target_pairs={{0,96},{16,112},{32,0},{48,16},{64,32},{80,48},{96,64},{112,80},{1... | collective-permute-start | bytes 786440 | tf_op jit(solution)/shard_map/ppermute | solution.py:282
  49.5 14.4 %collective-permute-start.7 = (f32[32,2048]{1,0:T(8,128)S(1)}, f32[32,2048]{1,0:T(8,128)S(1)}, u32[]{:S(2)}, u32[]{:S(2)}) collective-permute-start(f32[32,2048]{1,0:T(8,128)S(1)} %get-tuple-element.31), channel_id=1, source_target_pairs={{0,32},{16,48},{32,64},{48,80},{64,96},{80,112},{96,0},{112,16},{1... | collective-permute-start | bytes 786440 | tf_op jit(solution)/shard_map/ppermute | solution.py:282
  49.5 5.0 %collective-permute-start.18 = (f32[112,128]{1,0:T(8,128)S(1)}, f32[112,128]{1,0:T(8,128)S(1)}, u32[]{:S(2)}, u32[]{:S(2)}) collective-permute-start(f32[112,128]{1,0:T(8,128)S(1)} %shard_map.83.piece_ref), channel_id=1, source_target_pairs={{0,8},{1,17},{2,10},{3,19},{4,12},{5,21},{6,14},{7,23},{8,0},{9,25... | collective-permute-start | bytes 172040 | tf_op jit(solution)/shard_map/ppermute | solution.py:285
  52.2 4.5 %collective-permute-start.19 = (f32[112,128]{1,0:T(8,128)S(1)}, f32[112,128]{1,0:T(8,128)S(1)}, u32[]{:S(2)}, u32[]{:S(2)}) collective-permute-start(f32[112,128]{1,0:T(8,128)S(1)} %shard_map.83.piece_ref), channel_id=1, source_target_pairs={{0,8},{1,25},{2,10},{3,27},{4,12},{5,29},{6,14},{7,31},{8,0},{9,17... | collective-permute-start | bytes 172040 | tf_op jit(solution)/shard_map/ppermute | solution.py:286
  54.5 16.0 %collective-permute-start.12 = (f32[32,2048]{1,0:T(8,128)S(1)}, f32[32,2048]{1,0:T(8,128)S(1)}, u32[]{:S(2)}, u32[]{:S(2)}) collective-permute-start(f32[32,2048]{1,0:T(8,128)S(1)} %get-tuple-element.35), channel_id=1, source_target_pairs={{0,16},{16,0},{32,48},{48,32},{64,80},{80,64},{96,112},{112,96},{1... | collective-permute-start | bytes 786440 | tf_op jit(solution)/shard_map/ppermute | solution.py:297
  56.7 7.9 %collective-permute-start.20 = (f32[224,128]{1,0:T(8,128)S(1)}, f32[224,128]{1,0:T(8,128)S(1)}, u32[]{:S(2)}, u32[]{:S(2)}) collective-permute-start(f32[224,128]{1,0:T(8,128)S(1)} %shard_map.84.refs_0_), channel_id=1, source_target_pairs={{0,6},{1,7},{2,0},{3,1},{4,2},{5,3},{6,4},{7,5},{8,14},{9,15},{10,... | collective-permute-start | bytes 344072 | tf_op jit(solution)/shard_map/ppermute | solution.py:300
  59.1 5.5 %collective-permute-start.21 = (f32[224,128]{1,0:T(8,128)S(1)}, f32[224,128]{1,0:T(8,128)S(1)}, u32[]{:S(2)}, u32[]{:S(2)}) collective-permute-start(f32[224,128]{1,0:T(8,128)S(1)} %shard_map.84.refs_0_), channel_id=1, source_target_pairs={{0,4},{1,5},{2,6},{3,7},{4,0},{5,1},{6,2},{7,3},{8,12},{9,13},{10,... | collective-permute-start | bytes 344072 | tf_op jit(solution)/shard_map/ppermute | solution.py:300
  60.6 6.2 %collective-permute-start.22 = (f32[224,128]{1,0:T(8,128)S(1)}, f32[224,128]{1,0:T(8,128)S(1)}, u32[]{:S(2)}, u32[]{:S(2)}) collective-permute-start(f32[224,128]{1,0:T(8,128)S(1)} %shard_map.84.refs_0_), channel_id=1, source_target_pairs={{0,2},{1,3},{2,4},{3,5},{4,6},{5,7},{6,0},{7,1},{8,10},{9,11},{10,... | collective-permute-start | bytes 344072 | tf_op jit(solution)/shard_map/ppermute | solution.py:300
  66.9 5.1 %collective-permute-start.23 = (f32[896,128]{1,0:T(8,128)S(1)}, f32[896,128]{1,0:T(8,128)S(1)}, u32[]{:S(2)}, u32[]{:S(2)}) collective-permute-start(f32[896,128]{1,0:T(8,128)S(1)} %shard_map.85.refs_0_), channel_id=1, source_target_pairs={{0,1},{1,0},{2,3},{3,2},{4,5},{5,4},{6,7},{7,6},{8,9},{9,8},{10,11... | collective-permute-start | bytes 1376264 | tf_op jit(solution)/shard_map/ppermute | solution.py:302

commit v3 on v2

--- a/solution.py
+++ b/solution.py
@@ -54,9 +54,13 @@
     return lax.broadcasted_iota(jnp.int32, shape, 1)
 
 
-def select_kernel(w_ref, x_ref, c_ref, mine_ref, theirs_ref, x_out, c_out):
-    x_out[...] = x_ref[...]
-    c_out[...] = c_ref[...]
+def select_kernel(w_hbm, x_hbm, c_hbm, mine_ref, theirs_ref, x_out, c_out, w_ref, sems):
+    copies = [
+        pltpu.make_async_copy(a, b, sems.at[i])
+        for i, (a, b) in enumerate(((w_hbm, w_ref), (x_hbm, x_out), (c_hbm, c_out)))
+    ]
+    for copy in copies:
+        copy.start()
     filt = lax.axis_index("filt")
     z, xh = filt // 2, filt % 2
     src = lax.broadcasted_iota(jnp.int32, (256, 256), 0)
@@ -64,6 +68,8 @@
     side, turn, chan = lane >> 7, (lane >> 5) & 3, lane & 31
     want = ((z + turn) & 3) * 64 + ((xh + side) & 1) * 32 + chan
     pick = jnp.where(src == want, 1.0, 0.0).astype(BF)
+    for copy in copies:
+        copy.wait()
     got = jnp.dot(w_ref[...], pick, preferred_element_type=F32).astype(BF)
     mine_ref[...] = got[:, :128]
     theirs_ref[...] = got[:, 128:]
@@ -186,9 +192,13 @@
     lane = lax.broadcasted_iota(jnp.int32, (256, 256), 1)
     side, turn, chan = src >> 7, (src >> 5) & 3, src & 31
     want = ((z + turn) & 3) * 64 + ((xh + core + side) & 1) * 32 + chan
-    pick = jnp.where(lane == want, 1.0, 0.0)
-    got = jnp.dot(both_ref[: 3 * TAPS, :], pick, precision=lax.Precision.HIGHEST, preferred_element_type=F32)
-    got = got * factor
+    pick = jnp.where(lane == want, 1.0, 0.0).astype(BF)
+    left = both_ref[: 3 * TAPS, :] * factor
+    got = jnp.zeros(left.shape, F32)
+    for _ in range(3):
+        part = left.astype(BF)
+        left = left - part.astype(F32)
+        got = got + jnp.dot(part, pick, preferred_element_type=F32)
     for kd in range(3):
         for kh in range(3):
             grad_ref[(kd * 3 + kh) * 96 : (kd * 3 + kh) * 96 + 96, :] = got[
@@ -213,6 +223,21 @@
         out[...] = keep_ref[rows, :] + got_ref[rows, :]
 
 
+def bias_kernel(ref, out):
+    row = lax.broadcasted_iota(jnp.int32, (OWN, OWN), 0)
+    col = lax.broadcasted_iota(jnp.int32, (OWN, OWN), 1)
+    wide = jnp.where(row == col, ref[...].astype(F32), 0.0)
+    out[...] = jnp.sum(wide, axis=1, keepdims=True)
+
+
+def output_kernel(a, b, c, d, bias_ref, out):
+    out[...] = (a[...] + b[...]) + (c[...] + d[...]) + bias_ref[...]
+
+
+def add2_kernel(a, b, out):
+    out[...] = a[...] + b[...]
+
+
 def add4_kernel(a, b, c, d, out):
     out[...] = (a[...] + b[...]) + (c[...] + d[...])
 
@@ -223,11 +248,11 @@
     out_ref[PIECE:, :] = jnp.where(even, first_ref[...], second_ref[...])
 
 
-def call(kernel, outs, *args, scratch=()):
+def call(kernel, outs, *args, scratch=(), space=VM):
     return pl.pallas_call(
         kernel,
         out_shape=[jax.ShapeDtypeStruct(s, d) for s, d in outs],
-        in_specs=[VM] * len(args),
+        in_specs=[space] * len(args),
         out_specs=[VM] * len(outs),
         scratch_shapes=list(scratch),
         compiler_params=PARAMS,
@@ -243,9 +268,9 @@
     w_mine, w_theirs, x_near, c_near = call(
         select_kernel,
         [((864, 128), BF), ((864, 128), BF), ((OWN, PLANE), BF), ((OWN, PLANE), BF)],
-        weight.reshape(864, 256),
-        x_own,
-        c_own,
+        *(pltpu.with_memory_space_constraint(v, pltpu.HBM) for v in (weight.reshape(864, 256), x_own, c_own)),
+        scratch=[pltpu.VMEM((864, 256), BF), pltpu.SemaphoreType.DMA((3,))],
+        space=pl.BlockSpec(memory_space=pltpu.HBM),
     )
     w_other = lax.ppermute(w_theirs, "filt", ACROSS)
     cots = [c_near, c1, c2, c3]
@@ -277,10 +302,9 @@
     got = [lax.ppermute(parts[r], "space", along_y(r)) for r in (1, 3, 2)]
     (piece,) = call(add4_kernel, [((PIECE, 128), F32)], parts[0], *got)
 
-    summed = outs[0]
-    for r in (1, 3, 2):
-        summed = summed + lax.ppermute(outs[r], "filt", along_z(r))
-    output = summed + bias.astype(F32)[:, None]
+    (wide_bias,) = call(bias_kernel, [((OWN, 1), F32)], bias.reshape(1, OWN))
+    sums = [lax.ppermute(outs[r], "filt", along_z(r)) for r in (1, 3, 2)]
+    (output,) = call(output_kernel, [((OWN, PLANE), F32)], outs[0], *sums, wide_bias)
 
     first = lax.ppermute(piece, ("filt", "space"), swapped(0))
     second = lax.ppermute(piece, ("filt", "space"), swapped(8))
@@ -294,7 +318,8 @@
         w_other,
         scratch=[pltpu.VMEM((9 * 128, PLANE), BF)],
     )
-    grad_inputs = g_mine + lax.ppermute(g_theirs, "filt", ACROSS)
+    g_other = lax.ppermute(g_theirs, "filt", ACROSS)
+    (grad_inputs,) = call(add2_kernel, [((OWN, PLANE), F32)], g_mine, g_other)
 
     (pair,) = call(pair_kernel, [((2 * PIECE, 128), F32)], piece, first, second)
     turned = {r: lax.ppermute(pair, "space", along_y(-r)) for r in (1, 3, 2)}

time: 74 us -> 85.7 us (1.16)
  the two profiles are of different devices: /device:TPU:1 before, /device:TPU:24 now
where the time goes in v3:
time: 85.7 us; the launch traced here: 85.5 us
  waiting for transfers between devices  43.8 us (51%)
  starting transfers between devices  31.5 us (37%)
  Pallas kernels  9.45 us (11%)
    pallas_call x15, Pallas kernels, call(): pl.pallas_call(kernel, out_shape=[jax.ShapeDtypeStruct(s, d) for s, d in...  9.45 us
    ppermute x3, waiting for transfers between devices, step(): sums = [lax.ppermute(outs[r], 'filt', along_z(r)) for r in (1, 3, 2)]  8.14 us
    ppermute x3, waiting for transfers between devices, step(): c1, c3, c2 = (lax.ppermute(c_own, 'filt', along_z(-r)) for r in (1, 3, 2))  7.61 us
    ppermute x1, waiting for transfers between devices, step(): r_xlo = lax.ppermute(r_send, 'space', XLO)  5.8 us
    ppermute x1, waiting for transfers between devices, step(): w_other = lax.ppermute(w_theirs, 'filt', ACROSS)  5.3 us
    ppermute x3, starting transfers between devices, step(): c1, c3, c2 = (lax.ppermute(c_own, 'filt', along_z(-r)) for r in (1, 3, 2))  5.3 us
    ppermute x3, waiting for transfers between devices, step(): got = [lax.ppermute(parts[r], 'space', along_y(r)) for r in (1, 3, 2)]  4.98 us
    ppermute x3, starting transfers between devices, step(): sums = [lax.ppermute(outs[r], 'filt', along_z(r)) for r in (1, 3, 2)]  4.66 us
  transfers between devices with their start and end apart: 24, of which 13 were waited for; matrix products, arithmetic and copies ran while one was open for 0% of the time, Pallas kernels for 7%

profile of v3, /device:TPU:24, one launch (start us, length us, event | category | flops | bytes accessed | tf_op | source)
XLA Modules:
  0.0 85.5 jit_solution(7520947783705488719)
XLA Ops:
  0.6 3.1 %collective-permute-start = (bf16[32,2048]{1,0:T(8,128)(2,1)}, bf16[32,2048]{1,0:T(8,128)(2,1)S(1)}, u32[]{:S(2)}, u32[]{:S(2)}) collective-permute-start(bf16[32,2048]{1,0:T(8,128)(2,1)} %bitcast.12), channel_id=1, source_target_pairs={{0,16},{16,0},{32,48},{48,32},{64,80},{80,64},{96,112},{112,96},{1... | collective-permute-start | bytes 393224 | tf_op jit(solution)/shard_map/ppermute | solution.py:266
  3.7 1.4 %shard_map.75 = (bf16[864,128]{1,0:T(8,128)(2,1)S(1)}, bf16[864,128]{1,0:T(8,128)(2,1)S(1)}, bf16[32,2048]{1,0:T(8,128)(2,1)S(1)}, bf16[32,2048]{1,0:T(8,128)(2,1)S(1)}) custom-call(bf16[864,256]{1,0:T(8,128)(2,1)} %bitcast.9, bf16[32,2048]{1,0:T(8,128)(2,1)} %bitcast.13, bf16[32,2048]{1,0:T(8,128)(2,1)} %bitcast.14), custom_call_target="tpu_custom_call" | custom-call | tf_op jit(solution)/shard_map/pallas_call | solution.py:252
  5.1 2.5 %collective-permute-done.refs_1_ = bf16[32,2048]{1,0:T(8,128)(2,1)S(1)} collective-permute-done((bf16[32,2048]{1,0:T(8,128)(2,1)}, bf16[32,2048]{1,0:T(8,128)(2,1)S(1)}, u32[]{:S(2)}, u32[]{:S(2)}) %collective-permute-start) | collective-permute-done | bytes 131104 | tf_op jit(solution)/shard_map/ppermute | solution.py:266
  7.8 1.7 %collective-permute-start.2 = (bf16[64,2048]{1,0:T(8,128)(2,1)S(1)}, bf16[64,2048]{1,0:T(8,128)(2,1)S(1)}, u32[]{:S(2)}, u32[]{:S(2)}) collective-permute-start(bf16[64,2048]{1,0:T(8,128)(2,1)S(1)} %shard_map.76.here_ref), channel_id=1, source_target_pairs={{1,0},{2,1},{3,2},{4,3},{5,4},{6,5},{7,6},{8,7},{9,8},{10,9},{11,1... | collective-permute-start | bytes 786440 | tf_op jit(solution)/shard_map/ppermute | solution.py:280
  9.5 4.0 %collective-permute-start.3 = (bf16[32,2048]{1,0:T(8,128)(2,1)}, bf16[32,2048]{1,0:T(8,128)(2,1)S(1)}, u32[]{:S(2)}, u32[]{:S(2)}) collective-permute-start(bf16[32,2048]{1,0:T(8,128)(2,1)} %bitcast.15), channel_id=1, source_target_pairs={{0,96},{16,112},{32,0},{48,16},{64,32},{80,48},{96,64},{112,80},{1... | collective-permute-start | bytes 393224 | tf_op jit(solution)/shard_map/ppermute | solution.py:267
  13.5 1.3 %collective-permute-start.5 = (bf16[32,2048]{1,0:T(8,128)(2,1)}, bf16[32,2048]{1,0:T(8,128)(2,1)S(1)}, u32[]{:S(2)}, u32[]{:S(2)}) collective-permute-start(bf16[32,2048]{1,0:T(8,128)(2,1)} %bitcast.17), channel_id=1, source_target_pairs={{0,32},{16,48},{32,64},{48,80},{64,96},{80,112},{96,0},{112,16},{1... | collective-permute-start | bytes 393224 | tf_op jit(solution)/shard_map/ppermute | solution.py:267
  14.8 4.3 %collective-permute-done.3.c1.refs_1_ = bf16[32,2048]{1,0:T(8,128)(2,1)S(1)} collective-permute-done((bf16[32,2048]{1,0:T(8,128)(2,1)}, bf16[32,2048]{1,0:T(8,128)(2,1)S(1)}, u32[]{:S(2)}, u32[]{:S(2)}) %collective-permute-start.3) | collective-permute-done | bytes 131104 | tf_op jit(solution)/shard_map/ppermute | solution.py:267
  19.1 2.2 %collective-permute-done.4.c2.refs_2_ = bf16[32,2048]{1,0:T(8,128)(2,1)S(1)} collective-permute-done((bf16[32,2048]{1,0:T(8,128)(2,1)}, bf16[32,2048]{1,0:T(8,128)(2,1)S(1)}, u32[]{:S(2)}, u32[]{:S(2)}) %collective-permute-start.4) | collective-permute-done | bytes 131104 | tf_op jit(solution)/shard_map/ppermute | solution.py:267
  21.3 1.1 %collective-permute-done.5.c3.refs_3_ = bf16[32,2048]{1,0:T(8,128)(2,1)S(1)} collective-permute-done((bf16[32,2048]{1,0:T(8,128)(2,1)}, bf16[32,2048]{1,0:T(8,128)(2,1)S(1)}, u32[]{:S(2)}, u32[]{:S(2)}) %collective-permute-start.5) | collective-permute-done | bytes 131104 | tf_op jit(solution)/shard_map/ppermute | solution.py:267
  22.4 1.8 %shard_map.77 = (bf16[2,304,2048]{2,1,0:T(8,128)(2,1)S(1)}, f32[896,128]{1,0:T(8,128)S(1)}, f32[896,128]{1,0:T(8,128)S(1)}) custom-call(bf16[64,2048]{1,0:T(8,128)(2,1)S(1)} %collective-permute-done.1.prev_ref, bf16[64,2048]{1,0:T(8,128)(2,1)S(1)} %shard_map.76.here_ref, bf16[64,2048]{1,0:T(8,128)(2,1)S(1)} %collective-permute-done.2.next_ref, ...), custom_call_target="tpu_custom_call" | custom-call | tf_op jit(solution)/shard_map/pallas_call | solution.py:252
  24.4 1.8 %collective-permute-done.13.got_ref = f32[896,128]{1,0:T(8,128)S(1)} collective-permute-done((f32[896,128]{1,0:T(8,128)S(1)}, f32[896,128]{1,0:T(8,128)S(1)}, u32[]{:S(2)}, u32[]{:S(2)}) %collective-permute-start.13) | collective-permute-done | bytes 458784 | tf_op jit(solution)/shard_map/ppermute | solution.py:291
  26.2 0.9 %collective-permute-start.14 = (f32[448,128]{1,0:T(8,128)S(1)}, f32[448,128]{1,0:T(8,128)S(1)}, u32[]{:S(2)}, u32[]{:S(2)}) collective-permute-start(f32[448,128]{1,0:T(8,128)S(1)} %get-tuple-element.39), channel_id=1, source_target_pairs={{0,8},{1,9},{2,10},{3,11},{4,12},{5,13},{6,14},{7,15},{8,0},{9,1},... | collective-permute-start | bytes 688136 | tf_op jit(solution)/shard_map/ppermute | solution.py:297
  27.2 1.7 %collective-permute-start.11 = (bf16[128,2048]{1,0:T(8,128)(2,1)S(1)}, bf16[128,2048]{1,0:T(8,128)(2,1)S(1)}, u32[]{:S(2)}, u32[]{:S(2)}) collective-permute-start(bf16[128,2048]{1,0:T(8,128)(2,1)S(1)} %shard_map.81), channel_id=1, source_target_pairs={{1,0},{2,1},{3,2},{4,3},{5,4},{6,5},{7,6},{8,7},{9,8},{10,9},{11,1... | collective-permute-start | bytes 1572872 | tf_op jit(solution)/shard_map/ppermute | solution.py:299
  29.0 5.8 %collective-permute-done.14.got_ref = f32[448,128]{1,0:T(8,128)S(1)} collective-permute-done((f32[448,128]{1,0:T(8,128)S(1)}, f32[448,128]{1,0:T(8,128)S(1)}, u32[]{:S(2)}, u32[]{:S(2)}) %collective-permute-start.14) | collective-permute-done | bytes 229408 | tf_op jit(solution)/shard_map/ppermute | solution.py:297
  35.3 1.6 %collective-permute-start.16 = (f32[112,128]{1,0:T(8,128)S(1)}, f32[112,128]{1,0:T(8,128)S(1)}, u32[]{:S(2)}, u32[]{:S(2)}) collective-permute-start(f32[112,128]{1,0:T(8,128)S(1)} %get-tuple-element.42), channel_id=1, source_target_pairs={{0,6},{1,7},{2,0},{3,1},{4,2},{5,3},{6,4},{7,5},{8,14},{9,15},{10,... | collective-permute-start | bytes 172040 | tf_op jit(solution)/shard_map/ppermute | solution.py:302
  36.9 0.8 collective-permute-start.17
  37.7 3.3 %collective-permute-done.15.b = f32[112,128]{1,0:T(8,128)S(1)} collective-permute-done((f32[112,128]{1,0:T(8,128)S(1)}, f32[112,128]{1,0:T(8,128)S(1)}, u32[]{:S(2)}, u32[]{:S(2)}) %collective-permute-start.15) | collective-permute-done | bytes 57376 | tf_op jit(solution)/shard_map/ppermute | solution.py:302
  41.0 1.7 %collective-permute-done.16.c = f32[112,128]{1,0:T(8,128)S(1)} collective-permute-done((f32[112,128]{1,0:T(8,128)S(1)}, f32[112,128]{1,0:T(8,128)S(1)}, u32[]{:S(2)}, u32[]{:S(2)}) %collective-permute-start.16) | collective-permute-done | bytes 57376 | tf_op jit(solution)/shard_map/ppermute | solution.py:302
  42.7 1.6 %collective-permute-start.18 = (f32[112,128]{1,0:T(8,128)S(1)}, f32[112,128]{1,0:T(8,128)S(1)}, u32[]{:S(2)}, u32[]{:S(2)}) collective-permute-start(f32[112,128]{1,0:T(8,128)S(1)} %shard_map.86.piece_ref), channel_id=1, source_target_pairs={{0,8},{1,17},{2,10},{3,19},{4,12},{5,21},{6,14},{7,23},{8,0},{9,25... | collective-permute-start | bytes 172040 | tf_op jit(solution)/shard_map/ppermute | solution.py:309
  44.8 2.2 %collective-permute-done.18.first_ref = f32[112,128]{1,0:T(8,128)S(1)} collective-permute-done((f32[112,128]{1,0:T(8,128)S(1)}, f32[112,128]{1,0:T(8,128)S(1)}, u32[]{:S(2)}, u32[]{:S(2)}) %collective-permute-start.18) | collective-permute-done | bytes 57376 | tf_op jit(solution)/shard_map/ppermute | solution.py:309
  47.0 1.5 %collective-permute-done.19.second_ref = f32[112,128]{1,0:T(8,128)S(1)} collective-permute-done((f32[112,128]{1,0:T(8,128)S(1)}, f32[112,128]{1,0:T(8,128)S(1)}, u32[]{:S(2)}, u32[]{:S(2)}) %collective-permute-start.19) | collective-permute-done | bytes 57376 | tf_op jit(solution)/shard_map/ppermute | solution.py:310
  48.6 3.0 %collective-permute-start.21 = (f32[224,128]{1,0:T(8,128)S(1)}, f32[224,128]{1,0:T(8,128)S(1)}, u32[]{:S(2)}, u32[]{:S(2)}) collective-permute-start(f32[224,128]{1,0:T(8,128)S(1)} %shard_map.87.refs_0_), channel_id=1, source_target_pairs={{0,4},{1,5},{2,6},{3,7},{4,0},{5,1},{6,2},{7,3},{8,12},{9,13},{10,... | collective-permute-start | bytes 344072 | tf_op jit(solution)/shard_map/ppermute | solution.py:325
  51.9 4.0 %collective-permute-done.20.refs_1_ = f32[224,128]{1,0:T(8,128)S(1)} collective-permute-done((f32[224,128]{1,0:T(8,128)S(1)}, f32[224,128]{1,0:T(8,128)S(1)}, u32[]{:S(2)}, u32[]{:S(2)}) %collective-permute-start.20) | collective-permute-done | bytes 114720 | tf_op jit(solution)/shard_map/ppermute | solution.py:325
  55.9 3.9 %collective-permute-start.6 = (bf16[864,128]{1,0:T(8,128)(2,1)S(1)}, bf16[864,128]{1,0:T(8,128)(2,1)S(1)}, u32[]{:S(2)}, u32[]{:S(2)}) collective-permute-start(bf16[864,128]{1,0:T(8,128)(2,1)S(1)} %get-tuple-element.29), channel_id=1, source_target_pairs={{0,16},{16,0},{32,48},{48,32},{64,80},{80,64},{96,112},{112,96},{1... | collective-permute-start | bytes 663560 | tf_op jit(solution)/shard_map/ppermute | solution.py:275
  60.0 5.3 %collective-permute-done.6.wb_ref = bf16[864,128]{1,0:T(8,128)(2,1)S(1)} collective-permute-done((bf16[864,128]{1,0:T(8,128)(2,1)S(1)}, bf16[864,128]{1,0:T(8,128)(2,1)S(1)}, u32[]{:S(2)}, u32[]{:S(2)}) %collective-permute-start.6) | collective-permute-done | bytes 221216 | tf_op jit(solution)/shard_map/ppermute | solution.py:275
  65.3 1.4 %shard_map.78 = (f32[32,2048]{1,0:T(8,128)S(1)}, f32[32,2048]{1,0:T(8,128)S(1)}, f32[32,2048]{1,0:T(8,128)S(1)}, f32[32,2048]{1,0:T(8,128)S(1)}) custom-call(bf16[2,304,2048]{2,1,0:T(8,128)(2,1)S(1)} %get-tuple-element.27.xs_ref, bf16[864,128]{1,0:T(8,128)(2,1)S(1)} %get-tuple-element.28.wa_ref, bf16[864,128]{1,0:T(8,128)(2,1)S(1)} %collective-permute-done.6.wb_ref), custom_call_target="tpu_custom_call" | custom-call | tf_op jit(solution)/shard_map/pallas_call | solution.py:252
  66.8 3.2 %collective-permute-start.8 = (f32[32,2048]{1,0:T(8,128)S(1)}, f32[32,2048]{1,0:T(8,128)S(1)}, u32[]{:S(2)}, u32[]{:S(2)}) collective-permute-start(f32[32,2048]{1,0:T(8,128)S(1)} %get-tuple-element.32), channel_id=1, source_target_pairs={{0,96},{16,112},{32,0},{48,16},{64,32},{80,48},{96,64},{112,80},{1... | collective-permute-start | bytes 786440 | tf_op jit(solution)/shard_map/ppermute | solution.py:306
  70.0 1.4 %collective-permute-start.9 = (f32[32,2048]{1,0:T(8,128)S(1)}, f32[32,2048]{1,0:T(8,128)S(1)}, u32[]{:S(2)}, u32[]{:S(2)}) collective-permute-start(f32[32,2048]{1,0:T(8,128)S(1)} %get-tuple-element.33), channel_id=1, source_target_pairs={{0,64},{16,80},{32,96},{48,112},{64,0},{80,16},{96,32},{112,48},{1... | collective-permute-start | bytes 786440 | tf_op jit(solution)/shard_map/ppermute | solution.py:306
  71.4 1.5 %shard_map.82 = (f32[32,2048]{1,0:T(8,128)S(1)}, f32[32,2048]{1,0:T(8,128)S(1)}) custom-call(bf16[128,2048]{1,0:T(8,128)(2,1)S(1)} %collective-permute-done.10.prev_ref, bf16[128,2048]{1,0:T(8,128)(2,1)S(1)} %collective-permute-done.11.next_ref, bf16[32,2048]{1,0:T(8,128)(2,1)S(1)} %get-tuple-element.26.c0.refs_0_, ...), custom_call_target="tpu_custom_call" | custom-call | tf_op jit(solution)/shard_map/pallas_call | solution.py:252
  72.9 1.4 %collective-permute-start.12 = (f32[32,2048]{1,0:T(8,128)S(1)}, f32[32,2048]{1,0:T(8,128)S(1)}, u32[]{:S(2)}, u32[]{:S(2)}) collective-permute-start(f32[32,2048]{1,0:T(8,128)S(1)} %get-tuple-element.35), channel_id=1, source_target_pairs={{0,16},{16,0},{32,48},{48,32},{64,80},{80,64},{96,112},{112,96},{1... | collective-permute-start | bytes 786440 | tf_op jit(solution)/shard_map/ppermute | solution.py:321
  74.3 8.1 %collective-permute-done.7.b = f32[32,2048]{1,0:T(8,128)S(1)} collective-permute-done((f32[32,2048]{1,0:T(8,128)S(1)}, f32[32,2048]{1,0:T(8,128)S(1)}, u32[]{:S(2)}, u32[]{:S(2)}) %collective-permute-start.7) | collective-permute-done | bytes 262176 | tf_op jit(solution)/shard_map/ppermute | solution.py:306
  84.0 1.5 %shard_map.89 = (f32[864,256]{1,0:T(8,128)}, f32[1,32]{1,0:T(1,128)}) custom-call(f32[896,128]{1,0:T(8,128)S(1)} %shard_map.88.refs_0_, f32[896,128]{1,0:T(8,128)S(1)} %collective-permute-done.23.refs_1_), custom_call_target="tpu_custom_call" | custom-call | tf_op jit(solution)/shard_map/pallas_call | solution.py:252
  (33 shorter events, 3.7 us)
Async XLA Ops:
  0.6 7.0 %collective-permute-start = (bf16[32,2048]{1,0:T(8,128)(2,1)}, bf16[32,2048]{1,0:T(8,128)(2,1)S(1)}, u32[]{:S(2)}, u32[]{:S(2)}) collective-permute-start(bf16[32,2048]{1,0:T(8,128)(2,1)} %bitcast.12), channel_id=1, source_target_pairs={{0,16},{16,0},{32,48},{48,32},{64,80},{80,64},{96,112},{112,96},{1... | collective-permute-start | bytes 393224 | tf_op jit(solution)/shard_map/ppermute | solution.py:266
  7.7 14.7 %collective-permute-start.1 = (bf16[64,2048]{1,0:T(8,128)(2,1)S(1)}, bf16[64,2048]{1,0:T(8,128)(2,1)S(1)}, u32[]{:S(2)}, u32[]{:S(2)}) collective-permute-start(bf16[64,2048]{1,0:T(8,128)(2,1)S(1)} %shard_map.76.here_ref), channel_id=1, source_target_pairs={{0,1},{1,2},{2,3},{3,4},{4,5},{5,6},{6,7},{7,8},{8,9},{9,10},{10,1... | collective-permute-start | bytes 786440 | tf_op jit(solution)/shard_map/ppermute | solution.py:279
  7.8 14.7 %collective-permute-start.2 = (bf16[64,2048]{1,0:T(8,128)(2,1)S(1)}, bf16[64,2048]{1,0:T(8,128)(2,1)S(1)}, u32[]{:S(2)}, u32[]{:S(2)}) collective-permute-start(bf16[64,2048]{1,0:T(8,128)(2,1)S(1)} %shard_map.76.here_ref), channel_id=1, source_target_pairs={{1,0},{2,1},{3,2},{4,3},{5,4},{6,5},{7,6},{8,7},{9,8},{10,9},{11,1... | collective-permute-start | bytes 786440 | tf_op jit(solution)/shard_map/ppermute | solution.py:280
  9.5 9.6 %collective-permute-start.3 = (bf16[32,2048]{1,0:T(8,128)(2,1)}, bf16[32,2048]{1,0:T(8,128)(2,1)S(1)}, u32[]{:S(2)}, u32[]{:S(2)}) collective-permute-start(bf16[32,2048]{1,0:T(8,128)(2,1)} %bitcast.15), channel_id=1, source_target_pairs={{0,96},{16,112},{32,0},{48,16},{64,32},{80,48},{96,64},{112,80},{1... | collective-permute-start | bytes 393224 | tf_op jit(solution)/shard_map/ppermute | solution.py:267
  13.5 7.8 %collective-permute-start.4 = (bf16[32,2048]{1,0:T(8,128)(2,1)}, bf16[32,2048]{1,0:T(8,128)(2,1)S(1)}, u32[]{:S(2)}, u32[]{:S(2)}) collective-permute-start(bf16[32,2048]{1,0:T(8,128)(2,1)} %bitcast.16), channel_id=1, source_target_pairs={{0,64},{16,80},{32,96},{48,112},{64,0},{80,16},{96,32},{112,48},{1... | collective-permute-start | bytes 393224 | tf_op jit(solution)/shard_map/ppermute | solution.py:267
  13.5 8.9 %collective-permute-start.5 = (bf16[32,2048]{1,0:T(8,128)(2,1)}, bf16[32,2048]{1,0:T(8,128)(2,1)S(1)}, u32[]{:S(2)}, u32[]{:S(2)}) collective-permute-start(bf16[32,2048]{1,0:T(8,128)(2,1)} %bitcast.17), channel_id=1, source_target_pairs={{0,32},{16,48},{32,64},{48,80},{64,96},{80,112},{96,0},{112,16},{1... | collective-permute-start | bytes 393224 | tf_op jit(solution)/shard_map/ppermute | solution.py:267
  24.3 1.9 %collective-permute-start.13 = (f32[896,128]{1,0:T(8,128)S(1)}, f32[896,128]{1,0:T(8,128)S(1)}, u32[]{:S(2)}, u32[]{:S(2)}) collective-permute-start(f32[896,128]{1,0:T(8,128)S(1)} %get-tuple-element.37), channel_id=1, source_target_pairs={{0,1},{1,0},{2,3},{3,2},{4,5},{5,4},{6,7},{7,6},{8,9},{9,8},{10,11... | collective-permute-start | bytes 1376264 | tf_op jit(solution)/shard_map/ppermute | solution.py:291
  26.2 8.6 %collective-permute-start.14 = (f32[448,128]{1,0:T(8,128)S(1)}, f32[448,128]{1,0:T(8,128)S(1)}, u32[]{:S(2)}, u32[]{:S(2)}) collective-permute-start(f32[448,128]{1,0:T(8,128)S(1)} %get-tuple-element.39), channel_id=1, source_target_pairs={{0,8},{1,9},{2,10},{3,11},{4,12},{5,13},{6,14},{7,15},{8,0},{9,1},... | collective-permute-start | bytes 688136 | tf_op jit(solution)/shard_map/ppermute | solution.py:297
  27.2 42.9 %collective-permute-start.10 = (bf16[128,2048]{1,0:T(8,128)(2,1)S(1)}, bf16[128,2048]{1,0:T(8,128)(2,1)S(1)}, u32[]{:S(2)}, u32[]{:S(2)}) collective-permute-start(bf16[128,2048]{1,0:T(8,128)(2,1)S(1)} %shard_map.81), channel_id=1, source_target_pairs={{0,1},{1,2},{2,3},{3,4},{4,5},{5,6},{6,7},{7,8},{8,9},{9,10},{10,1... | collective-permute-start | bytes 1572872 | tf_op jit(solution)/shard_map/ppermute | solution.py:298
  27.2 44.1 %collective-permute-start.11 = (bf16[128,2048]{1,0:T(8,128)(2,1)S(1)}, bf16[128,2048]{1,0:T(8,128)(2,1)S(1)}, u32[]{:S(2)}, u32[]{:S(2)}) collective-permute-start(bf16[128,2048]{1,0:T(8,128)(2,1)S(1)} %shard_map.81), channel_id=1, source_target_pairs={{1,0},{2,1},{3,2},{4,3},{5,4},{6,5},{7,6},{8,7},{9,8},{10,9},{11,1... | collective-permute-start | bytes 1572872 | tf_op jit(solution)/shard_map/ppermute | solution.py:299
  34.8 6.2 %collective-permute-start.15 = (f32[112,128]{1,0:T(8,128)S(1)}, f32[112,128]{1,0:T(8,128)S(1)}, u32[]{:S(2)}, u32[]{:S(2)}) collective-permute-start(f32[112,128]{1,0:T(8,128)S(1)} %get-tuple-element.41), channel_id=1, source_target_pairs={{0,2},{1,3},{2,4},{3,5},{4,6},{5,7},{6,0},{7,1},{8,10},{9,11},{10,... | collective-permute-start | bytes 172040 | tf_op jit(solution)/shard_map/ppermute | solution.py:302
  35.3 7.4 %collective-permute-start.16 = (f32[112,128]{1,0:T(8,128)S(1)}, f32[112,128]{1,0:T(8,128)S(1)}, u32[]{:S(2)}, u32[]{:S(2)}) collective-permute-start(f32[112,128]{1,0:T(8,128)S(1)} %get-tuple-element.42), channel_id=1, source_target_pairs={{0,6},{1,7},{2,0},{3,1},{4,2},{5,3},{6,4},{7,5},{8,14},{9,15},{10,... | collective-permute-start | bytes 172040 | tf_op jit(solution)/shard_map/ppermute | solution.py:302
  36.9 5.8 %collective-permute-start.17 = (f32[112,128]{1,0:T(8,128)S(1)}, f32[112,128]{1,0:T(8,128)S(1)}, u32[]{:S(2)}, u32[]{:S(2)}) collective-permute-start(f32[112,128]{1,0:T(8,128)S(1)} %get-tuple-element.43), channel_id=1, source_target_pairs={{0,4},{1,5},{2,6},{3,7},{4,0},{5,1},{6,2},{7,3},{8,12},{9,13},{10,... | collective-permute-start | bytes 172040 | tf_op jit(solution)/shard_map/ppermute | solution.py:302
  42.7 4.3 %collective-permute-start.18 = (f32[112,128]{1,0:T(8,128)S(1)}, f32[112,128]{1,0:T(8,128)S(1)}, u32[]{:S(2)}, u32[]{:S(2)}) collective-permute-start(f32[112,128]{1,0:T(8,128)S(1)} %shard_map.86.piece_ref), channel_id=1, source_target_pairs={{0,8},{1,17},{2,10},{3,19},{4,12},{5,21},{6,14},{7,23},{8,0},{9,25... | collective-permute-start | bytes 172040 | tf_op jit(solution)/shard_map/ppermute | solution.py:309
  44.3 4.2 %collective-permute-start.19 = (f32[112,128]{1,0:T(8,128)S(1)}, f32[112,128]{1,0:T(8,128)S(1)}, u32[]{:S(2)}, u32[]{:S(2)}) collective-permute-start(f32[112,128]{1,0:T(8,128)S(1)} %shard_map.86.piece_ref), channel_id=1, source_target_pairs={{0,8},{1,25},{2,10},{3,27},{4,12},{5,29},{6,14},{7,31},{8,0},{9,17... | collective-permute-start | bytes 172040 | tf_op jit(solution)/shard_map/ppermute | solution.py:310
  48.5 7.4 %collective-permute-start.20 = (f32[224,128]{1,0:T(8,128)S(1)}, f32[224,128]{1,0:T(8,128)S(1)}, u32[]{:S(2)}, u32[]{:S(2)}) collective-permute-start(f32[224,128]{1,0:T(8,128)S(1)} %shard_map.87.refs_0_), channel_id=1, source_target_pairs={{0,6},{1,7},{2,0},{3,1},{4,2},{5,3},{6,4},{7,5},{8,14},{9,15},{10,... | collective-permute-start | bytes 344072 | tf_op jit(solution)/shard_map/ppermute | solution.py:325
  48.6 11.2 %collective-permute-start.21 = (f32[224,128]{1,0:T(8,128)S(1)}, f32[224,128]{1,0:T(8,128)S(1)}, u32[]{:S(2)}, u32[]{:S(2)}) collective-permute-start(f32[224,128]{1,0:T(8,128)S(1)} %shard_map.87.refs_0_), channel_id=1, source_target_pairs={{0,4},{1,5},{2,6},{3,7},{4,0},{5,1},{6,2},{7,3},{8,12},{9,13},{10,... | collective-permute-start | bytes 344072 | tf_op jit(solution)/shard_map/ppermute | solution.py:325
  51.5 8.3 %collective-permute-start.22 = (f32[224,128]{1,0:T(8,128)S(1)}, f32[224,128]{1,0:T(8,128)S(1)}, u32[]{:S(2)}, u32[]{:S(2)}) collective-permute-start(f32[224,128]{1,0:T(8,128)S(1)} %shard_map.87.refs_0_), channel_id=1, source_target_pairs={{0,2},{1,3},{2,4},{3,5},{4,6},{5,7},{6,0},{7,1},{8,10},{9,11},{10,... | collective-permute-start | bytes 344072 | tf_op jit(solution)/shard_map/ppermute | solution.py:325
  55.9 9.4 %collective-permute-start.6 = (bf16[864,128]{1,0:T(8,128)(2,1)S(1)}, bf16[864,128]{1,0:T(8,128)(2,1)S(1)}, u32[]{:S(2)}, u32[]{:S(2)}) collective-permute-start(bf16[864,128]{1,0:T(8,128)(2,1)S(1)} %get-tuple-element.29), channel_id=1, source_target_pairs={{0,16},{16,0},{32,48},{48,32},{64,80},{80,64},{96,112},{112,96},{1... | collective-permute-start | bytes 663560 | tf_op jit(solution)/shard_map/ppermute | solution.py:275
  59.9 14.4 %copy-start = (bf16[32]{0:T(256)(128)(2,1)S(1)}, bf16[32]{0:T(256)(128)(2,1)}, u32[]{:S(2)}) copy-start(bf16[32]{0:T(256)(128)(2,1)} %param.6) | copy-start | bytes 196
  59.9 24.1 %collective-permute-start.23 = (f32[896,128]{1,0:T(8,128)S(1)}, f32[896,128]{1,0:T(8,128)S(1)}, u32[]{:S(2)}, u32[]{:S(2)}) collective-permute-start(f32[896,128]{1,0:T(8,128)S(1)} %shard_map.88.refs_0_), channel_id=1, source_target_pairs={{0,1},{1,0},{2,3},{3,2},{4,5},{5,4},{6,7},{7,6},{8,9},{9,8},{10,11... | collective-permute-start | bytes 1376264 | tf_op jit(solution)/shard_map/ppermute | solution.py:327
  66.7 15.8 %collective-permute-start.7 = (f32[32,2048]{1,0:T(8,128)S(1)}, f32[32,2048]{1,0:T(8,128)S(1)}, u32[]{:S(2)}, u32[]{:S(2)}) collective-permute-start(f32[32,2048]{1,0:T(8,128)S(1)} %get-tuple-element.31), channel_id=1, source_target_pairs={{0,32},{16,48},{32,64},{48,80},{64,96},{80,112},{96,0},{112,16},{1... | collective-permute-start | bytes 786440 | tf_op jit(solution)/shard_map/ppermute | solution.py:306
  66.8 15.7 %collective-permute-start.8 = (f32[32,2048]{1,0:T(8,128)S(1)}, f32[32,2048]{1,0:T(8,128)S(1)}, u32[]{:S(2)}, u32[]{:S(2)}) collective-permute-start(f32[32,2048]{1,0:T(8,128)S(1)} %get-tuple-element.32), channel_id=1, source_target_pairs={{0,96},{16,112},{32,0},{48,16},{64,32},{80,48},{96,64},{112,80},{1... | collective-permute-start | bytes 786440 | tf_op jit(solution)/shard_map/ppermute | solution.py:306
  70.0 12.5 %collective-permute-start.9 = (f32[32,2048]{1,0:T(8,128)S(1)}, f32[32,2048]{1,0:T(8,128)S(1)}, u32[]{:S(2)}, u32[]{:S(2)}) collective-permute-start(f32[32,2048]{1,0:T(8,128)S(1)} %get-tuple-element.33), channel_id=1, source_target_pairs={{0,64},{16,80},{32,96},{48,112},{64,0},{80,16},{96,32},{112,48},{1... | collective-permute-start | bytes 786440 | tf_op jit(solution)/shard_map/ppermute | solution.py:306
  72.9 10.4 %collective-permute-start.12 = (f32[32,2048]{1,0:T(8,128)S(1)}, f32[32,2048]{1,0:T(8,128)S(1)}, u32[]{:S(2)}, u32[]{:S(2)}) collective-permute-start(f32[32,2048]{1,0:T(8,128)S(1)} %get-tuple-element.35), channel_id=1, source_target_pairs={{0,16},{16,0},{32,48},{48,32},{64,80},{80,64},{96,112},{112,96},{1... | collective-permute-start | bytes 786440 | tf_op jit(solution)/shard_map/ppermute | solution.py:321

commit v4 on v3

--- a/solution.py
+++ b/solution.py
@@ -1,3 +1,5 @@
+import functools
+
 import jax
 import jax.numpy as jnp
 from jax import lax
@@ -11,8 +13,11 @@
 PLANE = ROWS * WIDE
 OWN = 32
 TAPS = 9 * OWN
-HALF = 896
-PIECE = HALF // 8
+HALF = 3 * TAPS
+PIECE = HALF // 2
+CODED = PIECE + 16
+POWER = 12.0
+TOP = 120.0
 BF = jnp.bfloat16
 F32 = jnp.float32
 
@@ -141,8 +146,7 @@
         )
         for kh in range(3):
             ref[kh * TAPS : (kh + 1) * TAPS, :] = got[:TAPS, kh * 128 : kh * 128 + 128]
-        ref[3 * TAPS : 3 * TAPS + 16, :] = got[TAPS:, 128:256]
-        ref[3 * TAPS + 16 :, :] = got[TAPS:, 128:256]
+        ref[HALF:, :] = got[TAPS : TAPS + 8, 128:256]
 
 
 def input_grad_kernel(prev_ref, next_ref, c0, c1, c2, c3, wa_ref, wb_ref, mine_ref, theirs_ref, cs_ref):
@@ -178,22 +182,87 @@
         )
 
 
-def assemble_kernel(own_ref, other_ref, grad_ref, bias_ref, both_ref, *, factor):
+def encode(wide):
+    size = jnp.abs(wide)
+    scale = jnp.max(jnp.max(size, axis=1, keepdims=True), axis=0, keepdims=True)
+    scale = jnp.maximum(scale, 1e-30).astype(BF).astype(F32)
+    coded = jnp.exp2(jnp.log2(size * (1.0 / scale)) * POWER + TOP)
+    return jnp.where(wide < 0, -coded, coded).astype(BF), scale
+
+
+def decode(coded, scale):
+    wide = coded.astype(F32)
+    size = scale * jnp.exp2((jnp.log2(jnp.abs(wide)) - TOP) * (1.0 / POWER))
+    return jnp.where(wide < 0, -size, size)
+
+
+def write_coded(out_ref, wide, bias):
+    coded, scale = encode(wide)
+    high = bias.astype(BF).astype(F32)
+    low = bias - high
+    row = lax.broadcasted_iota(jnp.int32, (16, 128), 0)
+    tail = jnp.where(row == 0, scale, jnp.where(row == 1, high, jnp.where(row == 2, low, 0.0)))
+    out_ref[:PIECE, :] = coded
+    out_ref[PIECE:, :] = tail.astype(BF)
+
+
+def read_coded(ref, at=0):
+    tail = ref[at + PIECE : at + CODED, :].astype(F32)
+    return decode(ref[at : at + PIECE, :], tail[0:1, 0:1]), tail[1:2, :] + tail[2:3, :]
+
+
+def split_xlo_kernel(keep_ref, got_ref, send_out, keep_out):
+    xlo = lax.axis_index("space") // 8
+    bias = keep_ref[HALF:, :] + got_ref[HALF:, :]
+    for out, at in ((send_out, (1 - xlo) * PIECE), (keep_out, xlo * PIECE)):
+        rows = pl.ds(pl.multiple_of(at, 8), PIECE)
+        out[:PIECE, :] = keep_ref[rows, :] + got_ref[rows, :]
+        out[PIECE:, :] = bias
+
+
+def code_kernel(keep_ref, got_ref, out_ref):
+    write_coded(
+        out_ref,
+        keep_ref[:PIECE, :] + got_ref[:PIECE, :],
+        keep_ref[PIECE : PIECE + 1, :] + got_ref[PIECE : PIECE + 1, :],
+    )
+
+
+def piece_kernel(own_ref, y1_ref, y2_ref, y3_ref, out_ref, bias_ref, *, factor):
+    own, y1, y2, y3 = (read_coded(r) for r in (own_ref, y1_ref, y2_ref, y3_ref))
+    wide, bias = ((own[i] + y2[i]) + (y1[i] + y3[i]) for i in range(2))
+    write_coded(out_ref, wide * factor, bias)
+    bias_ref[...] = bias[:, :OWN] * factor
+
+
+def pair_kernel(piece_ref, first_ref, second_ref, out_ref):
+    even = (lax.axis_index("space") & 1) == 0
+    out_ref[:CODED, :] = jnp.where(even, piece_ref[...], first_ref[...])
+    out_ref[CODED:, :] = jnp.where(even, first_ref[...], second_ref[...])
+
+
+def place(pair_ref, out_ref, lane):
+    xlo = lax.axis_index("space") // 8
+    for rx in range(2):
+        to = pl.multiple_of((xlo ^ rx) * PIECE, 8)
+        out_ref[pl.ds(to, PIECE), lane : lane + 128] = read_coded(pair_ref, rx * CODED)[0]
+
+
+def decode_kernel(pair_ref, out_ref):
+    place(pair_ref, out_ref, 0)
+
+
+def assemble_kernel(own_ref, other_ref, grad_ref, both_ref):
     filt, space = lax.axis_index("filt"), lax.axis_index("space")
-    z, xh = filt // 2, filt % 2
-    xlo, y, core = space // 8, (space // 2) & 3, space & 1
-    for side, ref in enumerate((own_ref, other_ref)):
-        for ry in range(4):
-            for rx in range(2):
-                at = (ry * 2 + rx) * PIECE
-                to = pl.multiple_of(((xlo ^ rx) * 4 + ((y + ry) & 3)) * PIECE, 8)
-                both_ref[pl.ds(to, PIECE), side * 128 : side * 128 + 128] = ref[at : at + PIECE, :]
+    z, xh, core = filt // 2, filt % 2, space & 1
+    both_ref[:, :128] = own_ref[...]
+    place(other_ref, both_ref, 128)
     src = lax.broadcasted_iota(jnp.int32, (256, 256), 0)
     lane = lax.broadcasted_iota(jnp.int32, (256, 256), 1)
     side, turn, chan = src >> 7, (src >> 5) & 3, src & 31
     want = ((z + turn) & 3) * 64 + ((xh + core + side) & 1) * 32 + chan
     pick = jnp.where(lane == want, 1.0, 0.0).astype(BF)
-    left = both_ref[: 3 * TAPS, :] * factor
+    left = both_ref[...]
     got = jnp.zeros(left.shape, F32)
     for _ in range(3):
         part = left.astype(BF)
@@ -204,23 +273,6 @@
             grad_ref[(kd * 3 + kh) * 96 : (kd * 3 + kh) * 96 + 96, :] = got[
                 kh * TAPS + kd * 96 : kh * TAPS + kd * 96 + 96
             ]
-    tail = both_ref[3 * TAPS : 3 * TAPS + 1, :]
-    bias_ref[...] = jnp.where(core == 0, tail[:, :OWN], tail[:, 128 : 128 + OWN]) * factor
-
-
-def split_xlo_kernel(keep_ref, got_ref, send_out, keep_out):
-    half = HALF // 2
-    xlo = lax.axis_index("space") // 8
-    for out, at in ((send_out, (1 - xlo) * half), (keep_out, xlo * half)):
-        rows = pl.ds(pl.multiple_of(at, 8), half)
-        out[...] = keep_ref[rows, :] + got_ref[rows, :]
-
-
-def split_y_kernel(keep_ref, got_ref, *outs):
-    y = (lax.axis_index("space") // 2) & 3
-    for r, out in enumerate(outs):
-        rows = pl.ds(pl.multiple_of(((y + r) & 3) * PIECE, 8), PIECE)
-        out[...] = keep_ref[rows, :] + got_ref[rows, :]
 
 
 def bias_kernel(ref, out):
@@ -236,16 +288,6 @@
 
 def add2_kernel(a, b, out):
     out[...] = a[...] + b[...]
-
-
-def add4_kernel(a, b, c, d, out):
-    out[...] = (a[...] + b[...]) + (c[...] + d[...])
-
-
-def pair_kernel(piece_ref, first_ref, second_ref, out_ref):
-    even = (lax.axis_index("space") & 1) == 0
-    out_ref[:PIECE, :] = jnp.where(even, piece_ref[...], first_ref[...])
-    out_ref[PIECE:, :] = jnp.where(even, first_ref[...], second_ref[...])
 
 
 def call(kernel, outs, *args, scratch=(), space=VM):
@@ -281,7 +323,7 @@
 
     xs, keep, send = call(
         kernel_grad_kernel,
-        [((2, TAPS + 16, PLANE), BF)] + [((HALF, 128), F32)] * 2,
+        [((2, TAPS + 16, PLANE), BF)] + [((HALF + 8, 128), F32)] * 2,
         x_prev,
         x_here,
         x_next,
@@ -292,15 +334,22 @@
     outs = call(forward_kernel, [((32, PLANE), F32)] * 4, xs, w_mine, w_other)
     (c_here,) = call(join_kernel, [((128, PLANE), BF)], *cots)
 
-    half = HALF // 2
-    r_send, r_keep = call(split_xlo_kernel, [((half, 128), F32)] * 2, keep, r_core)
+    r_send, r_keep = call(split_xlo_kernel, [((PIECE + 8, 128), F32)] * 2, keep, r_core)
     r_xlo = lax.ppermute(r_send, "space", XLO)
     c_prev = lax.ppermute(c_here, "space", UP)
     c_next = lax.ppermute(c_here, "space", DOWN)
 
-    parts = call(split_y_kernel, [((PIECE, 128), F32)] * 4, r_keep, r_xlo)
-    got = [lax.ppermute(parts[r], "space", along_y(r)) for r in (1, 3, 2)]
-    (piece,) = call(add4_kernel, [((PIECE, 128), F32)], parts[0], *got)
+    (mine_y,) = call(code_kernel, [((CODED, 128), BF)], r_keep, r_xlo)
+    y1, y3, y2 = (lax.ppermute(mine_y, "space", along_y(-r)) for r in (1, 3, 2))
+    factor = float((16 * PLANE) ** -0.5)
+    piece, grad_bias = call(
+        functools.partial(piece_kernel, factor=factor),
+        [((CODED, 128), BF), ((1, OWN), F32)],
+        mine_y,
+        y1,
+        y2,
+        y3,
+    )
 
     (wide_bias,) = call(bias_kernel, [((OWN, 1), F32)], bias.reshape(1, OWN))
     sums = [lax.ppermute(outs[r], "filt", along_z(r)) for r in (1, 3, 2)]
@@ -321,17 +370,11 @@
     g_other = lax.ppermute(g_theirs, "filt", ACROSS)
     (grad_inputs,) = call(add2_kernel, [((OWN, PLANE), F32)], g_mine, g_other)
 
-    (pair,) = call(pair_kernel, [((2 * PIECE, 128), F32)], piece, first, second)
-    turned = {r: lax.ppermute(pair, "space", along_y(-r)) for r in (1, 3, 2)}
-    (mine,) = call(join_kernel, [((HALF, 128), F32)], pair, turned[1], turned[2], turned[3])
-    other = lax.ppermute(mine, "space", CORE)
-    factor = float((16 * PLANE) ** -0.5)
-    grad_weight, grad_bias = call(
-        lambda *refs: assemble_kernel(*refs, factor=factor),
-        [((864, 256), F32), ((1, OWN), F32)],
-        mine,
-        other,
-        scratch=[pltpu.VMEM((HALF, 256), F32)],
+    (pair,) = call(pair_kernel, [((2 * CODED, 128), BF)], piece, first, second)
+    other = lax.ppermute(pair, "space", CORE)
+    (mine,) = call(decode_kernel, [((HALF, 128), F32)], pair)
+    (grad_weight,) = call(
+        assemble_kernel, [((HALF, 256), F32)], mine, other, scratch=[pltpu.VMEM((HALF, 256), F32)]
     )
     return (
         output[None],

time: 85.7 us -> 73.3 us (0.86)
  the two profiles are of different devices: /device:TPU:24 before, /device:TPU:26 now
where the time goes in v4:
time: 73.3 us; the launch traced here: 73.1 us
  waiting for transfers between devices  35 us (48%)
  starting transfers between devices  26.4 us (36%)
  Pallas kernels  11 us (15%)
  between operations  0.78 us (1%)
    pallas_call x15, Pallas kernels, call(): pl.pallas_call(kernel, out_shape=[jax.ShapeDtypeStruct(s, d) for s, d in...  11 us
    ppermute x3, waiting for transfers between devices, step(): c1, c3, c2 = (lax.ppermute(c_own, 'filt', along_z(-r)) for r in (1, 3, 2))  6.94 us
    ppermute x3, waiting for transfers between devices, step(): y1, y3, y2 = (lax.ppermute(mine_y, 'space', along_y(-r)) for r in (1, 3, 2))  6.64 us
    ppermute x3, waiting for transfers between devices, step(): sums = [lax.ppermute(outs[r], 'filt', along_z(r)) for r in (1, 3, 2)]  6.03 us
    ppermute x1, waiting for transfers between devices, step(): r_xlo = lax.ppermute(r_send, 'space', XLO)  5.32 us
    ppermute x3, starting transfers between devices, step(): c1, c3, c2 = (lax.ppermute(c_own, 'filt', along_z(-r)) for r in (1, 3, 2))  5.3 us
    ppermute x1, waiting for transfers between devices, step(): w_other = lax.ppermute(w_theirs, 'filt', ACROSS)  4.82 us
    ppermute x3, starting transfers between devices, step(): y1, y3, y2 = (lax.ppermute(mine_y, 'space', along_y(-r)) for r in (1, 3, 2))  4.21 us
  transfers between devices with their start and end apart: 21, of which 9 were waited for; matrix products, arithmetic and copies ran while one was open for 0% of the time, Pallas kernels for 10%

profile of v4, /device:TPU:26, one launch (start us, length us, event | category | flops | bytes accessed | tf_op | source)
XLA Modules:
  0.0 73.1 jit_solution(14019216703563980504)
XLA Ops:
  0.6 2.2 %collective-permute-start = (bf16[32,2048]{1,0:T(8,128)(2,1)}, bf16[32,2048]{1,0:T(8,128)(2,1)S(1)}, u32[]{:S(2)}, u32[]{:S(2)}) collective-permute-start(bf16[32,2048]{1,0:T(8,128)(2,1)} %bitcast.13), channel_id=1, source_target_pairs={{0,16},{16,0},{32,48},{48,32},{64,80},{80,64},{96,112},{112,96},{1... | collective-permute-start | bytes 393224 | tf_op jit(solution)/shard_map/ppermute | solution.py:308
  2.8 1.4 %shard_map.75 = (bf16[864,128]{1,0:T(8,128)(2,1)S(1)}, bf16[864,128]{1,0:T(8,128)(2,1)S(1)}, bf16[32,2048]{1,0:T(8,128)(2,1)S(1)}, bf16[32,2048]{1,0:T(8,128)(2,1)S(1)}) custom-call(bf16[864,256]{1,0:T(8,128)(2,1)} %bitcast.10, bf16[32,2048]{1,0:T(8,128)(2,1)} %bitcast.14, bf16[32,2048]{1,0:T(8,128)(2,1)} %bitcast.15), custom_call_target="tpu_custom_call" | custom-call | tf_op jit(solution)/shard_map/pallas_call | solution.py:294
  4.2 3.4 %collective-permute-done.refs_1_ = bf16[32,2048]{1,0:T(8,128)(2,1)S(1)} collective-permute-done((bf16[32,2048]{1,0:T(8,128)(2,1)}, bf16[32,2048]{1,0:T(8,128)(2,1)S(1)}, u32[]{:S(2)}, u32[]{:S(2)}) %collective-permute-start) | collective-permute-done | bytes 131104 | tf_op jit(solution)/shard_map/ppermute | solution.py:308
  7.8 1.7 %collective-permute-start.2 = (bf16[64,2048]{1,0:T(8,128)(2,1)S(1)}, bf16[64,2048]{1,0:T(8,128)(2,1)S(1)}, u32[]{:S(2)}, u32[]{:S(2)}) collective-permute-start(bf16[64,2048]{1,0:T(8,128)(2,1)S(1)} %shard_map.76.here_ref), channel_id=1, source_target_pairs={{1,0},{2,1},{3,2},{4,3},{5,4},{6,5},{7,6},{8,7},{9,8},{10,9},{11,1... | collective-permute-start | bytes 786440 | tf_op jit(solution)/shard_map/ppermute | solution.py:322
  9.5 4.0 %collective-permute-start.3 = (bf16[32,2048]{1,0:T(8,128)(2,1)}, bf16[32,2048]{1,0:T(8,128)(2,1)S(1)}, u32[]{:S(2)}, u32[]{:S(2)}) collective-permute-start(bf16[32,2048]{1,0:T(8,128)(2,1)} %bitcast.16), channel_id=1, source_target_pairs={{0,96},{16,112},{32,0},{48,16},{64,32},{80,48},{96,64},{112,80},{1... | collective-permute-start | bytes 393224 | tf_op jit(solution)/shard_map/ppermute | solution.py:309
  13.5 1.3 %collective-permute-start.5 = (bf16[32,2048]{1,0:T(8,128)(2,1)}, bf16[32,2048]{1,0:T(8,128)(2,1)S(1)}, u32[]{:S(2)}, u32[]{:S(2)}) collective-permute-start(bf16[32,2048]{1,0:T(8,128)(2,1)} %bitcast.18), channel_id=1, source_target_pairs={{0,32},{16,48},{32,64},{48,80},{64,96},{80,112},{96,0},{112,16},{1... | collective-permute-start | bytes 393224 | tf_op jit(solution)/shard_map/ppermute | solution.py:309
  14.8 3.6 %collective-permute-done.3.c1.refs_1_ = bf16[32,2048]{1,0:T(8,128)(2,1)S(1)} collective-permute-done((bf16[32,2048]{1,0:T(8,128)(2,1)}, bf16[32,2048]{1,0:T(8,128)(2,1)S(1)}, u32[]{:S(2)}, u32[]{:S(2)}) %collective-permute-start.3) | collective-permute-done | bytes 131104 | tf_op jit(solution)/shard_map/ppermute | solution.py:309
  18.4 2.2 %collective-permute-done.4.c2.refs_2_ = bf16[32,2048]{1,0:T(8,128)(2,1)S(1)} collective-permute-done((bf16[32,2048]{1,0:T(8,128)(2,1)}, bf16[32,2048]{1,0:T(8,128)(2,1)S(1)}, u32[]{:S(2)}, u32[]{:S(2)}) %collective-permute-start.4) | collective-permute-done | bytes 131104 | tf_op jit(solution)/shard_map/ppermute | solution.py:309
  20.7 1.1 %collective-permute-done.5.c3.refs_3_ = bf16[32,2048]{1,0:T(8,128)(2,1)S(1)} collective-permute-done((bf16[32,2048]{1,0:T(8,128)(2,1)}, bf16[32,2048]{1,0:T(8,128)(2,1)S(1)}, u32[]{:S(2)}, u32[]{:S(2)}) %collective-permute-start.5) | collective-permute-done | bytes 131104 | tf_op jit(solution)/shard_map/ppermute | solution.py:309
  21.7 1.9 %shard_map.77 = (bf16[2,304,2048]{2,1,0:T(8,128)(2,1)S(1)}, f32[872,128]{1,0:T(8,128)S(1)}, f32[872,128]{1,0:T(8,128)S(1)}) custom-call(bf16[64,2048]{1,0:T(8,128)(2,1)S(1)} %collective-permute-done.1.prev_ref, bf16[64,2048]{1,0:T(8,128)(2,1)S(1)} %shard_map.76.here_ref, bf16[64,2048]{1,0:T(8,128)(2,1)S(1)} %collective-permute-done.2.next_ref, ...), custom_call_target="tpu_custom_call" | custom-call | tf_op jit(solution)/shard_map/pallas_call | solution.py:294
  23.7 1.8 %collective-permute-done.13.got_ref = f32[872,128]{1,0:T(8,128)S(1)} collective-permute-done((f32[872,128]{1,0:T(8,128)S(1)}, f32[872,128]{1,0:T(8,128)S(1)}, u32[]{:S(2)}, u32[]{:S(2)}) %collective-permute-start.13) | collective-permute-done | bytes 446496 | tf_op jit(solution)/shard_map/ppermute | solution.py:333
  25.6 1.3 %collective-permute-start.14 = (f32[440,128]{1,0:T(8,128)S(1)}, f32[440,128]{1,0:T(8,128)S(1)}, u32[]{:S(2)}, u32[]{:S(2)}) collective-permute-start(f32[440,128]{1,0:T(8,128)S(1)} %get-tuple-element.35), channel_id=1, source_target_pairs={{0,8},{1,9},{2,10},{3,11},{4,12},{5,13},{6,14},{7,15},{8,0},{9,1},... | collective-permute-start | bytes 675848 | tf_op jit(solution)/shard_map/ppermute | solution.py:338
  27.0 1.7 %collective-permute-start.11 = (bf16[128,2048]{1,0:T(8,128)(2,1)S(1)}, bf16[128,2048]{1,0:T(8,128)(2,1)S(1)}, u32[]{:S(2)}, u32[]{:S(2)}) collective-permute-start(bf16[128,2048]{1,0:T(8,128)(2,1)S(1)} %shard_map.81), channel_id=1, source_target_pairs={{1,0},{2,1},{3,2},{4,3},{5,4},{6,5},{7,6},{8,7},{9,8},{10,9},{11,1... | collective-permute-start | bytes 1572872 | tf_op jit(solution)/shard_map/ppermute | solution.py:340
  28.7 5.3 %collective-permute-done.14.got_ref = f32[440,128]{1,0:T(8,128)S(1)} collective-permute-done((f32[440,128]{1,0:T(8,128)S(1)}, f32[440,128]{1,0:T(8,128)S(1)}, u32[]{:S(2)}, u32[]{:S(2)}) %collective-permute-start.14) | collective-permute-done | bytes 225312 | tf_op jit(solution)/shard_map/ppermute | solution.py:338
  34.0 0.2 shard_map.85.own_ref
  34.3 0.8 %collective-permute-start.15 = (bf16[448,128]{1,0:T(8,128)(2,1)S(1)}, bf16[448,128]{1,0:T(8,128)(2,1)S(1)}, u32[]{:S(2)}, u32[]{:S(2)}) collective-permute-start(bf16[448,128]{1,0:T(8,128)(2,1)S(1)} %shard_map.85.own_ref), channel_id=1, source_target_pairs={{0,6},{1,7},{2,0},{3,1},{4,2},{5,3},{6,4},{7,5},{8,14},{9,15},{10,... | collective-permute-start | bytes 344072 | tf_op jit(solution)/shard_map/ppermute | solution.py:343
  35.1 1.8 %collective-permute-start.16 = (bf16[448,128]{1,0:T(8,128)(2,1)S(1)}, bf16[448,128]{1,0:T(8,128)(2,1)S(1)}, u32[]{:S(2)}, u32[]{:S(2)}) collective-permute-start(bf16[448,128]{1,0:T(8,128)(2,1)S(1)} %shard_map.85.own_ref), channel_id=1, source_target_pairs={{0,4},{1,5},{2,6},{3,7},{4,0},{5,1},{6,2},{7,3},{8,12},{9,13},{10,... | collective-permute-start | bytes 344072 | tf_op jit(solution)/shard_map/ppermute | solution.py:343
  36.9 1.6 %collective-permute-start.17 = (bf16[448,128]{1,0:T(8,128)(2,1)S(1)}, bf16[448,128]{1,0:T(8,128)(2,1)S(1)}, u32[]{:S(2)}, u32[]{:S(2)}) collective-permute-start(bf16[448,128]{1,0:T(8,128)(2,1)S(1)} %shard_map.85.own_ref), channel_id=1, source_target_pairs={{0,2},{1,3},{2,4},{3,5},{4,6},{5,7},{6,0},{7,1},{8,10},{9,11},{10,... | collective-permute-start | bytes 344072 | tf_op jit(solution)/shard_map/ppermute | solution.py:343
  38.5 6.6 %collective-permute-done.15.y1_ref = bf16[448,128]{1,0:T(8,128)(2,1)S(1)} collective-permute-done((bf16[448,128]{1,0:T(8,128)(2,1)S(1)}, bf16[448,128]{1,0:T(8,128)(2,1)S(1)}, u32[]{:S(2)}, u32[]{:S(2)}) %collective-permute-start.15) | collective-permute-done | bytes 114720 | tf_op jit(solution)/shard_map/ppermute | solution.py:343
  45.1 2.1 %collective-permute-start.6 = (bf16[864,128]{1,0:T(8,128)(2,1)S(1)}, bf16[864,128]{1,0:T(8,128)(2,1)S(1)}, u32[]{:S(2)}, u32[]{:S(2)}) collective-permute-start(bf16[864,128]{1,0:T(8,128)(2,1)S(1)} %get-tuple-element.25), channel_id=1, source_target_pairs={{0,16},{16,0},{32,48},{48,32},{64,80},{80,64},{96,112},{112,96},{1... | collective-permute-start | bytes 663560 | tf_op jit(solution)/shard_map/ppermute | solution.py:317
  47.2 0.9 %shard_map.86 = (bf16[448,128]{1,0:T(8,128)(2,1)S(1)}, f32[1,32]{1,0:T(1,128)}) custom-call(bf16[448,128]{1,0:T(8,128)(2,1)S(1)} %shard_map.85.own_ref, bf16[448,128]{1,0:T(8,128)(2,1)S(1)} %collective-permute-done.15.y1_ref, bf16[448,128]{1,0:T(8,128)(2,1)S(1)} %collective-permute-done.16.y2_ref, bf16[448,128]{1,0:T(8,128)(2,1)S(1)} %collective-permute-done.17.y3_ref), custom_call_target="tpu_custom_call" | custom-call | tf_op jit(solution)/shard_map/pallas_call | solution.py:294
  48.2 1.4 %collective-permute-start.18 = (bf16[448,128]{1,0:T(8,128)(2,1)S(1)}, bf16[448,128]{1,0:T(8,128)(2,1)S(1)}, u32[]{:S(2)}, u32[]{:S(2)}) collective-permute-start(bf16[448,128]{1,0:T(8,128)(2,1)S(1)} %get-tuple-element.36.piece_ref), channel_id=1, source_target_pairs={{0,8},{1,17},{2,10},{3,19},{4,12},{5,21},{6,14},{7,23},{8,0},{9,25... | collective-permute-start | bytes 344072 | tf_op jit(solution)/shard_map/ppermute | solution.py:358
  49.6 0.6 collective-permute-start.19
  50.2 4.8 %collective-permute-done.6.wb_ref = bf16[864,128]{1,0:T(8,128)(2,1)S(1)} collective-permute-done((bf16[864,128]{1,0:T(8,128)(2,1)S(1)}, bf16[864,128]{1,0:T(8,128)(2,1)S(1)}, u32[]{:S(2)}, u32[]{:S(2)}) %collective-permute-start.6) | collective-permute-done | bytes 221216 | tf_op jit(solution)/shard_map/ppermute | solution.py:317
  55.0 1.4 %shard_map.78 = (f32[32,2048]{1,0:T(8,128)S(1)}, f32[32,2048]{1,0:T(8,128)S(1)}, f32[32,2048]{1,0:T(8,128)S(1)}, f32[32,2048]{1,0:T(8,128)S(1)}) custom-call(bf16[2,304,2048]{2,1,0:T(8,128)(2,1)S(1)} %get-tuple-element.23.xs_ref, bf16[864,128]{1,0:T(8,128)(2,1)S(1)} %get-tuple-element.24.wa_ref, bf16[864,128]{1,0:T(8,128)(2,1)S(1)} %collective-permute-done.6.wb_ref), custom_call_target="tpu_custom_call" | custom-call | tf_op jit(solution)/shard_map/pallas_call | solution.py:294
  56.5 3.2 %collective-permute-start.8 = (f32[32,2048]{1,0:T(8,128)S(1)}, f32[32,2048]{1,0:T(8,128)S(1)}, u32[]{:S(2)}, u32[]{:S(2)}) collective-permute-start(f32[32,2048]{1,0:T(8,128)S(1)} %get-tuple-element.28), channel_id=1, source_target_pairs={{0,96},{16,112},{32,0},{48,16},{64,32},{80,48},{96,64},{112,80},{1... | collective-permute-start | bytes 786440 | tf_op jit(solution)/shard_map/ppermute | solution.py:355
  59.8 1.5 %shard_map.82 = (f32[32,2048]{1,0:T(8,128)S(1)}, f32[32,2048]{1,0:T(8,128)S(1)}) custom-call(bf16[128,2048]{1,0:T(8,128)(2,1)S(1)} %collective-permute-done.10.prev_ref, bf16[128,2048]{1,0:T(8,128)(2,1)S(1)} %collective-permute-done.11.next_ref, bf16[32,2048]{1,0:T(8,128)(2,1)S(1)} %get-tuple-element.22.c0.refs_0_, ...), custom_call_target="tpu_custom_call" | custom-call | tf_op jit(solution)/shard_map/pallas_call | solution.py:294
  61.3 2.2 %collective-permute-start.12 = (f32[32,2048]{1,0:T(8,128)S(1)}, f32[32,2048]{1,0:T(8,128)S(1)}, u32[]{:S(2)}, u32[]{:S(2)}) collective-permute-start(f32[32,2048]{1,0:T(8,128)S(1)} %get-tuple-element.31), channel_id=1, source_target_pairs={{0,16},{16,0},{32,48},{48,32},{64,80},{80,64},{96,112},{112,96},{1... | collective-permute-start | bytes 786440 | tf_op jit(solution)/shard_map/ppermute | solution.py:370
  63.7 6.0 %collective-permute-done.7.b = f32[32,2048]{1,0:T(8,128)S(1)} collective-permute-done((f32[32,2048]{1,0:T(8,128)S(1)}, f32[32,2048]{1,0:T(8,128)S(1)}, u32[]{:S(2)}, u32[]{:S(2)}) %collective-permute-start.7) | collective-permute-done | bytes 262176 | tf_op jit(solution)/shard_map/ppermute | solution.py:355
  69.7 0.8 %shard_map.80 = f32[32,2048]{1,0:T(8,128)} custom-call(f32[32,2048]{1,0:T(8,128)S(1)} %get-tuple-element.26.a, f32[32,2048]{1,0:T(8,128)S(1)} %collective-permute-done.7.b, f32[32,2048]{1,0:T(8,128)S(1)} %collective-permute-done.8.c, f32[32,2048]{1,0:T(8,128)S(1)} %collective-permute-done.9.d, f32[32,1]{1,0:T(8,128)S(1)} %shard_map.79.bias_ref), custom_call_target="tpu_custom_call" | custom-call | tf_op jit(solution)/shard_map/pallas_call | solution.py:294
  70.5 0.7 shard_map.83
  71.5 1.7 %shard_map.89 = f32[864,256]{1,0:T(8,128)} custom-call(f32[864,128]{1,0:T(8,128)S(1)} %shard_map.88.own_ref, bf16[896,128]{1,0:T(8,128)(2,1)S(1)} %collective-permute-done.20.other_ref), custom_call_target="tpu_custom_call" | custom-call | tf_op jit(solution)/shard_map/pallas_call | solution.py:294
  (27 shorter events, 0.9 us)
Async XLA Ops:
  0.6 7.0 %collective-permute-start = (bf16[32,2048]{1,0:T(8,128)(2,1)}, bf16[32,2048]{1,0:T(8,128)(2,1)S(1)}, u32[]{:S(2)}, u32[]{:S(2)}) collective-permute-start(bf16[32,2048]{1,0:T(8,128)(2,1)} %bitcast.13), channel_id=1, source_target_pairs={{0,16},{16,0},{32,48},{48,32},{64,80},{80,64},{96,112},{112,96},{1... | collective-permute-start | bytes 393224 | tf_op jit(solution)/shard_map/ppermute | solution.py:308
  7.7 14.1 %collective-permute-start.1 = (bf16[64,2048]{1,0:T(8,128)(2,1)S(1)}, bf16[64,2048]{1,0:T(8,128)(2,1)S(1)}, u32[]{:S(2)}, u32[]{:S(2)}) collective-permute-start(bf16[64,2048]{1,0:T(8,128)(2,1)S(1)} %shard_map.76.here_ref), channel_id=1, source_target_pairs={{0,1},{1,2},{2,3},{3,4},{4,5},{5,6},{6,7},{7,8},{8,9},{9,10},{10,1... | collective-permute-start | bytes 786440 | tf_op jit(solution)/shard_map/ppermute | solution.py:321
  7.8 14.0 %collective-permute-start.2 = (bf16[64,2048]{1,0:T(8,128)(2,1)S(1)}, bf16[64,2048]{1,0:T(8,128)(2,1)S(1)}, u32[]{:S(2)}, u32[]{:S(2)}) collective-permute-start(bf16[64,2048]{1,0:T(8,128)(2,1)S(1)} %shard_map.76.here_ref), channel_id=1, source_target_pairs={{1,0},{2,1},{3,2},{4,3},{5,4},{6,5},{7,6},{8,7},{9,8},{10,9},{11,1... | collective-permute-start | bytes 786440 | tf_op jit(solution)/shard_map/ppermute | solution.py:322
  9.5 8.9 %collective-permute-start.3 = (bf16[32,2048]{1,0:T(8,128)(2,1)}, bf16[32,2048]{1,0:T(8,128)(2,1)S(1)}, u32[]{:S(2)}, u32[]{:S(2)}) collective-permute-start(bf16[32,2048]{1,0:T(8,128)(2,1)} %bitcast.16), channel_id=1, source_target_pairs={{0,96},{16,112},{32,0},{48,16},{64,32},{80,48},{96,64},{112,80},{1... | collective-permute-start | bytes 393224 | tf_op jit(solution)/shard_map/ppermute | solution.py:309
  13.5 7.1 %collective-permute-start.4 = (bf16[32,2048]{1,0:T(8,128)(2,1)}, bf16[32,2048]{1,0:T(8,128)(2,1)S(1)}, u32[]{:S(2)}, u32[]{:S(2)}) collective-permute-start(bf16[32,2048]{1,0:T(8,128)(2,1)} %bitcast.17), channel_id=1, source_target_pairs={{0,64},{16,80},{32,96},{48,112},{64,0},{80,16},{96,32},{112,48},{1... | collective-permute-start | bytes 393224 | tf_op jit(solution)/shard_map/ppermute | solution.py:309
  13.5 8.2 %collective-permute-start.5 = (bf16[32,2048]{1,0:T(8,128)(2,1)}, bf16[32,2048]{1,0:T(8,128)(2,1)S(1)}, u32[]{:S(2)}, u32[]{:S(2)}) collective-permute-start(bf16[32,2048]{1,0:T(8,128)(2,1)} %bitcast.18), channel_id=1, source_target_pairs={{0,32},{16,48},{32,64},{48,80},{64,96},{80,112},{96,0},{112,16},{1... | collective-permute-start | bytes 393224 | tf_op jit(solution)/shard_map/ppermute | solution.py:309
  23.6 1.9 %collective-permute-start.13 = (f32[872,128]{1,0:T(8,128)S(1)}, f32[872,128]{1,0:T(8,128)S(1)}, u32[]{:S(2)}, u32[]{:S(2)}) collective-permute-start(f32[872,128]{1,0:T(8,128)S(1)} %get-tuple-element.33), channel_id=1, source_target_pairs={{0,1},{1,0},{2,3},{3,2},{4,5},{5,4},{6,7},{7,6},{8,9},{9,8},{10,11... | collective-permute-start | bytes 1339400 | tf_op jit(solution)/shard_map/ppermute | solution.py:333
  25.6 8.5 %collective-permute-start.14 = (f32[440,128]{1,0:T(8,128)S(1)}, f32[440,128]{1,0:T(8,128)S(1)}, u32[]{:S(2)}, u32[]{:S(2)}) collective-permute-start(f32[440,128]{1,0:T(8,128)S(1)} %get-tuple-element.35), channel_id=1, source_target_pairs={{0,8},{1,9},{2,10},{3,11},{4,12},{5,13},{6,14},{7,15},{8,0},{9,1},... | collective-permute-start | bytes 675848 | tf_op jit(solution)/shard_map/ppermute | solution.py:338
  26.9 29.7 %collective-permute-start.10 = (bf16[128,2048]{1,0:T(8,128)(2,1)S(1)}, bf16[128,2048]{1,0:T(8,128)(2,1)S(1)}, u32[]{:S(2)}, u32[]{:S(2)}) collective-permute-start(bf16[128,2048]{1,0:T(8,128)(2,1)S(1)} %shard_map.81), channel_id=1, source_target_pairs={{0,1},{1,2},{2,3},{3,4},{4,5},{5,6},{6,7},{7,8},{8,9},{9,10},{10,1... | collective-permute-start | bytes 1572872 | tf_op jit(solution)/shard_map/ppermute | solution.py:339
  27.0 32.8 %collective-permute-start.11 = (bf16[128,2048]{1,0:T(8,128)(2,1)S(1)}, bf16[128,2048]{1,0:T(8,128)(2,1)S(1)}, u32[]{:S(2)}, u32[]{:S(2)}) collective-permute-start(bf16[128,2048]{1,0:T(8,128)(2,1)S(1)} %shard_map.81), channel_id=1, source_target_pairs={{1,0},{2,1},{3,2},{4,3},{5,4},{6,5},{7,6},{8,7},{9,8},{10,9},{11,1... | collective-permute-start | bytes 1572872 | tf_op jit(solution)/shard_map/ppermute | solution.py:340
  34.3 10.8 %collective-permute-start.15 = (bf16[448,128]{1,0:T(8,128)(2,1)S(1)}, bf16[448,128]{1,0:T(8,128)(2,1)S(1)}, u32[]{:S(2)}, u32[]{:S(2)}) collective-permute-start(bf16[448,128]{1,0:T(8,128)(2,1)S(1)} %shard_map.85.own_ref), channel_id=1, source_target_pairs={{0,6},{1,7},{2,0},{3,1},{4,2},{5,3},{6,4},{7,5},{8,14},{9,15},{10,... | collective-permute-start | bytes 344072 | tf_op jit(solution)/shard_map/ppermute | solution.py:343
  35.1 12.2 %collective-permute-start.16 = (bf16[448,128]{1,0:T(8,128)(2,1)S(1)}, bf16[448,128]{1,0:T(8,128)(2,1)S(1)}, u32[]{:S(2)}, u32[]{:S(2)}) collective-permute-start(bf16[448,128]{1,0:T(8,128)(2,1)S(1)} %shard_map.85.own_ref), channel_id=1, source_target_pairs={{0,4},{1,5},{2,6},{3,7},{4,0},{5,1},{6,2},{7,3},{8,12},{9,13},{10,... | collective-permute-start | bytes 344072 | tf_op jit(solution)/shard_map/ppermute | solution.py:343
  36.9 10.3 %collective-permute-start.17 = (bf16[448,128]{1,0:T(8,128)(2,1)S(1)}, bf16[448,128]{1,0:T(8,128)(2,1)S(1)}, u32[]{:S(2)}, u32[]{:S(2)}) collective-permute-start(bf16[448,128]{1,0:T(8,128)(2,1)S(1)} %shard_map.85.own_ref), channel_id=1, source_target_pairs={{0,2},{1,3},{2,4},{3,5},{4,6},{5,7},{6,0},{7,1},{8,10},{9,11},{10,... | collective-permute-start | bytes 344072 | tf_op jit(solution)/shard_map/ppermute | solution.py:343
  45.1 9.9 %collective-permute-start.6 = (bf16[864,128]{1,0:T(8,128)(2,1)S(1)}, bf16[864,128]{1,0:T(8,128)(2,1)S(1)}, u32[]{:S(2)}, u32[]{:S(2)}) collective-permute-start(bf16[864,128]{1,0:T(8,128)(2,1)S(1)} %get-tuple-element.25), channel_id=1, source_target_pairs={{0,16},{16,0},{32,48},{48,32},{64,80},{80,64},{96,112},{112,96},{1... | collective-permute-start | bytes 663560 | tf_op jit(solution)/shard_map/ppermute | solution.py:317
  48.2 13.1 %collective-permute-start.18 = (bf16[448,128]{1,0:T(8,128)(2,1)S(1)}, bf16[448,128]{1,0:T(8,128)(2,1)S(1)}, u32[]{:S(2)}, u32[]{:S(2)}) collective-permute-start(bf16[448,128]{1,0:T(8,128)(2,1)S(1)} %get-tuple-element.36.piece_ref), channel_id=1, source_target_pairs={{0,8},{1,17},{2,10},{3,19},{4,12},{5,21},{6,14},{7,23},{8,0},{9,25... | collective-permute-start | bytes 344072 | tf_op jit(solution)/shard_map/ppermute | solution.py:358
  49.6 13.9 %collective-permute-start.19 = (bf16[448,128]{1,0:T(8,128)(2,1)S(1)}, bf16[448,128]{1,0:T(8,128)(2,1)S(1)}, u32[]{:S(2)}, u32[]{:S(2)}) collective-permute-start(bf16[448,128]{1,0:T(8,128)(2,1)S(1)} %get-tuple-element.36.piece_ref), channel_id=1, source_target_pairs={{0,8},{1,25},{2,10},{3,27},{4,12},{5,29},{6,14},{7,31},{8,0},{9,17... | collective-permute-start | bytes 344072 | tf_op jit(solution)/shard_map/ppermute | solution.py:359
  55.0 8.6 %copy-start = (bf16[32]{0:T(256)(128)(2,1)S(1)}, bf16[32]{0:T(256)(128)(2,1)}, u32[]{:S(2)}) copy-start(bf16[32]{0:T(256)(128)(2,1)} %param.6) | copy-start | bytes 196
  56.5 13.3 %collective-permute-start.7 = (f32[32,2048]{1,0:T(8,128)S(1)}, f32[32,2048]{1,0:T(8,128)S(1)}, u32[]{:S(2)}, u32[]{:S(2)}) collective-permute-start(f32[32,2048]{1,0:T(8,128)S(1)} %get-tuple-element.27), channel_id=1, source_target_pairs={{0,32},{16,48},{32,64},{48,80},{64,96},{80,112},{96,0},{112,16},{1... | collective-permute-start | bytes 786440 | tf_op jit(solution)/shard_map/ppermute | solution.py:355
  56.5 13.2 %collective-permute-start.8 = (f32[32,2048]{1,0:T(8,128)S(1)}, f32[32,2048]{1,0:T(8,128)S(1)}, u32[]{:S(2)}, u32[]{:S(2)}) collective-permute-start(f32[32,2048]{1,0:T(8,128)S(1)} %get-tuple-element.28), channel_id=1, source_target_pairs={{0,96},{16,112},{32,0},{48,16},{64,32},{80,48},{96,64},{112,80},{1... | collective-permute-start | bytes 786440 | tf_op jit(solution)/shard_map/ppermute | solution.py:355
  59.8 10.0 %collective-permute-start.9 = (f32[32,2048]{1,0:T(8,128)S(1)}, f32[32,2048]{1,0:T(8,128)S(1)}, u32[]{:S(2)}, u32[]{:S(2)}) collective-permute-start(f32[32,2048]{1,0:T(8,128)S(1)} %get-tuple-element.29), channel_id=1, source_target_pairs={{0,64},{16,80},{32,96},{48,112},{64,0},{80,16},{96,32},{112,48},{1... | collective-permute-start | bytes 786440 | tf_op jit(solution)/shard_map/ppermute | solution.py:355
  61.3 9.3 %collective-permute-start.12 = (f32[32,2048]{1,0:T(8,128)S(1)}, f32[32,2048]{1,0:T(8,128)S(1)}, u32[]{:S(2)}, u32[]{:S(2)}) collective-permute-start(f32[32,2048]{1,0:T(8,128)S(1)} %get-tuple-element.31), channel_id=1, source_target_pairs={{0,16},{16,0},{32,48},{48,32},{64,80},{80,64},{96,112},{112,96},{1... | collective-permute-start | bytes 786440 | tf_op jit(solution)/shard_map/ppermute | solution.py:370
  63.5 7.9 %collective-permute-start.20 = (bf16[896,128]{1,0:T(8,128)(2,1)S(1)}, bf16[896,128]{1,0:T(8,128)(2,1)S(1)}, u32[]{:S(2)}, u32[]{:S(2)}) collective-permute-start(bf16[896,128]{1,0:T(8,128)(2,1)S(1)} %shard_map.87.pair_ref), channel_id=1, source_target_pairs={{0,1},{1,0},{2,3},{3,2},{4,5},{5,4},{6,7},{7,6},{8,9},{9,8},{10,11... | collective-permute-start | bytes 688136 | tf_op jit(solution)/shard_map/ppermute | solution.py:374

commit v5 on v4

v5 whole, which is shorter than its diff:
```python
import functools

import jax
import jax.numpy as jnp
from jax import lax
from jax.experimental import pallas as pl
from jax.experimental.pallas import tpu as pltpu
from jax.sharding import PartitionSpec as P


ROWS = 32
WIDE = 64
PLANE = ROWS * WIDE
OWN = 32
TAPS = 9 * OWN
HALF = 3 * TAPS
PIECE = HALF // 2
CODED = PIECE + 16
POWER = 15.0
TOP = 120.0
BF = jnp.bfloat16
F32 = jnp.float32

VM = pl.BlockSpec(memory_space=pltpu.VMEM)
PARAMS = pltpu.CompilerParams(vmem_limit_bytes=48 * 1024 * 1024)


def along_z(step):
    return [(f, ((f // 2 + step) % 4) * 2 + f % 2) for f in range(8)]


ACROSS = [(f, f ^ 1) for f in range(8)]
BESIDE = [(s, (s + 1) % 16 if s & 1 else (s - 1) % 16) for s in range(16)]
CORE = [(s, s ^ 1) for s in range(16)]
XLO = [(s, s ^ 8) for s in range(16)]


def along_y(step):
    return [(s, (s & 9) | ((((s >> 1) + step) & 3) << 1)) for s in range(16)]


def crossing(flip, idle):
    return [
        (f * 16 + s, (f ^ 1) * 16 + (s ^ flip) if s & 1 else f * 16 + (s ^ idle))
        for f in range(8)
        for s in range(16)
    ]


def columns(shape):
    return lax.broadcasted_iota(jnp.int32, shape, 1) & (WIDE - 1)


def lanes(shape):
    return lax.broadcasted_iota(jnp.int32, shape, 1)


def select_kernel(w_hbm, x_hbm, c_hbm, mine_ref, theirs_ref, x_out, c_out, w_ref, sems):
    copies = [
        pltpu.make_async_copy(a, b, sems.at[i])
        for i, (a, b) in enumerate(((w_hbm, w_ref), (x_hbm, x_out), (c_hbm, c_out)))
    ]
    for copy in copies:
        copy.start()
    filt = lax.axis_index("filt")
    z, xh = filt // 2, filt % 2
    src = lax.broadcasted_iota(jnp.int32, (256, 256), 0)
    lane = lax.broadcasted_iota(jnp.int32, (256, 256), 1)
    side, turn, chan = lane >> 7, (lane >> 5) & 3, lane & 31
    want = ((z + turn) & 3) * 64 + ((xh + side) & 1) * 32 + chan
    pick = jnp.where(src == want, 1.0, 0.0).astype(BF)
    for copy in copies:
        copy.wait()
    got = jnp.dot(w_ref[...], pick, preferred_element_type=F32).astype(BF)
    mine_ref[...] = got[:, :128]
    theirs_ref[...] = got[:, 128:]


def join_kernel(*refs):
    *parts, out_ref = refs
    at = 0
    for ref in parts:
        out_ref[at : at + ref.shape[0], :] = ref[...]
        at += ref.shape[0]


def forward_kernel(xs_ref, wa_ref, wb_ref, o0, o1, o2, o3):
    rhs = jnp.concatenate([xs_ref[0, :TAPS, :], xs_ref[1, :TAPS, :]], axis=0)
    parts = []
    for kh in range(3):
        lhs = jnp.concatenate(
            [w[(kd * 3 + kh) * 96 : (kd * 3 + kh) * 96 + 96, :] for w in (wa_ref, wb_ref) for kd in range(3)],
            axis=0,
        )
        parts.append(
            lax.dot_general(lhs, rhs, (((0,), (0,)), ((), ())), preferred_element_type=F32)
        )
    lane = lanes((128, PLANE))
    total = (
        parts[1]
        + jnp.where(lane < WIDE, 0.0, pltpu.roll(parts[0], WIDE, 1))
        + jnp.where(lane >= PLANE - WIDE, 0.0, pltpu.roll(parts[2], PLANE - WIDE, 1))
    )
    for r, ref in enumerate((o0, o1, o2, o3)):
        ref[...] = total[r * 32 : r * 32 + 32]


def row_shifts(wide):
    lane = lanes(wide.shape)
    turned = pltpu.roll(wide, PLANE - WIDE, 1)
    up = jnp.where(lane >= PLANE - WIDE, 0.0, turned)
    down = jnp.where(lane < WIDE, 0.0, pltpu.roll(wide, WIDE, 1))
    return up.astype(BF), wide.astype(BF), down.astype(BF)


def beside():
    space = lax.axis_index("space")
    inside = jnp.logical_and(space != 0, space != 15).astype(F32)
    return inside, (space & 1) == 0


def kernel_grad_kernel(chip_ref, here_ref, far_ref, c0, c1, c2, c3, xs_ref, keep_ref, send_ref, cs_ref):
    core = lax.axis_index("space") & 1
    col = columns((64, PLANE))
    inside, even = beside()
    for ref, kd in ((chip_ref, jnp.where(even, 2, 0)), (here_ref, 1), (far_ref, jnp.where(even, 0, 2))):
        wide = ref[...].astype(F32)
        if ref is far_ref:
            wide = wide * inside
        left = jnp.where(col == 0, 0.0, pltpu.roll(wide, 1, 1))
        right = jnp.where(col == WIDE - 1, 0.0, pltpu.roll(wide, PLANE - 1, 1))
        for kw, part in enumerate((left, wide, right)):
            rows = pl.ds(pl.multiple_of((kd * 3 + kw) * OWN, OWN), OWN)
            narrow = part.astype(BF)
            xs_ref[0, rows, :] = narrow[:OWN]
            xs_ref[1, rows, :] = narrow[OWN:]
    xs_ref[:, TAPS:, :] = jnp.ones((2, 16, PLANE), BF)
    for r, ref in enumerate((c0, c1, c2, c3)):
        for kh, part in enumerate(row_shifts(ref[...].astype(F32))):
            cs_ref[kh * 128 + r * 32 : kh * 128 + r * 32 + 32, :] = part
    for slot, ref in enumerate((keep_ref, send_ref)):
        got = lax.dot_general(
            xs_ref[core ^ slot], cs_ref[...], (((1,), (1,)), ((), ())), preferred_element_type=F32
        )
        for kh in range(3):
            ref[kh * TAPS : (kh + 1) * TAPS, :] = got[:TAPS, kh * 128 : kh * 128 + 128]
        ref[HALF:, :] = got[TAPS : TAPS + 8, 128:256]


def input_grad_kernel(chip_ref, far_ref, c0, c1, c2, c3, wa_ref, wb_ref, mine_ref, theirs_ref, cs_ref):
    inside, even = beside()
    for r, ref in enumerate((c0, c1, c2, c3)):
        rows = slice(r * 32, r * 32 + 32)
        planes = (
            chip_ref[rows, :].astype(F32),
            ref[...].astype(F32),
            far_ref[rows, :].astype(F32) * inside,
        )
        for kd, wide in enumerate(planes):
            for kh, part in enumerate(row_shifts(wide)):
                at = (kd * 3 + kh) * 128 + r * 32
                cs_ref[at : at + 32, :] = part

    def taps(w, kd, kh):
        ahead, here, behind = (w[(k * 3 + kh) * 96 : (k * 3 + kh) * 96 + 96, :] for k in range(3))
        if kd == 1:
            return here
        first, second = (ahead, behind) if kd == 0 else (behind, ahead)
        return jnp.where(even, first, second)

    lhs = jnp.concatenate(
        [
            jnp.concatenate([taps(w, kd, kh) for kd in range(3) for kh in range(3)], axis=1)
            for w in (wa_ref, wb_ref)
        ],
        axis=0,
    )
    got = jnp.dot(lhs, cs_ref[...], preferred_element_type=F32)
    col = columns((OWN, PLANE))
    for h in range(2):
        base = h * 96
        part = (
            got[base + 32 : base + 64]
            + jnp.where(col == WIDE - 1, 0.0, pltpu.roll(got[base : base + 32], PLANE - 1, 1))
            + jnp.where(col == 0, 0.0, pltpu.roll(got[base + 64 : base + 96], 1, 1))
        )
        if h == 0:
            mine_ref[...] = part
        else:
            theirs_ref[:, :PLANE], scale = encode(part)
            theirs_ref[:, PLANE:] = jnp.broadcast_to(scale, (OWN, 128)).astype(BF)


def encode(wide):
    size = jnp.abs(wide)
    scale = jnp.max(jnp.max(size, axis=1, keepdims=True), axis=0, keepdims=True)
    scale = jnp.maximum(scale, 1e-30).astype(BF).astype(F32)
    coded = jnp.exp2(jnp.log2(size * (1.0 / scale)) * POWER + TOP)
    return jnp.where(wide < 0, -coded, coded).astype(BF), scale


def decode(coded, scale):
    wide = coded.astype(F32)
    size = scale * jnp.exp2((jnp.log2(jnp.abs(wide)) - TOP) * (1.0 / POWER))
    return jnp.where(wide < 0, -size, size)


def write_coded(out_ref, wide, bias):
    coded, scale = encode(wide)
    high = bias.astype(BF).astype(F32)
    low = bias - high
    row = lax.broadcasted_iota(jnp.int32, (16, 128), 0)
    tail = jnp.where(row == 0, scale, jnp.where(row == 1, high, jnp.where(row == 2, low, 0.0)))
    out_ref[:PIECE, :] = coded
    out_ref[PIECE:, :] = tail.astype(BF)


def read_coded(ref, at=0):
    tail = ref[at + PIECE : at + CODED, :].astype(F32)
    return decode(ref[at : at + PIECE, :], tail[0:1, 0:1]), tail[1:2, :] + tail[2:3, :]


def split_xlo_kernel(keep_ref, got_ref, send_out, cross_out, keep_out):
    xlo = lax.axis_index("space") // 8
    bias = keep_ref[HALF:, :] + got_ref[HALF:, :]
    send, keep = (
        keep_ref[rows, :] + got_ref[rows, :]
        for rows in (pl.ds(pl.multiple_of(at, 8), PIECE) for at in ((1 - xlo) * PIECE, xlo * PIECE))
    )
    write_coded(send_out, send, bias[:1])
    write_coded(cross_out, keep, bias[:1])
    keep_out[:PIECE, :] = keep
    keep_out[PIECE:, :] = bias


def code_kernel(keep_ref, near_ref, far_ref, out_ref):
    even = (lax.axis_index("space") & 1) == 0
    near, far = read_coded(near_ref), read_coded(far_ref)
    write_coded(
        out_ref,
        jnp.where(even, keep_ref[:PIECE, :], near[0]) + far[0],
        jnp.where(even, keep_ref[PIECE : PIECE + 1, :], near[1]) + far[1],
    )


def piece_kernel(own_ref, y1_ref, y2_ref, y3_ref, out_ref, *, factor):
    own, y1, y2, y3 = (read_coded(r) for r in (own_ref, y1_ref, y2_ref, y3_ref))
    wide, bias = ((own[i] + y2[i]) + (y1[i] + y3[i]) for i in range(2))
    z = lax.axis_index("filt") // 2
    write_coded(out_ref, pltpu.roll(wide * factor, z * 32, 1), bias * factor)


def place(pair_ref, out_ref):
    xlo = lax.axis_index("space") // 8
    for rx in range(2):
        to = pl.multiple_of((xlo ^ rx) * PIECE, 8)
        wide, bias = read_coded(pair_ref, rx * CODED)
        out_ref[pl.ds(to, PIECE), :] = wide
    return bias[:, :OWN]


def side_of(swap):
    return (lax.axis_index("filt") ^ lax.axis_index("space") ^ swap) & 1


def spread(wide, side):
    first, second, third, fourth = (
        pltpu.roll(wide, ((side + j) & 3) * 32, 1) for j in range(4)
    )
    low = lanes(wide.shape) < 64
    return jnp.where(low, first, second), jnp.where(low, third, fourth)


def decode_kernel(pair_ref, out_ref, bias_ref, half_ref):
    bias_ref[...] = place(pair_ref, half_ref)
    out_ref[:, :128], out_ref[:, 128:] = spread(half_ref[...], side_of(0))


def assemble_kernel(own_ref, own_bias_ref, other_ref, grad_hbm, bias_ref, half_ref, grad_ref, sems):
    bias = place(other_ref, half_ref)
    core = lax.axis_index("space") & 1
    bias_ref[...] = jnp.where(core == 0, own_bias_ref[...], bias)
    side = side_of(1)
    theirs = ((lanes((TAPS, 128)) >> 5) & 1) == side
    copies = []
    for kh in range(3):
        rows = slice(kh * TAPS, kh * TAPS + TAPS)
        for t, part in enumerate(spread(half_ref[rows, :], side)):
            cols = slice(t * 128, t * 128 + 128)
            whole = jnp.where(theirs, part, own_ref[rows, cols])
            grad_ref[kh, :, :, cols] = whole.reshape(3, 96, 128)
        copies.append(pltpu.make_async_copy(grad_ref.at[kh], grad_hbm.at[:, kh], sems.at[kh]))
        copies[-1].start()
    for copy in copies:
        copy.wait()


def bias_kernel(ref, out):
    row = lax.broadcasted_iota(jnp.int32, (OWN, OWN), 0)
    col = lax.broadcasted_iota(jnp.int32, (OWN, OWN), 1)
    wide = jnp.where(row == col, ref[...].astype(F32), 0.0)
    out[...] = jnp.sum(wide, axis=1, keepdims=True)


def biased_kernel(ref, bias_ref, out):
    out[...] = ref[...] + bias_ref[...]


def sums_kernel(a, b, c, d, mine_ref, theirs_ref, out, grad):
    out[...] = (a[...] + b[...]) + (c[...] + d[...])
    scale = theirs_ref[0:1, PLANE : PLANE + 1].astype(F32)
    grad[...] = mine_ref[...] + decode(theirs_ref[:, :PLANE], scale)


def call(kernel, outs, *args, scratch=(), space=VM, out_space=VM):
    return pl.pallas_call(
        kernel,
        out_shape=[jax.ShapeDtypeStruct(s, d) for s, d in outs],
        in_specs=[space] * len(args),
        out_specs=[out_space] + [VM] * (len(outs) - 1),
        scratch_shapes=list(scratch),
        compiler_params=PARAMS,
    )(*args)


def step(inputs, weight, bias, cotangent):
    x_own = inputs[0]
    c_own = cotangent[0]

    x_other = lax.ppermute(x_own, "filt", ACROSS)
    c1, c3, c2 = (lax.ppermute(c_own, "filt", along_z(-r)) for r in (1, 3, 2))
    w_mine, w_theirs, x_near, c_near = call(
        select_kernel,
        [((864, 128), BF), ((864, 128), BF), ((OWN, PLANE), BF), ((OWN, PLANE), BF)],
        *(pltpu.with_memory_space_constraint(v, pltpu.HBM) for v in (weight.reshape(864, 256), x_own, c_own)),
        scratch=[pltpu.VMEM((864, 256), BF), pltpu.SemaphoreType.DMA((3,))],
        space=pl.BlockSpec(memory_space=pltpu.HBM),
    )
    w_other = lax.ppermute(w_theirs, "filt", ACROSS)
    cots = [c_near, c1, c2, c3]

    (x_here,) = call(join_kernel, [((64, PLANE), BF)], x_near, x_other)
    x_chip = lax.ppermute(x_here, "space", CORE)
    x_far = lax.ppermute(x_here, "space", BESIDE)

    xs, keep, send = call(
        kernel_grad_kernel,
        [((2, TAPS + 16, PLANE), BF)] + [((HALF + 8, 128), F32)] * 2,
        x_chip,
        x_here,
        x_far,
        *cots,
        scratch=[pltpu.VMEM((384, PLANE), BF)],
    )
    r_core = lax.ppermute(send, "space", CORE)
    outs = call(forward_kernel, [((32, PLANE), F32)] * 4, xs, w_mine, w_other)
    (c_here,) = call(join_kernel, [((128, PLANE), BF)], *cots)

    r_send, r_cross, r_keep = call(
        split_xlo_kernel, [((CODED, 128), BF)] * 2 + [((PIECE + 8, 128), F32)], keep, r_core
    )
    r_far = lax.ppermute(r_send, ("filt", "space"), crossing(8, 8))
    r_near = lax.ppermute(r_cross, ("filt", "space"), crossing(0, 2))
    c_chip = lax.ppermute(c_here, "space", CORE)
    c_far = lax.ppermute(c_here, "space", BESIDE)

    (mine_y,) = call(code_kernel, [((CODED, 128), BF)], r_keep, r_near, r_far)
    y1, y3, y2 = (lax.ppermute(mine_y, "space", along_y(-r)) for r in (1, 3, 2))
    factor = float((16 * PLANE) ** -0.5)
    (piece,) = call(
        functools.partial(piece_kernel, factor=factor), [((CODED, 128), BF)], mine_y, y1, y2, y3
    )

    (wide_bias,) = call(bias_kernel, [((OWN, 1), F32)], bias.reshape(1, OWN))
    (biased,) = call(biased_kernel, [((OWN, PLANE), F32)], outs[0], wide_bias)
    sums = [lax.ppermute(outs[r], "filt", along_z(r)) for r in (1, 3, 2)]
    g_mine, g_theirs = call(
        input_grad_kernel,
        [((OWN, PLANE), F32), ((OWN, PLANE + 128), BF)],
        c_chip,
        c_far,
        *cots,
        w_mine,
        w_other,
        scratch=[pltpu.VMEM((9 * 128, PLANE), BF)],
    )
    g_other = lax.ppermute(g_theirs, "filt", ACROSS)
    output, grad_inputs = call(
        sums_kernel, [((OWN, PLANE), F32)] * 2, biased, *sums, g_mine, g_other
    )

    piece_far = lax.ppermute(piece, "space", XLO)
    (pair,) = call(join_kernel, [((2 * CODED, 128), BF)], piece, piece_far)
    other = lax.ppermute(pair, "space", CORE)
    mine, mine_bias = call(
        decode_kernel,
        [((HALF, 256), F32), ((1, OWN), F32)],
        pair,
        scratch=[pltpu.VMEM((HALF, 128), F32)],
    )
    grad_weight, grad_bias = call(
        assemble_kernel,
        [((3, 3, 96, 256), F32), ((1, OWN), F32)],
        mine,
        mine_bias,
        other,
        scratch=[
            pltpu.VMEM((HALF, 128), F32),
            pltpu.VMEM((3, 3, 96, 256), F32),
            pltpu.SemaphoreType.DMA((3,)),
        ],
        out_space=pl.BlockSpec(memory_space=pltpu.HBM),
    )
    return (
        output[None],
        grad_inputs[None],
        grad_weight.reshape(3, 3, 3, OWN, 256),
        grad_bias.reshape(OWN),
    )


def solution(mesh):
    placed = (
        P("space", "filt", None),
        P(None, None, None, "filt", None),
        P("filt"),
        P("space", "filt", None),
    )
    return jax.shard_map(
        step,
        mesh=mesh,
        in_specs=placed,
        out_specs=(
            P("space", "filt", None),
            P("space", "filt", None),
            P(None, None, None, "filt", None),
            P("filt"),
        ),
        check_vma=False,
    )
```

time: 73.3 us -> 74.1 us (1.011)
  the two profiles are of different devices: /device:TPU:26 before, /device:TPU:1 now
where the time goes in v5:
time: 74.1 us; the launch traced here: 73.2 us
  starting transfers between devices  30.9 us (42%)
  waiting for transfers between devices  29.8 us (40%)
  Pallas kernels  11.5 us (16%)
  between operations  0.93 us (1%)
    pallas_call x15, Pallas kernels, call(): pl.pallas_call(kernel, out_shape=[jax.ShapeDtypeStruct(s, d) for s, d in...  11.5 us
    ppermute x3, waiting for transfers between devices, step(): y1, y3, y2 = (lax.ppermute(mine_y, 'space', along_y(-r)) for r in (1, 3, 2))  6.37 us
    ppermute x3, waiting for transfers between devices, step(): c1, c3, c2 = (lax.ppermute(c_own, 'filt', along_z(-r)) for r in (1, 3, 2))  5.94 us
    ppermute x1, waiting for transfers between devices, step(): w_other = lax.ppermute(w_theirs, 'filt', ACROSS)  4.97 us
    ppermute x3, starting transfers between devices, step(): c1, c3, c2 = (lax.ppermute(c_own, 'filt', along_z(-r)) for r in (1, 3, 2))  4.46 us
    ppermute x1, starting transfers between devices, step(): r_core = lax.ppermute(send, 'space', CORE)  4.29 us
    ppermute x3, waiting for transfers between devices, step(): sums = [lax.ppermute(outs[r], 'filt', along_z(r)) for r in (1, 3, 2)]  3.81 us
    ppermute x1, starting transfers between devices, step(): x_other = lax.ppermute(x_own, 'filt', ACROSS)  3.64 us
  transfers between devices with their start and end apart: 21, of which 12 were waited for; matrix products, arithmetic and copies ran while one was open for 0% of the time, Pallas kernels for 10%

profile of v5, /device:TPU:1, one launch (start us, length us, event | category | flops | bytes accessed | tf_op | source)
XLA Modules:
  0.0 73.2 jit_solution(16544741326694164519)
XLA Ops:
  0.6 3.6 %collective-permute-start = (bf16[32,2048]{1,0:T(8,128)(2,1)}, bf16[32,2048]{1,0:T(8,128)(2,1)S(1)}, u32[]{:S(2)}, u32[]{:S(2)}) collective-permute-start(bf16[32,2048]{1,0:T(8,128)(2,1)} %bitcast.10), channel_id=1, source_target_pairs={{0,16},{16,0},{32,48},{48,32},{64,80},{80,64},{96,112},{112,96},{1... | collective-permute-start | bytes 393224 | tf_op jit(solution)/shard_map/ppermute | solution.py:330
  4.3 1.4 %shard_map.75 = (bf16[864,128]{1,0:T(8,128)(2,1)S(1)}, bf16[864,128]{1,0:T(8,128)(2,1)S(1)}, bf16[32,2048]{1,0:T(8,128)(2,1)S(1)}, bf16[32,2048]{1,0:T(8,128)(2,1)S(1)}) custom-call(bf16[864,256]{1,0:T(8,128)(2,1)} %bitcast.9, bf16[32,2048]{1,0:T(8,128)(2,1)} %bitcast.11, bf16[32,2048]{1,0:T(8,128)(2,1)} %bitcast.12), custom_call_target="tpu_custom_call" | custom-call | tf_op jit(solution)/shard_map/pallas_call | solution.py:316
  5.7 1.6 %collective-permute-done.refs_1_ = bf16[32,2048]{1,0:T(8,128)(2,1)S(1)} collective-permute-done((bf16[32,2048]{1,0:T(8,128)(2,1)}, bf16[32,2048]{1,0:T(8,128)(2,1)S(1)}, u32[]{:S(2)}, u32[]{:S(2)}) %collective-permute-start) | collective-permute-done | bytes 131104 | tf_op jit(solution)/shard_map/ppermute | solution.py:330
  7.3 1.7 %collective-permute-start.1 = (bf16[64,2048]{1,0:T(8,128)(2,1)S(1)}, bf16[64,2048]{1,0:T(8,128)(2,1)S(1)}, u32[]{:S(2)}, u32[]{:S(2)}) collective-permute-start(bf16[64,2048]{1,0:T(8,128)(2,1)S(1)} %shard_map.76.here_ref), channel_id=1, source_target_pairs={{0,1},{1,0},{2,3},{3,2},{4,5},{5,4},{6,7},{7,6},{8,9},{9,8},{10,11... | collective-permute-start | bytes 786440 | tf_op jit(solution)/shard_map/ppermute | solution.py:343
  9.0 1.5 %collective-permute-start.2 = (bf16[64,2048]{1,0:T(8,128)(2,1)S(1)}, bf16[64,2048]{1,0:T(8,128)(2,1)S(1)}, u32[]{:S(2)}, u32[]{:S(2)}) collective-permute-start(bf16[64,2048]{1,0:T(8,128)(2,1)S(1)} %shard_map.76.here_ref), channel_id=1, source_target_pairs={{0,15},{1,2},{2,1},{3,4},{4,3},{5,6},{6,5},{7,8},{8,7},{9,10},{10,... | collective-permute-start | bytes 786440 | tf_op jit(solution)/shard_map/ppermute | solution.py:344
  10.5 3.8 %collective-permute-start.3 = (bf16[32,2048]{1,0:T(8,128)(2,1)}, bf16[32,2048]{1,0:T(8,128)(2,1)S(1)}, u32[]{:S(2)}, u32[]{:S(2)}) collective-permute-start(bf16[32,2048]{1,0:T(8,128)(2,1)} %bitcast.13), channel_id=1, source_target_pairs={{0,96},{16,112},{32,0},{48,16},{64,32},{80,48},{96,64},{112,80},{1... | collective-permute-start | bytes 393224 | tf_op jit(solution)/shard_map/ppermute | solution.py:331
  14.3 0.7 collective-permute-start.5
  15.0 2.6 %collective-permute-done.3.c1.refs_1_ = bf16[32,2048]{1,0:T(8,128)(2,1)S(1)} collective-permute-done((bf16[32,2048]{1,0:T(8,128)(2,1)}, bf16[32,2048]{1,0:T(8,128)(2,1)S(1)}, u32[]{:S(2)}, u32[]{:S(2)}) %collective-permute-start.3) | collective-permute-done | bytes 131104 | tf_op jit(solution)/shard_map/ppermute | solution.py:331
  17.6 2.3 %collective-permute-done.4.c2.refs_2_ = bf16[32,2048]{1,0:T(8,128)(2,1)S(1)} collective-permute-done((bf16[32,2048]{1,0:T(8,128)(2,1)}, bf16[32,2048]{1,0:T(8,128)(2,1)S(1)}, u32[]{:S(2)}, u32[]{:S(2)}) %collective-permute-start.4) | collective-permute-done | bytes 131104 | tf_op jit(solution)/shard_map/ppermute | solution.py:331
  19.9 1.0 %collective-permute-done.5.c3.refs_3_ = bf16[32,2048]{1,0:T(8,128)(2,1)S(1)} collective-permute-done((bf16[32,2048]{1,0:T(8,128)(2,1)}, bf16[32,2048]{1,0:T(8,128)(2,1)S(1)}, u32[]{:S(2)}, u32[]{:S(2)}) %collective-permute-start.5) | collective-permute-done | bytes 131104 | tf_op jit(solution)/shard_map/ppermute | solution.py:331
  20.9 1.9 %shard_map.77 = (bf16[2,304,2048]{2,1,0:T(8,128)(2,1)S(1)}, f32[872,128]{1,0:T(8,128)S(1)}, f32[872,128]{1,0:T(8,128)S(1)}) custom-call(bf16[64,2048]{1,0:T(8,128)(2,1)S(1)} %collective-permute-done.1.chip_ref, bf16[64,2048]{1,0:T(8,128)(2,1)S(1)} %shard_map.76.here_ref, bf16[64,2048]{1,0:T(8,128)(2,1)S(1)} %collective-permute-done.2.far_ref, ...), custom_call_target="tpu_custom_call" | custom-call | tf_op jit(solution)/shard_map/pallas_call | solution.py:316
  22.9 4.3 %collective-permute-start.13 = (f32[872,128]{1,0:T(8,128)S(1)}, f32[872,128]{1,0:T(8,128)S(1)}, u32[]{:S(2)}, u32[]{:S(2)}) collective-permute-start(f32[872,128]{1,0:T(8,128)S(1)} %get-tuple-element.40), channel_id=1, source_target_pairs={{0,1},{1,0},{2,3},{3,2},{4,5},{5,4},{6,7},{7,6},{8,9},{9,8},{10,11... | collective-permute-start | bytes 1339400 | tf_op jit(solution)/shard_map/ppermute | solution.py:355
  27.3 1.3 %collective-permute-done.13.got_ref = f32[872,128]{1,0:T(8,128)S(1)} collective-permute-done((f32[872,128]{1,0:T(8,128)S(1)}, f32[872,128]{1,0:T(8,128)S(1)}, u32[]{:S(2)}, u32[]{:S(2)}) %collective-permute-start.13) | collective-permute-done | bytes 446496 | tf_op jit(solution)/shard_map/ppermute | solution.py:355
  29.0 2.5 %collective-permute-start.14 = (bf16[448,128]{1,0:T(8,128)(2,1)S(1)}, bf16[448,128]{1,0:T(8,128)(2,1)S(1)}, u32[]{:S(2)}, u32[]{:S(2)}) collective-permute-start(bf16[448,128]{1,0:T(8,128)(2,1)S(1)} %get-tuple-element.42), channel_id=1, source_target_pairs={{0,2},{1,17},{2,0},{3,19},{4,6},{5,21},{6,4},{7,23},{8,10},{9,25},... | collective-permute-start | bytes 344072 | tf_op jit(solution)/shard_map/ppermute | solution.py:363
  31.9 2.2 %collective-permute-done.14.near_ref = bf16[448,128]{1,0:T(8,128)(2,1)S(1)} collective-permute-done((bf16[448,128]{1,0:T(8,128)(2,1)S(1)}, bf16[448,128]{1,0:T(8,128)(2,1)S(1)}, u32[]{:S(2)}, u32[]{:S(2)}) %collective-permute-start.14) | collective-permute-done | bytes 114720 | tf_op jit(solution)/shard_map/ppermute | solution.py:363
  34.2 2.5 %collective-permute-done.15.far_ref = bf16[448,128]{1,0:T(8,128)(2,1)S(1)} collective-permute-done((bf16[448,128]{1,0:T(8,128)(2,1)S(1)}, bf16[448,128]{1,0:T(8,128)(2,1)S(1)}, u32[]{:S(2)}, u32[]{:S(2)}) %collective-permute-start.15) | collective-permute-done | bytes 114720 | tf_op jit(solution)/shard_map/ppermute | solution.py:362
  37.0 1.4 %collective-permute-start.16 = (bf16[448,128]{1,0:T(8,128)(2,1)S(1)}, bf16[448,128]{1,0:T(8,128)(2,1)S(1)}, u32[]{:S(2)}, u32[]{:S(2)}) collective-permute-start(bf16[448,128]{1,0:T(8,128)(2,1)S(1)} %shard_map.85.own_ref), channel_id=1, source_target_pairs={{0,6},{1,7},{2,0},{3,1},{4,2},{5,3},{6,4},{7,5},{8,14},{9,15},{10,... | collective-permute-start | bytes 344072 | tf_op jit(solution)/shard_map/ppermute | solution.py:368
  38.4 1.1 %collective-permute-start.17 = (bf16[448,128]{1,0:T(8,128)(2,1)S(1)}, bf16[448,128]{1,0:T(8,128)(2,1)S(1)}, u32[]{:S(2)}, u32[]{:S(2)}) collective-permute-start(bf16[448,128]{1,0:T(8,128)(2,1)S(1)} %shard_map.85.own_ref), channel_id=1, source_target_pairs={{0,4},{1,5},{2,6},{3,7},{4,0},{5,1},{6,2},{7,3},{8,12},{9,13},{10,... | collective-permute-start | bytes 344072 | tf_op jit(solution)/shard_map/ppermute | solution.py:368
  39.8 6.1 %collective-permute-done.16.y1_ref = bf16[448,128]{1,0:T(8,128)(2,1)S(1)} collective-permute-done((bf16[448,128]{1,0:T(8,128)(2,1)S(1)}, bf16[448,128]{1,0:T(8,128)(2,1)S(1)}, u32[]{:S(2)}, u32[]{:S(2)}) %collective-permute-start.16) | collective-permute-done | bytes 114720 | tf_op jit(solution)/shard_map/ppermute | solution.py:368
  46.0 1.2 %collective-permute-start.6 = (bf16[864,128]{1,0:T(8,128)(2,1)S(1)}, bf16[864,128]{1,0:T(8,128)(2,1)S(1)}, u32[]{:S(2)}, u32[]{:S(2)}) collective-permute-start(bf16[864,128]{1,0:T(8,128)(2,1)S(1)} %get-tuple-element.30), channel_id=1, source_target_pairs={{0,16},{16,0},{32,48},{48,32},{64,80},{80,64},{96,112},{112,96},{1... | collective-permute-start | bytes 663560 | tf_op jit(solution)/shard_map/ppermute | solution.py:339
  48.0 1.3 %collective-permute-start.19 = (bf16[448,128]{1,0:T(8,128)(2,1)S(1)}, bf16[448,128]{1,0:T(8,128)(2,1)S(1)}, u32[]{:S(2)}, u32[]{:S(2)}) collective-permute-start(bf16[448,128]{1,0:T(8,128)(2,1)S(1)} %shard_map.86.refs_0_), channel_id=1, source_target_pairs={{0,8},{1,9},{2,10},{3,11},{4,12},{5,13},{6,14},{7,15},{8,0},{9,1},... | collective-permute-start | bytes 344072 | tf_op jit(solution)/shard_map/ppermute | solution.py:392
  49.3 5.0 %collective-permute-done.6.wb_ref = bf16[864,128]{1,0:T(8,128)(2,1)S(1)} collective-permute-done((bf16[864,128]{1,0:T(8,128)(2,1)S(1)}, bf16[864,128]{1,0:T(8,128)(2,1)S(1)}, u32[]{:S(2)}, u32[]{:S(2)}) %collective-permute-start.6) | collective-permute-done | bytes 221216 | tf_op jit(solution)/shard_map/ppermute | solution.py:339
  54.3 1.4 %shard_map.78 = (f32[32,2048]{1,0:T(8,128)S(1)}, f32[32,2048]{1,0:T(8,128)S(1)}, f32[32,2048]{1,0:T(8,128)S(1)}, f32[32,2048]{1,0:T(8,128)S(1)}) custom-call(bf16[2,304,2048]{2,1,0:T(8,128)(2,1)S(1)} %get-tuple-element.28.xs_ref, bf16[864,128]{1,0:T(8,128)(2,1)S(1)} %get-tuple-element.29.wa_ref, bf16[864,128]{1,0:T(8,128)(2,1)S(1)} %collective-permute-done.6.wb_ref), custom_call_target="tpu_custom_call" | custom-call | tf_op jit(solution)/shard_map/pallas_call | solution.py:316
  55.8 2.7 %collective-permute-start.8 = (f32[32,2048]{1,0:T(8,128)S(1)}, f32[32,2048]{1,0:T(8,128)S(1)}, u32[]{:S(2)}, u32[]{:S(2)}) collective-permute-start(f32[32,2048]{1,0:T(8,128)S(1)} %get-tuple-element.33), channel_id=1, source_target_pairs={{0,96},{16,112},{32,0},{48,16},{64,32},{80,48},{96,64},{112,80},{1... | collective-permute-start | bytes 786440 | tf_op jit(solution)/shard_map/ppermute | solution.py:376
  58.5 2.5 %collective-permute-start.20 = (bf16[896,128]{1,0:T(8,128)(2,1)S(1)}, bf16[896,128]{1,0:T(8,128)(2,1)S(1)}, u32[]{:S(2)}, u32[]{:S(2)}) collective-permute-start(bf16[896,128]{1,0:T(8,128)(2,1)S(1)} %shard_map.87.pair_ref), channel_id=1, source_target_pairs={{0,1},{1,0},{2,3},{3,2},{4,5},{5,4},{6,7},{7,6},{8,9},{9,8},{10,11... | collective-permute-start | bytes 688136 | tf_op jit(solution)/shard_map/ppermute | solution.py:394
  61.0 1.6 %shard_map.82 = (f32[32,2048]{1,0:T(8,128)S(1)}, bf16[32,2176]{1,0:T(8,128)(2,1)S(1)}) custom-call(bf16[128,2048]{1,0:T(8,128)(2,1)S(1)} %collective-permute-done.10.chip_ref, bf16[128,2048]{1,0:T(8,128)(2,1)S(1)} %collective-permute-done.11.far_ref, bf16[32,2048]{1,0:T(8,128)(2,1)S(1)} %get-tuple-element.27.c0.refs_0_, ...), custom_call_target="tpu_custom_call" | custom-call | tf_op jit(solution)/shard_map/pallas_call | solution.py:316
  62.7 1.7 %collective-permute-start.12 = (bf16[32,2176]{1,0:T(8,128)(2,1)S(1)}, bf16[32,2176]{1,0:T(8,128)(2,1)S(1)}, u32[]{:S(2)}, u32[]{:S(2)}) collective-permute-start(bf16[32,2176]{1,0:T(8,128)(2,1)S(1)} %get-tuple-element.36), channel_id=1, source_target_pairs={{0,16},{16,0},{32,48},{48,32},{64,80},{80,64},{96,112},{112,96},{1... | collective-permute-start | bytes 417800 | tf_op jit(solution)/shard_map/ppermute | solution.py:387
  64.5 3.8 %collective-permute-done.9.d = f32[32,2048]{1,0:T(8,128)S(1)} collective-permute-done((f32[32,2048]{1,0:T(8,128)S(1)}, f32[32,2048]{1,0:T(8,128)S(1)}, u32[]{:S(2)}, u32[]{:S(2)}) %collective-permute-start.9) | collective-permute-done | bytes 262176 | tf_op jit(solution)/shard_map/ppermute | solution.py:376
  68.3 1.1 %collective-permute-done.12.theirs_ref = bf16[32,2176]{1,0:T(8,128)(2,1)S(1)} collective-permute-done((bf16[32,2176]{1,0:T(8,128)(2,1)S(1)}, bf16[32,2176]{1,0:T(8,128)(2,1)S(1)}, u32[]{:S(2)}, u32[]{:S(2)}) %collective-permute-start.12) | collective-permute-done | bytes 139296 | tf_op jit(solution)/shard_map/ppermute | solution.py:387
  69.4 0.9 %shard_map.83 = (f32[32,2048]{1,0:T(8,128)}, f32[32,2048]{1,0:T(8,128)}) custom-call(f32[32,2048]{1,0:T(8,128)S(1)} %shard_map.80.a, f32[32,2048]{1,0:T(8,128)S(1)} %collective-permute-done.7.b, f32[32,2048]{1,0:T(8,128)S(1)} %collective-permute-done.8.c, f32[32,2048]{1,0:T(8,128)S(1)} %collective-permute-done.9.d, ...), custom_call_target="tpu_custom_call" | custom-call | tf_op jit(solution)/shard_map/pallas_call | solution.py:316
  70.3 0.7 shard_map.88
  71.1 2.0 %shard_map.89 = (f32[3,3,96,256]{3,2,1,0:T(8,128)}, f32[1,32]{1,0:T(1,128)}) custom-call(f32[864,256]{1,0:T(8,128)S(1)} %get-tuple-element.44.own_ref, f32[1,32]{1,0:T(1,128)S(1)} %get-tuple-element.45.own_bias_ref, bf16[896,128]{1,0:T(8,128)(2,1)S(1)} %collective-permute-done.20.other_ref), custom_call_target="tpu_custom_call" | custom-call | tf_op jit(solution)/shard_map/pallas_call | solution.py:316
  (27 shorter events, 2.8 us)
Async XLA Ops:
  0.6 6.7 %collective-permute-start = (bf16[32,2048]{1,0:T(8,128)(2,1)}, bf16[32,2048]{1,0:T(8,128)(2,1)S(1)}, u32[]{:S(2)}, u32[]{:S(2)}) collective-permute-start(bf16[32,2048]{1,0:T(8,128)(2,1)} %bitcast.10), channel_id=1, source_target_pairs={{0,16},{16,0},{32,48},{48,32},{64,80},{80,64},{96,112},{112,96},{1... | collective-permute-start | bytes 393224 | tf_op jit(solution)/shard_map/ppermute | solution.py:330
  7.3 13.6 %collective-permute-start.1 = (bf16[64,2048]{1,0:T(8,128)(2,1)S(1)}, bf16[64,2048]{1,0:T(8,128)(2,1)S(1)}, u32[]{:S(2)}, u32[]{:S(2)}) collective-permute-start(bf16[64,2048]{1,0:T(8,128)(2,1)S(1)} %shard_map.76.here_ref), channel_id=1, source_target_pairs={{0,1},{1,0},{2,3},{3,2},{4,5},{5,4},{6,7},{7,6},{8,9},{9,8},{10,11... | collective-permute-start | bytes 786440 | tf_op jit(solution)/shard_map/ppermute | solution.py:343
  9.0 11.9 %collective-permute-start.2 = (bf16[64,2048]{1,0:T(8,128)(2,1)S(1)}, bf16[64,2048]{1,0:T(8,128)(2,1)S(1)}, u32[]{:S(2)}, u32[]{:S(2)}) collective-permute-start(bf16[64,2048]{1,0:T(8,128)(2,1)S(1)} %shard_map.76.here_ref), channel_id=1, source_target_pairs={{0,15},{1,2},{2,1},{3,4},{4,3},{5,6},{6,5},{7,8},{8,7},{9,10},{10,... | collective-permute-start | bytes 786440 | tf_op jit(solution)/shard_map/ppermute | solution.py:344
  10.5 7.1 %collective-permute-start.3 = (bf16[32,2048]{1,0:T(8,128)(2,1)}, bf16[32,2048]{1,0:T(8,128)(2,1)S(1)}, u32[]{:S(2)}, u32[]{:S(2)}) collective-permute-start(bf16[32,2048]{1,0:T(8,128)(2,1)} %bitcast.13), channel_id=1, source_target_pairs={{0,96},{16,112},{32,0},{48,16},{64,32},{80,48},{96,64},{112,80},{1... | collective-permute-start | bytes 393224 | tf_op jit(solution)/shard_map/ppermute | solution.py:331
  14.3 5.6 %collective-permute-start.4 = (bf16[32,2048]{1,0:T(8,128)(2,1)}, bf16[32,2048]{1,0:T(8,128)(2,1)S(1)}, u32[]{:S(2)}, u32[]{:S(2)}) collective-permute-start(bf16[32,2048]{1,0:T(8,128)(2,1)} %bitcast.14), channel_id=1, source_target_pairs={{0,64},{16,80},{32,96},{48,112},{64,0},{80,16},{96,32},{112,48},{1... | collective-permute-start | bytes 393224 | tf_op jit(solution)/shard_map/ppermute | solution.py:331
  14.3 6.6 %collective-permute-start.5 = (bf16[32,2048]{1,0:T(8,128)(2,1)}, bf16[32,2048]{1,0:T(8,128)(2,1)S(1)}, u32[]{:S(2)}, u32[]{:S(2)}) collective-permute-start(bf16[32,2048]{1,0:T(8,128)(2,1)} %bitcast.15), channel_id=1, source_target_pairs={{0,32},{16,48},{32,64},{48,80},{64,96},{80,112},{96,0},{112,16},{1... | collective-permute-start | bytes 393224 | tf_op jit(solution)/shard_map/ppermute | solution.py:331
  22.9 5.7 %collective-permute-start.13 = (f32[872,128]{1,0:T(8,128)S(1)}, f32[872,128]{1,0:T(8,128)S(1)}, u32[]{:S(2)}, u32[]{:S(2)}) collective-permute-start(f32[872,128]{1,0:T(8,128)S(1)} %get-tuple-element.40), channel_id=1, source_target_pairs={{0,1},{1,0},{2,3},{3,2},{4,5},{5,4},{6,7},{7,6},{8,9},{9,8},{10,11... | collective-permute-start | bytes 1339400 | tf_op jit(solution)/shard_map/ppermute | solution.py:355
  27.2 31.3 %collective-permute-start.10 = (bf16[128,2048]{1,0:T(8,128)(2,1)S(1)}, bf16[128,2048]{1,0:T(8,128)(2,1)S(1)}, u32[]{:S(2)}, u32[]{:S(2)}) collective-permute-start(bf16[128,2048]{1,0:T(8,128)(2,1)S(1)} %shard_map.81), channel_id=1, source_target_pairs={{0,1},{1,0},{2,3},{3,2},{4,5},{5,4},{6,7},{7,6},{8,9},{9,8},{10,11... | collective-permute-start | bytes 1572872 | tf_op jit(solution)/shard_map/ppermute | solution.py:364
  29.0 5.2 %collective-permute-start.14 = (bf16[448,128]{1,0:T(8,128)(2,1)S(1)}, bf16[448,128]{1,0:T(8,128)(2,1)S(1)}, u32[]{:S(2)}, u32[]{:S(2)}) collective-permute-start(bf16[448,128]{1,0:T(8,128)(2,1)S(1)} %get-tuple-element.42), channel_id=1, source_target_pairs={{0,2},{1,17},{2,0},{3,19},{4,6},{5,21},{6,4},{7,23},{8,10},{9,25},... | collective-permute-start | bytes 344072 | tf_op jit(solution)/shard_map/ppermute | solution.py:363
  31.5 5.1 %collective-permute-start.15 = (bf16[448,128]{1,0:T(8,128)(2,1)S(1)}, bf16[448,128]{1,0:T(8,128)(2,1)S(1)}, u32[]{:S(2)}, u32[]{:S(2)}) collective-permute-start(bf16[448,128]{1,0:T(8,128)(2,1)S(1)} %get-tuple-element.43), channel_id=1, source_target_pairs={{0,8},{1,25},{2,10},{3,27},{4,12},{5,29},{6,14},{7,31},{8,0},{9,17... | collective-permute-start | bytes 344072 | tf_op jit(solution)/shard_map/ppermute | solution.py:362
  31.9 29.1 %collective-permute-start.11 = (bf16[128,2048]{1,0:T(8,128)(2,1)S(1)}, bf16[128,2048]{1,0:T(8,128)(2,1)S(1)}, u32[]{:S(2)}, u32[]{:S(2)}) collective-permute-start(bf16[128,2048]{1,0:T(8,128)(2,1)S(1)} %shard_map.81), channel_id=1, source_target_pairs={{0,15},{1,2},{2,1},{3,4},{4,3},{5,6},{6,5},{7,8},{8,7},{9,10},{10,... | collective-permute-start | bytes 1572872 | tf_op jit(solution)/shard_map/ppermute | solution.py:365
  37.0 8.9 %collective-permute-start.16 = (bf16[448,128]{1,0:T(8,128)(2,1)S(1)}, bf16[448,128]{1,0:T(8,128)(2,1)S(1)}, u32[]{:S(2)}, u32[]{:S(2)}) collective-permute-start(bf16[448,128]{1,0:T(8,128)(2,1)S(1)} %shard_map.85.own_ref), channel_id=1, source_target_pairs={{0,6},{1,7},{2,0},{3,1},{4,2},{5,3},{6,4},{7,5},{8,14},{9,15},{10,... | collective-permute-start | bytes 344072 | tf_op jit(solution)/shard_map/ppermute | solution.py:368
  38.4 8.7 %collective-permute-start.17 = (bf16[448,128]{1,0:T(8,128)(2,1)S(1)}, bf16[448,128]{1,0:T(8,128)(2,1)S(1)}, u32[]{:S(2)}, u32[]{:S(2)}) collective-permute-start(bf16[448,128]{1,0:T(8,128)(2,1)S(1)} %shard_map.85.own_ref), channel_id=1, source_target_pairs={{0,4},{1,5},{2,6},{3,7},{4,0},{5,1},{6,2},{7,3},{8,12},{9,13},{10,... | collective-permute-start | bytes 344072 | tf_op jit(solution)/shard_map/ppermute | solution.py:368
  39.4 7.9 %collective-permute-start.18 = (bf16[448,128]{1,0:T(8,128)(2,1)S(1)}, bf16[448,128]{1,0:T(8,128)(2,1)S(1)}, u32[]{:S(2)}, u32[]{:S(2)}) collective-permute-start(bf16[448,128]{1,0:T(8,128)(2,1)S(1)} %shard_map.85.own_ref), channel_id=1, source_target_pairs={{0,2},{1,3},{2,4},{3,5},{4,6},{5,7},{6,0},{7,1},{8,10},{9,11},{10,... | collective-permute-start | bytes 344072 | tf_op jit(solution)/shard_map/ppermute | solution.py:368
  46.0 8.3 %collective-permute-start.6 = (bf16[864,128]{1,0:T(8,128)(2,1)S(1)}, bf16[864,128]{1,0:T(8,128)(2,1)S(1)}, u32[]{:S(2)}, u32[]{:S(2)}) collective-permute-start(bf16[864,128]{1,0:T(8,128)(2,1)S(1)} %get-tuple-element.30), channel_id=1, source_target_pairs={{0,16},{16,0},{32,48},{48,32},{64,80},{80,64},{96,112},{112,96},{1... | collective-permute-start | bytes 663560 | tf_op jit(solution)/shard_map/ppermute | solution.py:339
  48.0 10.5 %collective-permute-start.19 = (bf16[448,128]{1,0:T(8,128)(2,1)S(1)}, bf16[448,128]{1,0:T(8,128)(2,1)S(1)}, u32[]{:S(2)}, u32[]{:S(2)}) collective-permute-start(bf16[448,128]{1,0:T(8,128)(2,1)S(1)} %shard_map.86.refs_0_), channel_id=1, source_target_pairs={{0,8},{1,9},{2,10},{3,11},{4,12},{5,13},{6,14},{7,15},{8,0},{9,1},... | collective-permute-start | bytes 344072 | tf_op jit(solution)/shard_map/ppermute | solution.py:392
  54.3 10.1 %copy-start = (bf16[32]{0:T(256)(128)(2,1)S(1)}, bf16[32]{0:T(256)(128)(2,1)}, u32[]{:S(2)}) copy-start(bf16[32]{0:T(256)(128)(2,1)} %param.6) | copy-start | bytes 196
  55.7 8.8 %collective-permute-start.7 = (f32[32,2048]{1,0:T(8,128)S(1)}, f32[32,2048]{1,0:T(8,128)S(1)}, u32[]{:S(2)}, u32[]{:S(2)}) collective-permute-start(f32[32,2048]{1,0:T(8,128)S(1)} %get-tuple-element.32), channel_id=1, source_target_pairs={{0,32},{16,48},{32,64},{48,80},{64,96},{80,112},{96,0},{112,16},{1... | collective-permute-start | bytes 786440 | tf_op jit(solution)/shard_map/ppermute | solution.py:376
  55.8 8.7 %collective-permute-start.8 = (f32[32,2048]{1,0:T(8,128)S(1)}, f32[32,2048]{1,0:T(8,128)S(1)}, u32[]{:S(2)}, u32[]{:S(2)}) collective-permute-start(f32[32,2048]{1,0:T(8,128)S(1)} %get-tuple-element.33), channel_id=1, source_target_pairs={{0,96},{16,112},{32,0},{48,16},{64,32},{80,48},{96,64},{112,80},{1... | collective-permute-start | bytes 786440 | tf_op jit(solution)/shard_map/ppermute | solution.py:376
  58.5 9.9 %collective-permute-start.9 = (f32[32,2048]{1,0:T(8,128)S(1)}, f32[32,2048]{1,0:T(8,128)S(1)}, u32[]{:S(2)}, u32[]{:S(2)}) collective-permute-start(f32[32,2048]{1,0:T(8,128)S(1)} %get-tuple-element.34), channel_id=1, source_target_pairs={{0,64},{16,80},{32,96},{48,112},{64,0},{80,16},{96,32},{112,48},{1... | collective-permute-start | bytes 786440 | tf_op jit(solution)/shard_map/ppermute | solution.py:376
  58.5 12.5 %collective-permute-start.20 = (bf16[896,128]{1,0:T(8,128)(2,1)S(1)}, bf16[896,128]{1,0:T(8,128)(2,1)S(1)}, u32[]{:S(2)}, u32[]{:S(2)}) collective-permute-start(bf16[896,128]{1,0:T(8,128)(2,1)S(1)} %shard_map.87.pair_ref), channel_id=1, source_target_pairs={{0,1},{1,0},{2,3},{3,2},{4,5},{5,4},{6,7},{7,6},{8,9},{9,8},{10,11... | collective-permute-start | bytes 688136 | tf_op jit(solution)/shard_map/ppermute | solution.py:394
  62.7 6.8 %collective-permute-start.12 = (bf16[32,2176]{1,0:T(8,128)(2,1)S(1)}, bf16[32,2176]{1,0:T(8,128)(2,1)S(1)}, u32[]{:S(2)}, u32[]{:S(2)}) collective-permute-start(bf16[32,2176]{1,0:T(8,128)(2,1)S(1)} %get-tuple-element.36), channel_id=1, source_target_pairs={{0,16},{16,0},{32,48},{48,32},{64,80},{80,64},{96,112},{112,96},{1... | collective-permute-start | bytes 417800 | tf_op jit(solution)/shard_map/ppermute | solution.py:387

commit v6 on v5

--- a/solution.py
+++ b/solution.py
@@ -29,6 +29,8 @@
     return [(f, ((f // 2 + step) % 4) * 2 + f % 2) for f in range(8)]
 
 
+Z_FIRST = [(f, f ^ 2) for f in range(8)]
+Z_SECOND = [(f, f ^ 6) for f in range(8)]
 ACROSS = [(f, f ^ 1) for f in range(8)]
 BESIDE = [(s, (s + 1) % 16 if s & 1 else (s - 1) % 16) for s in range(16)]
 CORE = [(s, s ^ 1) for s in range(16)]
@@ -84,7 +86,7 @@
         at += ref.shape[0]
 
 
-def forward_kernel(xs_ref, wa_ref, wb_ref, o0, o1, o2, o3):
+def forward_kernel(xs_ref, wa_ref, wb_ref, mine_ref, first_ref, send_ref):
     rhs = jnp.concatenate([xs_ref[0, :TAPS, :], xs_ref[1, :TAPS, :]], axis=0)
     parts = []
     for kh in range(3):
@@ -101,8 +103,11 @@
         + jnp.where(lane < WIDE, 0.0, pltpu.roll(parts[0], WIDE, 1))
         + jnp.where(lane >= PLANE - WIDE, 0.0, pltpu.roll(parts[2], PLANE - WIDE, 1))
     )
-    for r, ref in enumerate((o0, o1, o2, o3)):
-        ref[...] = total[r * 32 : r * 32 + 32]
+    even = ((lax.axis_index("filt") // 2) & 1) == 0
+    near, across, far = (total[r * 32 : r * 32 + 32] for r in (1, 2, 3))
+    mine_ref[...] = total[:32]
+    first_ref[...] = jnp.where(even, near, far)
+    write_rows(send_ref, jnp.concatenate([jnp.where(even, far, near), across], axis=0))
 
 
 def row_shifts(wide):
@@ -187,8 +192,7 @@
         if h == 0:
             mine_ref[...] = part
         else:
-            theirs_ref[:, :PLANE], scale = encode(part)
-            theirs_ref[:, PLANE:] = jnp.broadcast_to(scale, (OWN, 128)).astype(BF)
+            write_rows(theirs_ref, part)
 
 
 def encode(wide):
@@ -215,9 +219,22 @@
     out_ref[PIECE:, :] = tail.astype(BF)
 
 
-def read_coded(ref, at=0):
-    tail = ref[at + PIECE : at + CODED, :].astype(F32)
-    return decode(ref[at : at + PIECE, :], tail[0:1, 0:1]), tail[1:2, :] + tail[2:3, :]
+def read_tail(tail):
+    return tail[1:2, :] + tail[2:3, :]
+
+
+def read_coded(ref):
+    tail = ref[PIECE:CODED, :].astype(F32)
+    return decode(ref[:PIECE, :], tail[0:1, 0:1]), read_tail(tail)
+
+
+def write_rows(out_ref, wide):
+    out_ref[:, :PLANE], scale = encode(wide)
+    out_ref[:, PLANE:] = jnp.broadcast_to(scale, (wide.shape[0], 128)).astype(BF)
+
+
+def read_rows(coded):
+    return decode(coded[:, :PLANE], coded[0:1, PLANE : PLANE + 1].astype(F32))
 
 
 def split_xlo_kernel(keep_ref, got_ref, send_out, cross_out, keep_out):
@@ -250,15 +267,6 @@
     write_coded(out_ref, pltpu.roll(wide * factor, z * 32, 1), bias * factor)
 
 
-def place(pair_ref, out_ref):
-    xlo = lax.axis_index("space") // 8
-    for rx in range(2):
-        to = pl.multiple_of((xlo ^ rx) * PIECE, 8)
-        wide, bias = read_coded(pair_ref, rx * CODED)
-        out_ref[pl.ds(to, PIECE), :] = wide
-    return bias[:, :OWN]
-
-
 def side_of(swap):
     return (lax.axis_index("filt") ^ lax.axis_index("space") ^ swap) & 1
 
@@ -271,27 +279,50 @@
     return jnp.where(low, first, second), jnp.where(low, third, fourth)
 
 
-def decode_kernel(pair_ref, out_ref, bias_ref, half_ref):
-    bias_ref[...] = place(pair_ref, half_ref)
-    out_ref[:, :128], out_ref[:, 128:] = spread(half_ref[...], side_of(0))
-
-
-def assemble_kernel(own_ref, own_bias_ref, other_ref, grad_hbm, bias_ref, half_ref, grad_ref, sems):
-    bias = place(other_ref, half_ref)
+def decode_kernel(own_ref, out_ref):
+    out_ref[:, :128], out_ref[:, 128:] = spread(read_coded(own_ref)[0], side_of(0))
+
+
+def write_half(turn, own_ref, got_ref, grad_hbm, rows_ref, sems):
+    wide, bias = read_coded(got_ref)
+    side = side_of(1)
+    theirs = ((lanes((PIECE, 128)) >> 5) & 1) == side
+    for t, part in enumerate(spread(wide, side)):
+        cols = slice(t * 128, t * 128 + 128)
+        rows_ref[:, cols] = jnp.where(theirs, part, own_ref[:, cols])
+    half = (lax.axis_index("space") // 8) ^ turn
+    spans = []
+    for j in range(4):
+        block = j + 5 * half
+        to = lax.rem(block, 3) * 3 + lax.div(block, 3)
+        spans.append((half * 48 + j * 96, 96, to, 0))
+    spans.append(((1 - half) * 384, 48, 4, half * 48))
+    copies = [
+        pltpu.make_async_copy(
+            rows_ref.at[pl.ds(pl.multiple_of(at, 16), size), :],
+            grad_hbm.at[to, pl.ds(row if isinstance(row, int) else pl.multiple_of(row, 16), size), :],
+            sems.at[i],
+        )
+        for i, (at, size, to, row) in enumerate(spans)
+    ]
+    for copy in copies:
+        copy.start()
+    return bias[:, :OWN], copies
+
+
+def first_kernel(own_ref, piece_ref, got_ref, grad_hbm, bias_hbm, rows_ref, sems, bias_ref, bias_sem):
+    bias, copies = write_half(0, own_ref, got_ref, grad_hbm, rows_ref, sems)
     core = lax.axis_index("space") & 1
-    bias_ref[...] = jnp.where(core == 0, own_bias_ref[...], bias)
-    side = side_of(1)
-    theirs = ((lanes((TAPS, 128)) >> 5) & 1) == side
-    copies = []
-    for kh in range(3):
-        rows = slice(kh * TAPS, kh * TAPS + TAPS)
-        for t, part in enumerate(spread(half_ref[rows, :], side)):
-            cols = slice(t * 128, t * 128 + 128)
-            whole = jnp.where(theirs, part, own_ref[rows, cols])
-            grad_ref[kh, :, :, cols] = whole.reshape(3, 96, 128)
-        copies.append(pltpu.make_async_copy(grad_ref.at[kh], grad_hbm.at[:, kh], sems.at[kh]))
-        copies[-1].start()
+    own_bias = read_tail(piece_ref[PIECE:CODED, :].astype(F32))[:, :OWN]
+    bias_ref[...] = jnp.where(core == 0, own_bias, bias)
+    copies.append(pltpu.make_async_copy(bias_ref, bias_hbm, bias_sem))
+    copies[-1].start()
     for copy in copies:
+        copy.wait()
+
+
+def second_kernel(own_ref, got_ref, _, grad_hbm, rows_ref, sems):
+    for copy in write_half(1, own_ref, got_ref, grad_hbm, rows_ref, sems)[1]:
         copy.wait()
 
 
@@ -302,22 +333,32 @@
     out[...] = jnp.sum(wide, axis=1, keepdims=True)
 
 
-def biased_kernel(ref, bias_ref, out):
-    out[...] = ref[...] + bias_ref[...]
-
-
-def sums_kernel(a, b, c, d, mine_ref, theirs_ref, out, grad):
-    out[...] = (a[...] + b[...]) + (c[...] + d[...])
-    scale = theirs_ref[0:1, PLANE : PLANE + 1].astype(F32)
-    grad[...] = mine_ref[...] + decode(theirs_ref[:, :PLANE], scale)
-
-
-def call(kernel, outs, *args, scratch=(), space=VM, out_space=VM):
+def halve_kernel(mine_ref, first_ref, got_ref, sum_ref, send_ref):
+    got = read_rows(got_ref[...])
+    sum_ref[...] = mine_ref[...] + got[:OWN]
+    write_rows(send_ref, first_ref[...] + got[OWN:])
+
+
+def sums_kernel(mine_ref, got_ref, bias_ref, near_ref, theirs_ref, out_hbm, grad_hbm, out_ref, grad_ref, sems):
+    copies = [
+        pltpu.make_async_copy(out_ref, out_hbm, sems.at[0]),
+        pltpu.make_async_copy(grad_ref, grad_hbm, sems.at[1]),
+    ]
+    out_ref[...] = mine_ref[...] + read_rows(got_ref[...]) + bias_ref[...]
+    copies[0].start()
+    grad_ref[...] = near_ref[...] + read_rows(theirs_ref[...])
+    copies[1].start()
+    for copy in copies:
+        copy.wait()
+
+
+def call(kernel, outs, *args, scratch=(), space=VM, out_space=VM, over=None):
     return pl.pallas_call(
         kernel,
         out_shape=[jax.ShapeDtypeStruct(s, d) for s, d in outs],
-        in_specs=[space] * len(args),
-        out_specs=[out_space] + [VM] * (len(outs) - 1),
+        in_specs=[space if i != over else out_space for i in range(len(args))],
+        input_output_aliases={} if over is None else {over: 0},
+        out_specs=[out_space] * len(outs),
         scratch_shapes=list(scratch),
         compiler_params=PARAMS,
     )(*args)
@@ -353,7 +394,18 @@
         scratch=[pltpu.VMEM((384, PLANE), BF)],
     )
     r_core = lax.ppermute(send, "space", CORE)
-    outs = call(forward_kernel, [((32, PLANE), F32)] * 4, xs, w_mine, w_other)
+    o_mine, o_first, o_send = call(
+        forward_kernel,
+        [((OWN, PLANE), F32)] * 2 + [((2 * OWN, PLANE + 128), BF)],
+        xs,
+        w_mine,
+        w_other,
+    )
+    o_got = lax.ppermute(o_send, "filt", Z_SECOND)
+    o_sum, o_send = call(
+        halve_kernel, [((OWN, PLANE), F32), ((OWN, PLANE + 128), BF)], o_mine, o_first, o_got
+    )
+    o_got = lax.ppermute(o_send, "filt", Z_FIRST)
     (c_here,) = call(join_kernel, [((128, PLANE), BF)], *cots)
 
     r_send, r_cross, r_keep = call(
@@ -372,8 +424,7 @@
     )
 
     (wide_bias,) = call(bias_kernel, [((OWN, 1), F32)], bias.reshape(1, OWN))
-    (biased,) = call(biased_kernel, [((OWN, PLANE), F32)], outs[0], wide_bias)
-    sums = [lax.ppermute(outs[r], "filt", along_z(r)) for r in (1, 3, 2)]
+
     g_mine, g_theirs = call(
         input_grad_kernel,
         [((OWN, PLANE), F32), ((OWN, PLANE + 128), BF)],
@@ -385,31 +436,39 @@
         scratch=[pltpu.VMEM((9 * 128, PLANE), BF)],
     )
     g_other = lax.ppermute(g_theirs, "filt", ACROSS)
+    wide = [((OWN, PLANE), F32)] * 2
     output, grad_inputs = call(
-        sums_kernel, [((OWN, PLANE), F32)] * 2, biased, *sums, g_mine, g_other
+        sums_kernel,
+        wide,
+        o_sum,
+        o_got,
+        wide_bias,
+        g_mine,
+        g_other,
+        scratch=[pltpu.VMEM(*v) for v in wide] + [pltpu.SemaphoreType.DMA((2,))],
+        out_space=pl.BlockSpec(memory_space=pltpu.HBM),
     )
 
     piece_far = lax.ppermute(piece, "space", XLO)
-    (pair,) = call(join_kernel, [((2 * CODED, 128), BF)], piece, piece_far)
-    other = lax.ppermute(pair, "space", CORE)
-    mine, mine_bias = call(
-        decode_kernel,
-        [((HALF, 256), F32), ((1, OWN), F32)],
-        pair,
-        scratch=[pltpu.VMEM((HALF, 128), F32)],
-    )
-    grad_weight, grad_bias = call(
-        assemble_kernel,
-        [((3, 3, 96, 256), F32), ((1, OWN), F32)],
+    got_near = lax.ppermute(piece, "space", CORE)
+    got_far = lax.ppermute(piece_far, "space", CORE)
+    decoded = [((PIECE, 256), F32)]
+    (mine,) = call(decode_kernel, decoded, piece)
+    (mine_far,) = call(decode_kernel, decoded, piece_far)
+    grad = ((9, 96, 256), F32)
+    scratch = [pltpu.VMEM((PIECE, 256), F32), pltpu.SemaphoreType.DMA((5,))]
+    hbm = pl.BlockSpec(memory_space=pltpu.HBM)
+    half_done, grad_bias = call(
+        first_kernel,
+        [grad, ((1, OWN), F32)],
         mine,
-        mine_bias,
-        other,
-        scratch=[
-            pltpu.VMEM((HALF, 128), F32),
-            pltpu.VMEM((3, 3, 96, 256), F32),
-            pltpu.SemaphoreType.DMA((3,)),
-        ],
-        out_space=pl.BlockSpec(memory_space=pltpu.HBM),
+        piece,
+        got_near,
+        scratch=scratch + [pltpu.VMEM((1, OWN), F32), pltpu.SemaphoreType.DMA],
+        out_space=hbm,
+    )
+    (grad_weight,) = call(
+        second_kernel, [grad], mine_far, got_far, half_done, scratch=scratch, out_space=hbm, over=2
     )
     return (
         output[None],

time: 74.1 us -> 72 us (0.972)
  waiting for transfers between devices: 29.8 us -> 22.4 us
  starting transfers between devices: 30.9 us -> 35.5 us
  Pallas kernels: 11.5 us -> 12.5 us
    ppermute x3, starting transfers between devices: 2.84 us -> 8.8 us  [step(): y1, y3, y2 = (lax.ppermute(mine_y, 'space', along_y(-r)) for r in (1, 3, 2))]
    ppermute x1, waiting for transfers between devices: 4.97 us -> 0.01 us  [step(): w_other = lax.ppermute(w_theirs, 'filt', ACROSS)]
    ppermute x4, waiting for transfers between devices: 3.81 us -> 0.32 us  [the longest x1 0.32 us: step(): o_got = lax.ppermute(o_send, 'filt', Z_FIRST)]
    ppermute x4, starting transfers between devices: 5.25 us -> 2.21 us  [the longest x1 1.13 us: step(): got_near = lax.ppermute(piece, 'space', CORE)]
    ppermute x1, waiting for transfers between devices: 2.46 us -> 0.01 us  [step(): r_far = lax.ppermute(r_send, ('filt', 'space'), crossing(8, 8))]
    ppermute x1, waiting for transfers between devices: 2.25 us -> 4.57 us  [step(): r_near = lax.ppermute(r_cross, ('filt', 'space'), crossing(0, 2))]
    ppermute x1, starting transfers between devices: 2.54 us -> 0.31 us  [step(): r_near = lax.ppermute(r_cross, ('filt', 'space'), crossing(0, 2))]
    ppermute x1, starting transfers between devices: 0.44 us -> 2.47 us  [step(): r_far = lax.ppermute(r_send, ('filt', 'space'), crossing(8, 8))]
  transfers between devices with their start and end apart: 21 -> 21, of which waited for: 12 -> 9; matrix products, arithmetic and copies ran while one was open for 0% -> 0% of each run, Pallas kernels for 10% -> 13%
where the time goes in v6:
time: 72 us; the launch traced here: 71.3 us
  starting transfers between devices  35.5 us (49%)
  waiting for transfers between devices  22.4 us (31%)
  Pallas kernels  12.5 us (17%)
  between operations  0.93 us (1%)
    pallas_call x16, Pallas kernels, call(): pl.pallas_call(kernel, out_shape=[jax.ShapeDtypeStruct(s, d) for s, d in...  12.5 us
    ppermute x3, starting transfers between devices, step(): y1, y3, y2 = (lax.ppermute(mine_y, 'space', along_y(-r)) for r in (1, 3, 2))  8.8 us
    ppermute x3, waiting for transfers between devices, step(): y1, y3, y2 = (lax.ppermute(mine_y, 'space', along_y(-r)) for r in (1, 3, 2))  7.53 us
    ppermute x3, waiting for transfers between devices, step(): c1, c3, c2 = (lax.ppermute(c_own, 'filt', along_z(-r)) for r in (1, 3, 2))  5.94 us
    ppermute x1, waiting for transfers between devices, step(): r_near = lax.ppermute(r_cross, ('filt', 'space'), crossing(0, 2))  4.57 us
    ppermute x3, starting transfers between devices, step(): c1, c3, c2 = (lax.ppermute(c_own, 'filt', along_z(-r)) for r in (1, 3, 2))  4.46 us
    ppermute x1, starting transfers between devices, step(): r_core = lax.ppermute(send, 'space', CORE)  4.29 us
    ppermute x1, starting transfers between devices, step(): x_other = lax.ppermute(x_own, 'filt', ACROSS)  3.64 us
  transfers between devices with their start and end apart: 21, of which 9 were waited for; matrix products, arithmetic and copies ran while one was open for 0% of the time, Pallas kernels for 13%

profile of v6, /device:TPU:1, one launch (start us, length us, event | category | flops | bytes accessed | tf_op | source)
XLA Modules:
  0.0 71.3 jit_solution(15569032838986542691)
XLA Ops:
  0.6 3.6 %collective-permute-start = (bf16[32,2048]{1,0:T(8,128)(2,1)}, bf16[32,2048]{1,0:T(8,128)(2,1)S(1)}, u32[]{:S(2)}, u32[]{:S(2)}) collective-permute-start(bf16[32,2048]{1,0:T(8,128)(2,1)} %bitcast.11), channel_id=1, source_target_pairs={{0,16},{16,0},{32,48},{48,32},{64,80},{80,64},{96,112},{112,96},{1... | collective-permute-start | bytes 393224 | tf_op jit(solution)/shard_map/ppermute | solution.py:371
  4.3 1.4 %shard_map.75 = (bf16[864,128]{1,0:T(8,128)(2,1)S(1)}, bf16[864,128]{1,0:T(8,128)(2,1)S(1)}, bf16[32,2048]{1,0:T(8,128)(2,1)S(1)}, bf16[32,2048]{1,0:T(8,128)(2,1)S(1)}) custom-call(bf16[864,256]{1,0:T(8,128)(2,1)} %bitcast.10, bf16[32,2048]{1,0:T(8,128)(2,1)} %bitcast.12, bf16[32,2048]{1,0:T(8,128)(2,1)} %bitcast.13), custom_call_target="tpu_custom_call" | custom-call | tf_op jit(solution)/shard_map/pallas_call | solution.py:356
  5.7 1.6 %collective-permute-done.refs_1_ = bf16[32,2048]{1,0:T(8,128)(2,1)S(1)} collective-permute-done((bf16[32,2048]{1,0:T(8,128)(2,1)}, bf16[32,2048]{1,0:T(8,128)(2,1)S(1)}, u32[]{:S(2)}, u32[]{:S(2)}) %collective-permute-start) | collective-permute-done | bytes 131104 | tf_op jit(solution)/shard_map/ppermute | solution.py:371
  7.3 1.7 %collective-permute-start.1 = (bf16[64,2048]{1,0:T(8,128)(2,1)S(1)}, bf16[64,2048]{1,0:T(8,128)(2,1)S(1)}, u32[]{:S(2)}, u32[]{:S(2)}) collective-permute-start(bf16[64,2048]{1,0:T(8,128)(2,1)S(1)} %shard_map.76.here_ref), channel_id=1, source_target_pairs={{0,1},{1,0},{2,3},{3,2},{4,5},{5,4},{6,7},{7,6},{8,9},{9,8},{10,11... | collective-permute-start | bytes 786440 | tf_op jit(solution)/shard_map/ppermute | solution.py:384
  9.0 1.5 %collective-permute-start.2 = (bf16[64,2048]{1,0:T(8,128)(2,1)S(1)}, bf16[64,2048]{1,0:T(8,128)(2,1)S(1)}, u32[]{:S(2)}, u32[]{:S(2)}) collective-permute-start(bf16[64,2048]{1,0:T(8,128)(2,1)S(1)} %shard_map.76.here_ref), channel_id=1, source_target_pairs={{0,15},{1,2},{2,1},{3,4},{4,3},{5,6},{6,5},{7,8},{8,7},{9,10},{10,... | collective-permute-start | bytes 786440 | tf_op jit(solution)/shard_map/ppermute | solution.py:385
  10.5 3.8 %collective-permute-start.3 = (bf16[32,2048]{1,0:T(8,128)(2,1)}, bf16[32,2048]{1,0:T(8,128)(2,1)S(1)}, u32[]{:S(2)}, u32[]{:S(2)}) collective-permute-start(bf16[32,2048]{1,0:T(8,128)(2,1)} %bitcast.14), channel_id=1, source_target_pairs={{0,96},{16,112},{32,0},{48,16},{64,32},{80,48},{96,64},{112,80},{1... | collective-permute-start | bytes 393224 | tf_op jit(solution)/shard_map/ppermute | solution.py:372
  14.3 0.7 collective-permute-start.5
  15.0 2.6 %collective-permute-done.3.c1.refs_1_ = bf16[32,2048]{1,0:T(8,128)(2,1)S(1)} collective-permute-done((bf16[32,2048]{1,0:T(8,128)(2,1)}, bf16[32,2048]{1,0:T(8,128)(2,1)S(1)}, u32[]{:S(2)}, u32[]{:S(2)}) %collective-permute-start.3) | collective-permute-done | bytes 131104 | tf_op jit(solution)/shard_map/ppermute | solution.py:372
  17.6 2.3 %collective-permute-done.4.c2.refs_2_ = bf16[32,2048]{1,0:T(8,128)(2,1)S(1)} collective-permute-done((bf16[32,2048]{1,0:T(8,128)(2,1)}, bf16[32,2048]{1,0:T(8,128)(2,1)S(1)}, u32[]{:S(2)}, u32[]{:S(2)}) %collective-permute-start.4) | collective-permute-done | bytes 131104 | tf_op jit(solution)/shard_map/ppermute | solution.py:372
  19.9 1.0 %collective-permute-done.5.c3.refs_3_ = bf16[32,2048]{1,0:T(8,128)(2,1)S(1)} collective-permute-done((bf16[32,2048]{1,0:T(8,128)(2,1)}, bf16[32,2048]{1,0:T(8,128)(2,1)S(1)}, u32[]{:S(2)}, u32[]{:S(2)}) %collective-permute-start.5) | collective-permute-done | bytes 131104 | tf_op jit(solution)/shard_map/ppermute | solution.py:372
  20.9 1.9 %shard_map.77 = (bf16[2,304,2048]{2,1,0:T(8,128)(2,1)S(1)}, f32[872,128]{1,0:T(8,128)S(1)}, f32[872,128]{1,0:T(8,128)S(1)}) custom-call(bf16[64,2048]{1,0:T(8,128)(2,1)S(1)} %collective-permute-done.1.chip_ref, bf16[64,2048]{1,0:T(8,128)(2,1)S(1)} %shard_map.76.here_ref, bf16[64,2048]{1,0:T(8,128)(2,1)S(1)} %collective-permute-done.2.far_ref, ...), custom_call_target="tpu_custom_call" | custom-call | tf_op jit(solution)/shard_map/pallas_call | solution.py:356
  22.9 4.3 %collective-permute-start.12 = (f32[872,128]{1,0:T(8,128)S(1)}, f32[872,128]{1,0:T(8,128)S(1)}, u32[]{:S(2)}, u32[]{:S(2)}) collective-permute-start(f32[872,128]{1,0:T(8,128)S(1)} %get-tuple-element.40), channel_id=1, source_target_pairs={{0,1},{1,0},{2,3},{3,2},{4,5},{5,4},{6,7},{7,6},{8,9},{9,8},{10,11... | collective-permute-start | bytes 1339400 | tf_op jit(solution)/shard_map/ppermute | solution.py:396
  27.3 1.0 %collective-permute-start.10 = (bf16[128,2048]{1,0:T(8,128)(2,1)S(1)}, bf16[128,2048]{1,0:T(8,128)(2,1)S(1)}, u32[]{:S(2)}, u32[]{:S(2)}) collective-permute-start(bf16[128,2048]{1,0:T(8,128)(2,1)S(1)} %shard_map.81), channel_id=1, source_target_pairs={{0,15},{1,2},{2,1},{3,4},{4,3},{5,6},{6,5},{7,8},{8,7},{9,10},{10,... | collective-permute-start | bytes 1572872 | tf_op jit(solution)/shard_map/ppermute | solution.py:417
  28.3 2.7 %collective-permute-start.6 = (bf16[864,128]{1,0:T(8,128)(2,1)S(1)}, bf16[864,128]{1,0:T(8,128)(2,1)S(1)}, u32[]{:S(2)}, u32[]{:S(2)}) collective-permute-start(bf16[864,128]{1,0:T(8,128)(2,1)S(1)} %get-tuple-element.29), channel_id=1, source_target_pairs={{0,16},{16,0},{32,48},{48,32},{64,80},{80,64},{96,112},{112,96},{1... | collective-permute-start | bytes 663560 | tf_op jit(solution)/shard_map/ppermute | solution.py:380
  31.7 2.5 %collective-permute-start.14 = (bf16[448,128]{1,0:T(8,128)(2,1)S(1)}, bf16[448,128]{1,0:T(8,128)(2,1)S(1)}, u32[]{:S(2)}, u32[]{:S(2)}) collective-permute-start(bf16[448,128]{1,0:T(8,128)(2,1)S(1)} %get-tuple-element.43), channel_id=1, source_target_pairs={{0,8},{1,25},{2,10},{3,27},{4,12},{5,29},{6,14},{7,31},{8,0},{9,17... | collective-permute-start | bytes 344072 | tf_op jit(solution)/shard_map/ppermute | solution.py:414
  34.2 4.6 %collective-permute-done.13.near_ref = bf16[448,128]{1,0:T(8,128)(2,1)S(1)} collective-permute-done((bf16[448,128]{1,0:T(8,128)(2,1)S(1)}, bf16[448,128]{1,0:T(8,128)(2,1)S(1)}, u32[]{:S(2)}, u32[]{:S(2)}) %collective-permute-start.13) | collective-permute-done | bytes 114720 | tf_op jit(solution)/shard_map/ppermute | solution.py:415
  39.1 8.2 %collective-permute-start.15 = (bf16[448,128]{1,0:T(8,128)(2,1)S(1)}, bf16[448,128]{1,0:T(8,128)(2,1)S(1)}, u32[]{:S(2)}, u32[]{:S(2)}) collective-permute-start(bf16[448,128]{1,0:T(8,128)(2,1)S(1)} %shard_map.85.own_ref), channel_id=1, source_target_pairs={{0,6},{1,7},{2,0},{3,1},{4,2},{5,3},{6,4},{7,5},{8,14},{9,15},{10,... | collective-permute-start | bytes 344072 | tf_op jit(solution)/shard_map/ppermute | solution.py:420
  47.3 1.7 %shard_map.78 = (f32[32,2048]{1,0:T(8,128)S(1)}, f32[32,2048]{1,0:T(8,128)S(1)}, bf16[64,2176]{1,0:T(8,128)(2,1)S(1)}) custom-call(bf16[2,304,2048]{2,1,0:T(8,128)(2,1)S(1)} %get-tuple-element.27.xs_ref, bf16[864,128]{1,0:T(8,128)(2,1)S(1)} %get-tuple-element.28.wa_ref, bf16[864,128]{1,0:T(8,128)(2,1)S(1)} %collective-permute-done.6.wb_ref), custom_call_target="tpu_custom_call" | custom-call | tf_op jit(solution)/shard_map/pallas_call | solution.py:356
  49.0 0.7 collective-permute-start.7
  49.8 0.6 collective-permute-start.17
  50.4 5.0 %collective-permute-done.16.y2_ref = bf16[448,128]{1,0:T(8,128)(2,1)S(1)} collective-permute-done((bf16[448,128]{1,0:T(8,128)(2,1)S(1)}, bf16[448,128]{1,0:T(8,128)(2,1)S(1)}, u32[]{:S(2)}, u32[]{:S(2)}) %collective-permute-start.16) | collective-permute-done | bytes 114720 | tf_op jit(solution)/shard_map/ppermute | solution.py:420
  55.3 2.6 %collective-permute-done.17.y3_ref = bf16[448,128]{1,0:T(8,128)(2,1)S(1)} collective-permute-done((bf16[448,128]{1,0:T(8,128)(2,1)S(1)}, bf16[448,128]{1,0:T(8,128)(2,1)S(1)}, u32[]{:S(2)}, u32[]{:S(2)}) %collective-permute-start.17) | collective-permute-done | bytes 114720 | tf_op jit(solution)/shard_map/ppermute | solution.py:420
  57.9 0.6 shard_map.86.own_ref.piece_ref
  58.5 0.4 collective-permute-start.18
  58.9 1.6 %shard_map.82 = (f32[32,2048]{1,0:T(8,128)S(1)}, bf16[32,2176]{1,0:T(8,128)(2,1)S(1)}) custom-call(bf16[128,2048]{1,0:T(8,128)(2,1)S(1)} %collective-permute-done.9.chip_ref, bf16[128,2048]{1,0:T(8,128)(2,1)S(1)} %collective-permute-done.10.far_ref, bf16[32,2048]{1,0:T(8,128)(2,1)S(1)} %get-tuple-element.26.c0.refs_0_, ...), custom_call_target="tpu_custom_call" | custom-call | tf_op jit(solution)/shard_map/pallas_call | solution.py:356
  60.6 1.9 %collective-permute-start.11 = (bf16[32,2176]{1,0:T(8,128)(2,1)S(1)}, bf16[32,2176]{1,0:T(8,128)(2,1)S(1)}, u32[]{:S(2)}, u32[]{:S(2)}) collective-permute-start(bf16[32,2176]{1,0:T(8,128)(2,1)S(1)} %get-tuple-element.36), channel_id=1, source_target_pairs={{0,16},{16,0},{32,48},{48,32},{64,80},{80,64},{96,112},{112,96},{1... | collective-permute-start | bytes 417800 | tf_op jit(solution)/shard_map/ppermute | solution.py:438
  62.4 0.4 shard_map.79
  62.9 1.1 %collective-permute-start.20 = (bf16[448,128]{1,0:T(8,128)(2,1)S(1)}, bf16[448,128]{1,0:T(8,128)(2,1)S(1)}, u32[]{:S(2)}, u32[]{:S(2)}) collective-permute-start(bf16[448,128]{1,0:T(8,128)(2,1)S(1)} %shard_map.86.own_ref.piece_ref), channel_id=1, source_target_pairs={{0,1},{1,0},{2,3},{3,2},{4,5},{5,4},{6,7},{7,6},{8,9},{9,8},{10,11... | collective-permute-start | bytes 344072 | tf_op jit(solution)/shard_map/ppermute | solution.py:453
  64.4 2.4 %collective-permute-done.11.theirs_ref = bf16[32,2176]{1,0:T(8,128)(2,1)S(1)} collective-permute-done((bf16[32,2176]{1,0:T(8,128)(2,1)S(1)}, bf16[32,2176]{1,0:T(8,128)(2,1)S(1)}, u32[]{:S(2)}, u32[]{:S(2)}) %collective-permute-start.11) | collective-permute-done | bytes 139296 | tf_op jit(solution)/shard_map/ppermute | solution.py:438
  67.1 1.0 %shard_map.83 = (f32[32,2048]{1,0:T(8,128)}, f32[32,2048]{1,0:T(8,128)}) custom-call(f32[32,2048]{1,0:T(8,128)S(1)} %get-tuple-element.33.mine_ref, bf16[32,2176]{1,0:T(8,128)(2,1)S(1)} %collective-permute-done.8.got_ref, f32[32,1]{1,0:T(8,128)S(1)} %shard_map.80.bias_ref, f32[32,2048]{1,0:T(8,128)S(1)} %get-tuple-element.35.near_ref, ...), custom_call_target="tpu_custom_call" | custom-call | tf_op jit(solution)/shard_map/pallas_call | solution.py:356
  68.8 1.1 %shard_map.89 = (f32[9,96,256]{2,1,0:T(8,128)}, f32[1,32]{1,0:T(1,128)}) custom-call(f32[432,256]{1,0:T(8,128)S(1)} %shard_map.88.own_ref, bf16[448,128]{1,0:T(8,128)(2,1)S(1)} %shard_map.86.own_ref.piece_ref, bf16[448,128]{1,0:T(8,128)(2,1)S(1)} %collective-permute-done.20.got_ref), custom_call_target="tpu_custom_call" | custom-call | tf_op jit(solution)/shard_map/pallas_call | solution.py:356
  70.0 1.1 %shard_map.90 = f32[9,96,256]{2,1,0:T(8,128)} custom-call(f32[432,256]{1,0:T(8,128)S(1)} %shard_map.87.own_ref, bf16[448,128]{1,0:T(8,128)(2,1)S(1)} %collective-permute-done.19.got_ref, f32[9,96,256]{2,1,0:T(8,128)} %get-tuple-element.44._), custom_call_target="tpu_custom_call", output_to_operand_aliasing={{}: (2, {})} | custom-call | tf_op jit(solution)/shard_map/pallas_call | solution.py:356
  (28 shorter events, 2.6 us)
Async XLA Ops:
  0.6 6.7 %collective-permute-start = (bf16[32,2048]{1,0:T(8,128)(2,1)}, bf16[32,2048]{1,0:T(8,128)(2,1)S(1)}, u32[]{:S(2)}, u32[]{:S(2)}) collective-permute-start(bf16[32,2048]{1,0:T(8,128)(2,1)} %bitcast.11), channel_id=1, source_target_pairs={{0,16},{16,0},{32,48},{48,32},{64,80},{80,64},{96,112},{112,96},{1... | collective-permute-start | bytes 393224 | tf_op jit(solution)/shard_map/ppermute | solution.py:371
  7.3 13.6 %collective-permute-start.1 = (bf16[64,2048]{1,0:T(8,128)(2,1)S(1)}, bf16[64,2048]{1,0:T(8,128)(2,1)S(1)}, u32[]{:S(2)}, u32[]{:S(2)}) collective-permute-start(bf16[64,2048]{1,0:T(8,128)(2,1)S(1)} %shard_map.76.here_ref), channel_id=1, source_target_pairs={{0,1},{1,0},{2,3},{3,2},{4,5},{5,4},{6,7},{7,6},{8,9},{9,8},{10,11... | collective-permute-start | bytes 786440 | tf_op jit(solution)/shard_map/ppermute | solution.py:384
  9.0 11.9 %collective-permute-start.2 = (bf16[64,2048]{1,0:T(8,128)(2,1)S(1)}, bf16[64,2048]{1,0:T(8,128)(2,1)S(1)}, u32[]{:S(2)}, u32[]{:S(2)}) collective-permute-start(bf16[64,2048]{1,0:T(8,128)(2,1)S(1)} %shard_map.76.here_ref), channel_id=1, source_target_pairs={{0,15},{1,2},{2,1},{3,4},{4,3},{5,6},{6,5},{7,8},{8,7},{9,10},{10,... | collective-permute-start | bytes 786440 | tf_op jit(solution)/shard_map/ppermute | solution.py:385
  10.5 7.1 %collective-permute-start.3 = (bf16[32,2048]{1,0:T(8,128)(2,1)}, bf16[32,2048]{1,0:T(8,128)(2,1)S(1)}, u32[]{:S(2)}, u32[]{:S(2)}) collective-permute-start(bf16[32,2048]{1,0:T(8,128)(2,1)} %bitcast.14), channel_id=1, source_target_pairs={{0,96},{16,112},{32,0},{48,16},{64,32},{80,48},{96,64},{112,80},{1... | collective-permute-start | bytes 393224 | tf_op jit(solution)/shard_map/ppermute | solution.py:372
  14.3 5.6 %collective-permute-start.4 = (bf16[32,2048]{1,0:T(8,128)(2,1)}, bf16[32,2048]{1,0:T(8,128)(2,1)S(1)}, u32[]{:S(2)}, u32[]{:S(2)}) collective-permute-start(bf16[32,2048]{1,0:T(8,128)(2,1)} %bitcast.15), channel_id=1, source_target_pairs={{0,64},{16,80},{32,96},{48,112},{64,0},{80,16},{96,32},{112,48},{1... | collective-permute-start | bytes 393224 | tf_op jit(solution)/shard_map/ppermute | solution.py:372
  14.3 6.6 %collective-permute-start.5 = (bf16[32,2048]{1,0:T(8,128)(2,1)}, bf16[32,2048]{1,0:T(8,128)(2,1)S(1)}, u32[]{:S(2)}, u32[]{:S(2)}) collective-permute-start(bf16[32,2048]{1,0:T(8,128)(2,1)} %bitcast.16), channel_id=1, source_target_pairs={{0,32},{16,48},{32,64},{48,80},{64,96},{80,112},{96,0},{112,16},{1... | collective-permute-start | bytes 393224 | tf_op jit(solution)/shard_map/ppermute | solution.py:372
  22.9 8.1 %collective-permute-start.12 = (f32[872,128]{1,0:T(8,128)S(1)}, f32[872,128]{1,0:T(8,128)S(1)}, u32[]{:S(2)}, u32[]{:S(2)}) collective-permute-start(f32[872,128]{1,0:T(8,128)S(1)} %get-tuple-element.40), channel_id=1, source_target_pairs={{0,1},{1,0},{2,3},{3,2},{4,5},{5,4},{6,7},{7,6},{8,9},{9,8},{10,11... | collective-permute-start | bytes 1339400 | tf_op jit(solution)/shard_map/ppermute | solution.py:396
  27.2 31.7 %collective-permute-start.9 = (bf16[128,2048]{1,0:T(8,128)(2,1)S(1)}, bf16[128,2048]{1,0:T(8,128)(2,1)S(1)}, u32[]{:S(2)}, u32[]{:S(2)}) collective-permute-start(bf16[128,2048]{1,0:T(8,128)(2,1)S(1)} %shard_map.81), channel_id=1, source_target_pairs={{0,1},{1,0},{2,3},{3,2},{4,5},{5,4},{6,7},{7,6},{8,9},{9,8},{10,11... | collective-permute-start | bytes 1572872 | tf_op jit(solution)/shard_map/ppermute | solution.py:416
  27.3 31.6 %collective-permute-start.10 = (bf16[128,2048]{1,0:T(8,128)(2,1)S(1)}, bf16[128,2048]{1,0:T(8,128)(2,1)S(1)}, u32[]{:S(2)}, u32[]{:S(2)}) collective-permute-start(bf16[128,2048]{1,0:T(8,128)(2,1)S(1)} %shard_map.81), channel_id=1, source_target_pairs={{0,15},{1,2},{2,1},{3,4},{4,3},{5,6},{6,5},{7,8},{8,7},{9,10},{10,... | collective-permute-start | bytes 1572872 | tf_op jit(solution)/shard_map/ppermute | solution.py:417
  28.3 19.0 %collective-permute-start.6 = (bf16[864,128]{1,0:T(8,128)(2,1)S(1)}, bf16[864,128]{1,0:T(8,128)(2,1)S(1)}, u32[]{:S(2)}, u32[]{:S(2)}) collective-permute-start(bf16[864,128]{1,0:T(8,128)(2,1)S(1)} %get-tuple-element.29), channel_id=1, source_target_pairs={{0,16},{16,0},{32,48},{48,32},{64,80},{80,64},{96,112},{112,96},{1... | collective-permute-start | bytes 663560 | tf_op jit(solution)/shard_map/ppermute | solution.py:380
  31.4 7.3 %collective-permute-start.13 = (bf16[448,128]{1,0:T(8,128)(2,1)S(1)}, bf16[448,128]{1,0:T(8,128)(2,1)S(1)}, u32[]{:S(2)}, u32[]{:S(2)}) collective-permute-start(bf16[448,128]{1,0:T(8,128)(2,1)S(1)} %get-tuple-element.42), channel_id=1, source_target_pairs={{0,2},{1,17},{2,0},{3,19},{4,6},{5,21},{6,4},{7,23},{8,10},{9,25},... | collective-permute-start | bytes 344072 | tf_op jit(solution)/shard_map/ppermute | solution.py:415
  31.7 7.0 %collective-permute-start.14 = (bf16[448,128]{1,0:T(8,128)(2,1)S(1)}, bf16[448,128]{1,0:T(8,128)(2,1)S(1)}, u32[]{:S(2)}, u32[]{:S(2)}) collective-permute-start(bf16[448,128]{1,0:T(8,128)(2,1)S(1)} %get-tuple-element.43), channel_id=1, source_target_pairs={{0,8},{1,25},{2,10},{3,27},{4,12},{5,29},{6,14},{7,31},{8,0},{9,17... | collective-permute-start | bytes 344072 | tf_op jit(solution)/shard_map/ppermute | solution.py:414
  39.1 10.7 %collective-permute-start.15 = (bf16[448,128]{1,0:T(8,128)(2,1)S(1)}, bf16[448,128]{1,0:T(8,128)(2,1)S(1)}, u32[]{:S(2)}, u32[]{:S(2)}) collective-permute-start(bf16[448,128]{1,0:T(8,128)(2,1)S(1)} %shard_map.85.own_ref), channel_id=1, source_target_pairs={{0,6},{1,7},{2,0},{3,1},{4,2},{5,3},{6,4},{7,5},{8,14},{9,15},{10,... | collective-permute-start | bytes 344072 | tf_op jit(solution)/shard_map/ppermute | solution.py:420
  47.3 17.1 %copy-start = (bf16[32]{0:T(256)(128)(2,1)S(1)}, bf16[32]{0:T(256)(128)(2,1)}, u32[]{:S(2)}) copy-start(bf16[32]{0:T(256)(128)(2,1)} %param.6) | copy-start | bytes 196
  49.0 13.4 %collective-permute-start.7 = (bf16[64,2176]{1,0:T(8,128)(2,1)S(1)}, bf16[64,2176]{1,0:T(8,128)(2,1)S(1)}, u32[]{:S(2)}, u32[]{:S(2)}) collective-permute-start(bf16[64,2176]{1,0:T(8,128)(2,1)S(1)} %get-tuple-element.32), channel_id=1, source_target_pairs={{0,96},{16,112},{32,64},{48,80},{64,32},{80,48},{96,0},{112,16},{1... | collective-permute-start | bytes 835592 | tf_op jit(solution)/shard_map/ppermute | solution.py:404
  49.7 5.6 %collective-permute-start.16 = (bf16[448,128]{1,0:T(8,128)(2,1)S(1)}, bf16[448,128]{1,0:T(8,128)(2,1)S(1)}, u32[]{:S(2)}, u32[]{:S(2)}) collective-permute-start(bf16[448,128]{1,0:T(8,128)(2,1)S(1)} %shard_map.85.own_ref), channel_id=1, source_target_pairs={{0,4},{1,5},{2,6},{3,7},{4,0},{5,1},{6,2},{7,3},{8,12},{9,13},{10,... | collective-permute-start | bytes 344072 | tf_op jit(solution)/shard_map/ppermute | solution.py:420
  49.8 8.1 %collective-permute-start.17 = (bf16[448,128]{1,0:T(8,128)(2,1)S(1)}, bf16[448,128]{1,0:T(8,128)(2,1)S(1)}, u32[]{:S(2)}, u32[]{:S(2)}) collective-permute-start(bf16[448,128]{1,0:T(8,128)(2,1)S(1)} %shard_map.85.own_ref), channel_id=1, source_target_pairs={{0,2},{1,3},{2,4},{3,5},{4,6},{5,7},{6,0},{7,1},{8,10},{9,11},{10,... | collective-permute-start | bytes 344072 | tf_op jit(solution)/shard_map/ppermute | solution.py:420
  58.5 5.6 %collective-permute-start.18 = (bf16[448,128]{1,0:T(8,128)(2,1)S(1)}, bf16[448,128]{1,0:T(8,128)(2,1)S(1)}, u32[]{:S(2)}, u32[]{:S(2)}) collective-permute-start(bf16[448,128]{1,0:T(8,128)(2,1)S(1)} %shard_map.86.own_ref.piece_ref), channel_id=1, source_target_pairs={{0,8},{1,9},{2,10},{3,11},{4,12},{5,13},{6,14},{7,15},{8,0},{9,1},... | collective-permute-start | bytes 344072 | tf_op jit(solution)/shard_map/ppermute | solution.py:452
  60.6 6.2 %collective-permute-start.11 = (bf16[32,2176]{1,0:T(8,128)(2,1)S(1)}, bf16[32,2176]{1,0:T(8,128)(2,1)S(1)}, u32[]{:S(2)}, u32[]{:S(2)}) collective-permute-start(bf16[32,2176]{1,0:T(8,128)(2,1)S(1)} %get-tuple-element.36), channel_id=1, source_target_pairs={{0,16},{16,0},{32,48},{48,32},{64,80},{80,64},{96,112},{112,96},{1... | collective-permute-start | bytes 417800 | tf_op jit(solution)/shard_map/ppermute | solution.py:438
  62.8 4.3 %collective-permute-start.8 = (bf16[32,2176]{1,0:T(8,128)(2,1)S(1)}, bf16[32,2176]{1,0:T(8,128)(2,1)S(1)}, u32[]{:S(2)}, u32[]{:S(2)}) collective-permute-start(bf16[32,2176]{1,0:T(8,128)(2,1)S(1)} %get-tuple-element.34), channel_id=1, source_target_pairs={{0,32},{16,48},{32,0},{48,16},{64,96},{80,112},{96,64},{112,80},{1... | collective-permute-start | bytes 417800 | tf_op jit(solution)/shard_map/ppermute | solution.py:408
  62.9 5.9 %collective-permute-start.20 = (bf16[448,128]{1,0:T(8,128)(2,1)S(1)}, bf16[448,128]{1,0:T(8,128)(2,1)S(1)}, u32[]{:S(2)}, u32[]{:S(2)}) collective-permute-start(bf16[448,128]{1,0:T(8,128)(2,1)S(1)} %shard_map.86.own_ref.piece_ref), channel_id=1, source_target_pairs={{0,1},{1,0},{2,3},{3,2},{4,5},{5,4},{6,7},{7,6},{8,9},{9,8},{10,11... | collective-permute-start | bytes 344072 | tf_op jit(solution)/shard_map/ppermute | solution.py:453
  64.1 5.9 %collective-permute-start.19 = (bf16[448,128]{1,0:T(8,128)(2,1)S(1)}, bf16[448,128]{1,0:T(8,128)(2,1)S(1)}, u32[]{:S(2)}, u32[]{:S(2)}) collective-permute-start(bf16[448,128]{1,0:T(8,128)(2,1)S(1)} %collective-permute-done.18.own_ref), channel_id=1, source_target_pairs={{0,1},{1,0},{2,3},{3,2},{4,5},{5,4},{6,7},{7,6},{8,9},{9,8},{10,11... | collective-permute-start | bytes 344072 | tf_op jit(solution)/shard_map/ppermute | solution.py:454

commit v7 on v6

--- a/solution.py
+++ b/solution.py
@@ -15,6 +15,7 @@
 TAPS = 9 * OWN
 HALF = 3 * TAPS
 PIECE = HALF // 2
+PART = 5 * 96
 CODED = PIECE + 16
 POWER = 15.0
 TOP = 120.0
@@ -32,7 +33,11 @@
 Z_FIRST = [(f, f ^ 2) for f in range(8)]
 Z_SECOND = [(f, f ^ 6) for f in range(8)]
 ACROSS = [(f, f ^ 1) for f in range(8)]
-BESIDE = [(s, (s + 1) % 16 if s & 1 else (s - 1) % 16) for s in range(16)]
+BESIDE = [
+    (f * 16 + s, (f ^ 2) * 16 + s if s in (0, 15) else f * 16 + (s + 1 if s & 1 else s - 1))
+    for f in range(8)
+    for s in range(16)
+]
 CORE = [(s, s ^ 1) for s in range(16)]
 XLO = [(s, s ^ 8) for s in range(16)]
 
@@ -75,7 +80,8 @@
         copy.wait()
     got = jnp.dot(w_ref[...], pick, preferred_element_type=F32).astype(BF)
     mine_ref[...] = got[:, :128]
-    theirs_ref[...] = got[:, 128:]
+    even = (lax.axis_index("space") & 1) == 0
+    theirs_ref[...] = jnp.where(even, got[:PART, 128:], got[864 - PART :, 128:])
 
 
 def join_kernel(*refs):
@@ -84,6 +90,13 @@
     for ref in parts:
         out_ref[at : at + ref.shape[0], :] = ref[...]
         at += ref.shape[0]
+
+
+def join_w_kernel(near_ref, far_ref, out_ref):
+    even = (lax.axis_index("space") & 1) == 0
+    near, far = near_ref[...], far_ref[...]
+    out_ref[:PART, :] = jnp.where(even, near, far)
+    out_ref[PART:, :] = jnp.where(even, far, near)[2 * PART - 864 :]
 
 
 def forward_kernel(xs_ref, wa_ref, wb_ref, mine_ref, first_ref, send_ref):
@@ -326,11 +339,14 @@
         copy.wait()
 
 
+def widen_kernel(ref, out):
+    out[...] = ref[...].astype(F32)
+
+
 def bias_kernel(ref, out):
     row = lax.broadcasted_iota(jnp.int32, (OWN, OWN), 0)
     col = lax.broadcasted_iota(jnp.int32, (OWN, OWN), 1)
-    wide = jnp.where(row == col, ref[...].astype(F32), 0.0)
-    out[...] = jnp.sum(wide, axis=1, keepdims=True)
+    out[...] = jnp.sum(jnp.where(row == col, ref[...], 0.0), axis=1, keepdims=True)
 
 
 def halve_kernel(mine_ref, first_ref, got_ref, sum_ref, send_ref):
@@ -372,17 +388,19 @@
     c1, c3, c2 = (lax.ppermute(c_own, "filt", along_z(-r)) for r in (1, 3, 2))
     w_mine, w_theirs, x_near, c_near = call(
         select_kernel,
-        [((864, 128), BF), ((864, 128), BF), ((OWN, PLANE), BF), ((OWN, PLANE), BF)],
+        [((864, 128), BF), ((PART, 128), BF), ((OWN, PLANE), BF), ((OWN, PLANE), BF)],
         *(pltpu.with_memory_space_constraint(v, pltpu.HBM) for v in (weight.reshape(864, 256), x_own, c_own)),
         scratch=[pltpu.VMEM((864, 256), BF), pltpu.SemaphoreType.DMA((3,))],
         space=pl.BlockSpec(memory_space=pltpu.HBM),
     )
-    w_other = lax.ppermute(w_theirs, "filt", ACROSS)
+    w_half = lax.ppermute(w_theirs, "filt", ACROSS)
+    w_rest = lax.ppermute(w_half, "space", CORE)
+    (w_other,) = call(join_w_kernel, [((864, 128), BF)], w_half, w_rest)
     cots = [c_near, c1, c2, c3]
 
     (x_here,) = call(join_kernel, [((64, PLANE), BF)], x_near, x_other)
     x_chip = lax.ppermute(x_here, "space", CORE)
-    x_far = lax.ppermute(x_here, "space", BESIDE)
+    x_far = lax.ppermute(x_here, ("filt", "space"), BESIDE)
 
     xs, keep, send = call(
         kernel_grad_kernel,
@@ -414,7 +432,7 @@
     r_far = lax.ppermute(r_send, ("filt", "space"), crossing(8, 8))
     r_near = lax.ppermute(r_cross, ("filt", "space"), crossing(0, 2))
     c_chip = lax.ppermute(c_here, "space", CORE)
-    c_far = lax.ppermute(c_here, "space", BESIDE)
+    c_far = lax.ppermute(c_here, ("filt", "space"), BESIDE)
 
     (mine_y,) = call(code_kernel, [((CODED, 128), BF)], r_keep, r_near, r_far)
     y1, y3, y2 = (lax.ppermute(mine_y, "space", along_y(-r)) for r in (1, 3, 2))
@@ -423,7 +441,8 @@
         functools.partial(piece_kernel, factor=factor), [((CODED, 128), BF)], mine_y, y1, y2, y3
     )
 
-    (wide_bias,) = call(bias_kernel, [((OWN, 1), F32)], bias.reshape(1, OWN))
+    (row_bias,) = call(widen_kernel, [((1, OWN), F32)], bias.reshape(1, OWN))
+    (wide_bias,) = call(bias_kernel, [((OWN, 1), F32)], row_bias)
 
     g_mine, g_theirs = call(
         input_grad_kernel,

time: 72 us -> 68.7 us (0.954)
  starting transfers between devices: 35.5 us -> 30.2 us
  waiting for transfers between devices: 22.4 us -> 24.7 us
    ppermute x1, starting transfers between devices: 4.29 us -> 0.95 us  [step(): r_core = lax.ppermute(send, 'space', CORE)]
    ppermute x3, waiting for transfers between devices: 5.94 us -> 8.56 us  [step(): c1, c3, c2 = (lax.ppermute(c_own, 'filt', along_z(-r)) for r in (1, 3, 2))]
    ppermute x3, starting transfers between devices: 8.8 us -> 6.32 us  [step(): y1, y3, y2 = (lax.ppermute(mine_y, 'space', along_y(-r)) for r in (1, 3, 2))]
    ppermute x1, waiting for transfers between devices: 4.57 us -> 3.31 us  [step(): r_near = lax.ppermute(r_cross, ('filt', 'space'), crossing(0, 2))]
    ppermute x1, starting transfers between devices: 0.29 us -> 1.23 us  [step(): got_far = lax.ppermute(piece_far, 'space', CORE)]
    ppermute x3, waiting for transfers between devices: 7.53 us -> 8.4 us  [step(): y1, y3, y2 = (lax.ppermute(mine_y, 'space', along_y(-r)) for r in (1, 3, 2))]
    ppermute x3 -> x4, starting transfers between devices: 5.2 us -> 5.57 us  [the longest x1 2.75 us: step(): w_half = lax.ppermute(w_theirs, 'filt', ACROSS)]
    pallas_call x16 -> x18, Pallas kernels: 12.5 us -> 12.5 us  [call(): pl.pallas_call(kernel, out_shape=[jax.ShapeDtypeStruct(s, d) for s, d in...]
  transfers between devices with their start and end apart: 21 -> 22, of which waited for: 9 -> 9; matrix products, arithmetic and copies ran while one was open for 0% -> 0% of each run, Pallas kernels for 13% -> 14%
where the time goes in v7:
time: 68.7 us; the launch traced here: 68.4 us
  starting transfers between devices  30.2 us (44%)
  waiting for transfers between devices  24.7 us (36%)
  Pallas kernels  12.5 us (18%)
  between operations  0.97 us (1%)
    pallas_call x18, Pallas kernels, call(): pl.pallas_call(kernel, out_shape=[jax.ShapeDtypeStruct(s, d) for s, d in...  12.5 us
    ppermute x3, waiting for transfers between devices, step(): c1, c3, c2 = (lax.ppermute(c_own, 'filt', along_z(-r)) for r in (1, 3, 2))  8.56 us
    ppermute x3, waiting for transfers between devices, step(): y1, y3, y2 = (lax.ppermute(mine_y, 'space', along_y(-r)) for r in (1, 3, 2))  8.4 us
    ppermute x3, starting transfers between devices, step(): y1, y3, y2 = (lax.ppermute(mine_y, 'space', along_y(-r)) for r in (1, 3, 2))  6.32 us
    ppermute x3, starting transfers between devices, step(): c1, c3, c2 = (lax.ppermute(c_own, 'filt', along_z(-r)) for r in (1, 3, 2))  4.46 us
    ppermute x1, starting transfers between devices, step(): x_other = lax.ppermute(x_own, 'filt', ACROSS)  3.64 us
    ppermute x1, waiting for transfers between devices, step(): r_near = lax.ppermute(r_cross, ('filt', 'space'), crossing(0, 2))  3.31 us
    ppermute x1, starting transfers between devices, step(): w_half = lax.ppermute(w_theirs, 'filt', ACROSS)  2.75 us
  transfers between devices with their start and end apart: 22, of which 9 were waited for; matrix products, arithmetic and copies ran while one was open for 0% of the time, Pallas kernels for 14%

profile of v7, /device:TPU:1, one launch (start us, length us, event | category | flops | bytes accessed | tf_op | source)
XLA Modules:
  0.0 68.4 jit_solution(17876148798254669985)
XLA Ops:
  0.6 3.6 %collective-permute-start = (bf16[32,2048]{1,0:T(8,128)(2,1)}, bf16[32,2048]{1,0:T(8,128)(2,1)S(1)}, u32[]{:S(2)}, u32[]{:S(2)}) collective-permute-start(bf16[32,2048]{1,0:T(8,128)(2,1)} %bitcast.11), channel_id=1, source_target_pairs={{0,16},{16,0},{32,48},{48,32},{64,80},{80,64},{96,112},{112,96},{1... | collective-permute-start | bytes 393224 | tf_op jit(solution)/shard_map/ppermute | solution.py:387
  4.3 1.4 %shard_map.75 = (bf16[864,128]{1,0:T(8,128)(2,1)S(1)}, bf16[480,128]{1,0:T(8,128)(2,1)S(1)}, bf16[32,2048]{1,0:T(8,128)(2,1)S(1)}, bf16[32,2048]{1,0:T(8,128)(2,1)S(1)}) custom-call(bf16[864,256]{1,0:T(8,128)(2,1)} %bitcast.10, bf16[32,2048]{1,0:T(8,128)(2,1)} %bitcast.12, bf16[32,2048]{1,0:T(8,128)(2,1)} %bitcast.13), custom_call_target="tpu_custom_call" | custom-call | tf_op jit(solution)/shard_map/pallas_call | solution.py:372
  5.7 1.6 %collective-permute-done.refs_1_ = bf16[32,2048]{1,0:T(8,128)(2,1)S(1)} collective-permute-done((bf16[32,2048]{1,0:T(8,128)(2,1)}, bf16[32,2048]{1,0:T(8,128)(2,1)S(1)}, u32[]{:S(2)}, u32[]{:S(2)}) %collective-permute-start) | collective-permute-done | bytes 131104 | tf_op jit(solution)/shard_map/ppermute | solution.py:387
  7.3 1.7 %collective-permute-start.1 = (bf16[64,2048]{1,0:T(8,128)(2,1)S(1)}, bf16[64,2048]{1,0:T(8,128)(2,1)S(1)}, u32[]{:S(2)}, u32[]{:S(2)}) collective-permute-start(bf16[64,2048]{1,0:T(8,128)(2,1)S(1)} %shard_map.76.here_ref), channel_id=1, source_target_pairs={{0,1},{1,0},{2,3},{3,2},{4,5},{5,4},{6,7},{7,6},{8,9},{9,8},{10,11... | collective-permute-start | bytes 786440 | tf_op jit(solution)/shard_map/ppermute | solution.py:402
  9.0 1.5 %collective-permute-start.2 = (bf16[64,2048]{1,0:T(8,128)(2,1)S(1)}, bf16[64,2048]{1,0:T(8,128)(2,1)S(1)}, u32[]{:S(2)}, u32[]{:S(2)}) collective-permute-start(bf16[64,2048]{1,0:T(8,128)(2,1)S(1)} %shard_map.76.here_ref), channel_id=1, source_target_pairs={{0,32},{1,2},{2,1},{3,4},{4,3},{5,6},{6,5},{7,8},{8,7},{9,10},{10,... | collective-permute-start | bytes 786440 | tf_op jit(solution)/shard_map/ppermute | solution.py:403
  10.5 3.8 %collective-permute-start.3 = (bf16[32,2048]{1,0:T(8,128)(2,1)}, bf16[32,2048]{1,0:T(8,128)(2,1)S(1)}, u32[]{:S(2)}, u32[]{:S(2)}) collective-permute-start(bf16[32,2048]{1,0:T(8,128)(2,1)} %bitcast.14), channel_id=1, source_target_pairs={{0,96},{16,112},{32,0},{48,16},{64,32},{80,48},{96,64},{112,80},{1... | collective-permute-start | bytes 393224 | tf_op jit(solution)/shard_map/ppermute | solution.py:388
  14.3 0.7 %collective-permute-start.5 = (bf16[32,2048]{1,0:T(8,128)(2,1)}, bf16[32,2048]{1,0:T(8,128)(2,1)S(1)}, u32[]{:S(2)}, u32[]{:S(2)}) collective-permute-start(bf16[32,2048]{1,0:T(8,128)(2,1)} %bitcast.16), channel_id=1, source_target_pairs={{0,32},{16,48},{32,64},{48,80},{64,96},{80,112},{96,0},{112,16},{1... | collective-permute-start | bytes 393224 | tf_op jit(solution)/shard_map/ppermute | solution.py:388
  15.0 5.5 %collective-permute-done.3.c1.refs_1_ = bf16[32,2048]{1,0:T(8,128)(2,1)S(1)} collective-permute-done((bf16[32,2048]{1,0:T(8,128)(2,1)}, bf16[32,2048]{1,0:T(8,128)(2,1)S(1)}, u32[]{:S(2)}, u32[]{:S(2)}) %collective-permute-start.3) | collective-permute-done | bytes 131104 | tf_op jit(solution)/shard_map/ppermute | solution.py:388
  20.4 1.1 %collective-permute-done.4.c2.refs_2_ = bf16[32,2048]{1,0:T(8,128)(2,1)S(1)} collective-permute-done((bf16[32,2048]{1,0:T(8,128)(2,1)}, bf16[32,2048]{1,0:T(8,128)(2,1)S(1)}, u32[]{:S(2)}, u32[]{:S(2)}) %collective-permute-start.4) | collective-permute-done | bytes 131104 | tf_op jit(solution)/shard_map/ppermute | solution.py:388
  21.6 2.0 %collective-permute-done.5.c3.refs_3_ = bf16[32,2048]{1,0:T(8,128)(2,1)S(1)} collective-permute-done((bf16[32,2048]{1,0:T(8,128)(2,1)}, bf16[32,2048]{1,0:T(8,128)(2,1)S(1)}, u32[]{:S(2)}, u32[]{:S(2)}) %collective-permute-start.5) | collective-permute-done | bytes 131104 | tf_op jit(solution)/shard_map/ppermute | solution.py:388
  23.6 1.9 %shard_map.77 = (bf16[2,304,2048]{2,1,0:T(8,128)(2,1)S(1)}, f32[872,128]{1,0:T(8,128)S(1)}, f32[872,128]{1,0:T(8,128)S(1)}) custom-call(bf16[64,2048]{1,0:T(8,128)(2,1)S(1)} %collective-permute-done.1.chip_ref, bf16[64,2048]{1,0:T(8,128)(2,1)S(1)} %shard_map.76.here_ref, bf16[64,2048]{1,0:T(8,128)(2,1)S(1)} %collective-permute-done.2.far_ref, ...), custom_call_target="tpu_custom_call" | custom-call | tf_op jit(solution)/shard_map/pallas_call | solution.py:372
  25.5 1.0 %collective-permute-start.13 = (f32[872,128]{1,0:T(8,128)S(1)}, f32[872,128]{1,0:T(8,128)S(1)}, u32[]{:S(2)}, u32[]{:S(2)}) collective-permute-start(f32[872,128]{1,0:T(8,128)S(1)} %get-tuple-element.40), channel_id=1, source_target_pairs={{0,1},{1,0},{2,3},{3,2},{4,5},{5,4},{6,7},{7,6},{8,9},{9,8},{10,11... | collective-permute-start | bytes 1339400 | tf_op jit(solution)/shard_map/ppermute | solution.py:414
  26.5 2.8 %collective-permute-start.6 = (bf16[480,128]{1,0:T(8,128)(2,1)S(1)}, bf16[480,128]{1,0:T(8,128)(2,1)S(1)}, u32[]{:S(2)}, u32[]{:S(2)}) collective-permute-start(bf16[480,128]{1,0:T(8,128)(2,1)S(1)} %get-tuple-element.29), channel_id=1, source_target_pairs={{0,16},{16,0},{32,48},{48,32},{64,80},{80,64},{96,112},{112,96},{1... | collective-permute-start | bytes 368648 | tf_op jit(solution)/shard_map/ppermute | solution.py:396
  29.2 0.5 collective-permute-start.10
  29.7 1.3 %collective-permute-start.11 = (bf16[128,2048]{1,0:T(8,128)(2,1)S(1)}, bf16[128,2048]{1,0:T(8,128)(2,1)S(1)}, u32[]{:S(2)}, u32[]{:S(2)}) collective-permute-start(bf16[128,2048]{1,0:T(8,128)(2,1)S(1)} %shard_map.83), channel_id=1, source_target_pairs={{0,32},{1,2},{2,1},{3,4},{4,3},{5,6},{6,5},{7,8},{8,7},{9,10},{10,... | collective-permute-start | bytes 1572872 | tf_op jit(solution)/shard_map/ppermute | solution.py:435
  31.7 2.5 %collective-permute-start.15 = (bf16[448,128]{1,0:T(8,128)(2,1)S(1)}, bf16[448,128]{1,0:T(8,128)(2,1)S(1)}, u32[]{:S(2)}, u32[]{:S(2)}) collective-permute-start(bf16[448,128]{1,0:T(8,128)(2,1)S(1)} %get-tuple-element.43), channel_id=1, source_target_pairs={{0,8},{1,25},{2,10},{3,27},{4,12},{5,29},{6,14},{7,31},{8,0},{9,17... | collective-permute-start | bytes 344072 | tf_op jit(solution)/shard_map/ppermute | solution.py:432
  34.2 3.3 %collective-permute-done.14.near_ref = bf16[448,128]{1,0:T(8,128)(2,1)S(1)} collective-permute-done((bf16[448,128]{1,0:T(8,128)(2,1)S(1)}, bf16[448,128]{1,0:T(8,128)(2,1)S(1)}, u32[]{:S(2)}, u32[]{:S(2)}) %collective-permute-start.14) | collective-permute-done | bytes 114720 | tf_op jit(solution)/shard_map/ppermute | solution.py:433
  38.1 5.7 %collective-permute-start.16 = (bf16[448,128]{1,0:T(8,128)(2,1)S(1)}, bf16[448,128]{1,0:T(8,128)(2,1)S(1)}, u32[]{:S(2)}, u32[]{:S(2)}) collective-permute-start(bf16[448,128]{1,0:T(8,128)(2,1)S(1)} %shard_map.87.own_ref), channel_id=1, source_target_pairs={{0,6},{1,7},{2,0},{3,1},{4,2},{5,3},{6,4},{7,5},{8,14},{9,15},{10,... | collective-permute-start | bytes 344072 | tf_op jit(solution)/shard_map/ppermute | solution.py:438
  43.9 1.7 %shard_map.79 = (f32[32,2048]{1,0:T(8,128)S(1)}, f32[32,2048]{1,0:T(8,128)S(1)}, bf16[64,2176]{1,0:T(8,128)(2,1)S(1)}) custom-call(bf16[2,304,2048]{2,1,0:T(8,128)(2,1)S(1)} %get-tuple-element.27.xs_ref, bf16[864,128]{1,0:T(8,128)(2,1)S(1)} %get-tuple-element.28.wa_ref, bf16[864,128]{1,0:T(8,128)(2,1)S(1)} %shard_map.78.wb_ref), custom_call_target="tpu_custom_call" | custom-call | tf_op jit(solution)/shard_map/pallas_call | solution.py:372
  45.6 0.7 %collective-permute-start.8 = (bf16[64,2176]{1,0:T(8,128)(2,1)S(1)}, bf16[64,2176]{1,0:T(8,128)(2,1)S(1)}, u32[]{:S(2)}, u32[]{:S(2)}) collective-permute-start(bf16[64,2176]{1,0:T(8,128)(2,1)S(1)} %get-tuple-element.32), channel_id=1, source_target_pairs={{0,96},{16,112},{32,64},{48,80},{64,32},{80,48},{96,0},{112,16},{1... | collective-permute-start | bytes 835592 | tf_op jit(solution)/shard_map/ppermute | solution.py:422
  46.4 0.6 collective-permute-start.18
  47.0 6.1 %collective-permute-done.17.y2_ref = bf16[448,128]{1,0:T(8,128)(2,1)S(1)} collective-permute-done((bf16[448,128]{1,0:T(8,128)(2,1)S(1)}, bf16[448,128]{1,0:T(8,128)(2,1)S(1)}, u32[]{:S(2)}, u32[]{:S(2)}) %collective-permute-start.17) | collective-permute-done | bytes 114720 | tf_op jit(solution)/shard_map/ppermute | solution.py:438
  53.0 2.3 %collective-permute-done.18.y3_ref = bf16[448,128]{1,0:T(8,128)(2,1)S(1)} collective-permute-done((bf16[448,128]{1,0:T(8,128)(2,1)S(1)}, bf16[448,128]{1,0:T(8,128)(2,1)S(1)}, u32[]{:S(2)}, u32[]{:S(2)}) %collective-permute-start.18) | collective-permute-done | bytes 114720 | tf_op jit(solution)/shard_map/ppermute | solution.py:438
  55.4 0.6 shard_map.88.own_ref.piece_ref
  56.0 1.7 %shard_map.84 = (f32[32,2048]{1,0:T(8,128)S(1)}, bf16[32,2176]{1,0:T(8,128)(2,1)S(1)}) custom-call(bf16[128,2048]{1,0:T(8,128)(2,1)S(1)} %collective-permute-done.10.chip_ref, bf16[128,2048]{1,0:T(8,128)(2,1)S(1)} %collective-permute-done.11.far_ref, bf16[32,2048]{1,0:T(8,128)(2,1)S(1)} %get-tuple-element.26.c0.refs_0_, ...), custom_call_target="tpu_custom_call" | custom-call | tf_op jit(solution)/shard_map/pallas_call | solution.py:372
  57.7 1.3 %collective-permute-start.12 = (bf16[32,2176]{1,0:T(8,128)(2,1)S(1)}, bf16[32,2176]{1,0:T(8,128)(2,1)S(1)}, u32[]{:S(2)}, u32[]{:S(2)}) collective-permute-start(bf16[32,2176]{1,0:T(8,128)(2,1)S(1)} %get-tuple-element.36), channel_id=1, source_target_pairs={{0,16},{16,0},{32,48},{48,32},{64,80},{80,64},{96,112},{112,96},{1... | collective-permute-start | bytes 417800 | tf_op jit(solution)/shard_map/ppermute | solution.py:457
  59.5 0.9 %collective-permute-start.21 = (bf16[448,128]{1,0:T(8,128)(2,1)S(1)}, bf16[448,128]{1,0:T(8,128)(2,1)S(1)}, u32[]{:S(2)}, u32[]{:S(2)}) collective-permute-start(bf16[448,128]{1,0:T(8,128)(2,1)S(1)} %shard_map.88.own_ref.piece_ref), channel_id=1, source_target_pairs={{0,1},{1,0},{2,3},{3,2},{4,5},{5,4},{6,7},{7,6},{8,9},{9,8},{10,11... | collective-permute-start | bytes 344072 | tf_op jit(solution)/shard_map/ppermute | solution.py:472
  60.4 1.2 %collective-permute-start.20 = (bf16[448,128]{1,0:T(8,128)(2,1)S(1)}, bf16[448,128]{1,0:T(8,128)(2,1)S(1)}, u32[]{:S(2)}, u32[]{:S(2)}) collective-permute-start(bf16[448,128]{1,0:T(8,128)(2,1)S(1)} %collective-permute-done.19.own_ref), channel_id=1, source_target_pairs={{0,1},{1,0},{2,3},{3,2},{4,5},{5,4},{6,7},{7,6},{8,9},{9,8},{10,11... | collective-permute-start | bytes 344072 | tf_op jit(solution)/shard_map/ppermute | solution.py:473
  61.7 2.5 %collective-permute-done.12.theirs_ref = bf16[32,2176]{1,0:T(8,128)(2,1)S(1)} collective-permute-done((bf16[32,2176]{1,0:T(8,128)(2,1)S(1)}, bf16[32,2176]{1,0:T(8,128)(2,1)S(1)}, u32[]{:S(2)}, u32[]{:S(2)}) %collective-permute-start.12) | collective-permute-done | bytes 139296 | tf_op jit(solution)/shard_map/ppermute | solution.py:457
  64.2 1.0 %shard_map.85 = (f32[32,2048]{1,0:T(8,128)}, f32[32,2048]{1,0:T(8,128)}) custom-call(f32[32,2048]{1,0:T(8,128)S(1)} %get-tuple-element.33.mine_ref, bf16[32,2176]{1,0:T(8,128)(2,1)S(1)} %collective-permute-done.9.got_ref, f32[32,1]{1,0:T(8,128)S(1)} %shard_map.82.bias_ref, f32[32,2048]{1,0:T(8,128)S(1)} %get-tuple-element.35.near_ref, ...), custom_call_target="tpu_custom_call" | custom-call | tf_op jit(solution)/shard_map/pallas_call | solution.py:372
  66.0 1.1 %shard_map.91 = (f32[9,96,256]{2,1,0:T(8,128)}, f32[1,32]{1,0:T(1,128)}) custom-call(f32[432,256]{1,0:T(8,128)S(1)} %shard_map.90.own_ref, bf16[448,128]{1,0:T(8,128)(2,1)S(1)} %shard_map.88.own_ref.piece_ref, bf16[448,128]{1,0:T(8,128)(2,1)S(1)} %collective-permute-done.21.got_ref), custom_call_target="tpu_custom_call" | custom-call | tf_op jit(solution)/shard_map/pallas_call | solution.py:372
  67.1 1.1 %shard_map.92 = f32[9,96,256]{2,1,0:T(8,128)} custom-call(f32[432,256]{1,0:T(8,128)S(1)} %shard_map.89.own_ref, bf16[448,128]{1,0:T(8,128)(2,1)S(1)} %collective-permute-done.20.got_ref, f32[9,96,256]{2,1,0:T(8,128)} %get-tuple-element.44._), custom_call_target="tpu_custom_call", output_to_operand_aliasing={{}: (2, {})} | custom-call | tf_op jit(solution)/shard_map/pallas_call | solution.py:372
  (32 shorter events, 2.7 us)
Async XLA Ops:
  0.6 6.7 %collective-permute-start = (bf16[32,2048]{1,0:T(8,128)(2,1)}, bf16[32,2048]{1,0:T(8,128)(2,1)S(1)}, u32[]{:S(2)}, u32[]{:S(2)}) collective-permute-start(bf16[32,2048]{1,0:T(8,128)(2,1)} %bitcast.11), channel_id=1, source_target_pairs={{0,16},{16,0},{32,48},{48,32},{64,80},{80,64},{96,112},{112,96},{1... | collective-permute-start | bytes 393224 | tf_op jit(solution)/shard_map/ppermute | solution.py:387
  7.3 16.2 %collective-permute-start.1 = (bf16[64,2048]{1,0:T(8,128)(2,1)S(1)}, bf16[64,2048]{1,0:T(8,128)(2,1)S(1)}, u32[]{:S(2)}, u32[]{:S(2)}) collective-permute-start(bf16[64,2048]{1,0:T(8,128)(2,1)S(1)} %shard_map.76.here_ref), channel_id=1, source_target_pairs={{0,1},{1,0},{2,3},{3,2},{4,5},{5,4},{6,7},{7,6},{8,9},{9,8},{10,11... | collective-permute-start | bytes 786440 | tf_op jit(solution)/shard_map/ppermute | solution.py:402
  9.0 14.5 %collective-permute-start.2 = (bf16[64,2048]{1,0:T(8,128)(2,1)S(1)}, bf16[64,2048]{1,0:T(8,128)(2,1)S(1)}, u32[]{:S(2)}, u32[]{:S(2)}) collective-permute-start(bf16[64,2048]{1,0:T(8,128)(2,1)S(1)} %shard_map.76.here_ref), channel_id=1, source_target_pairs={{0,32},{1,2},{2,1},{3,4},{4,3},{5,6},{6,5},{7,8},{8,7},{9,10},{10,... | collective-permute-start | bytes 786440 | tf_op jit(solution)/shard_map/ppermute | solution.py:403
  10.5 9.9 %collective-permute-start.3 = (bf16[32,2048]{1,0:T(8,128)(2,1)}, bf16[32,2048]{1,0:T(8,128)(2,1)S(1)}, u32[]{:S(2)}, u32[]{:S(2)}) collective-permute-start(bf16[32,2048]{1,0:T(8,128)(2,1)} %bitcast.14), channel_id=1, source_target_pairs={{0,96},{16,112},{32,0},{48,16},{64,32},{80,48},{96,64},{112,80},{1... | collective-permute-start | bytes 393224 | tf_op jit(solution)/shard_map/ppermute | solution.py:388
  14.3 7.3 %collective-permute-start.4 = (bf16[32,2048]{1,0:T(8,128)(2,1)}, bf16[32,2048]{1,0:T(8,128)(2,1)S(1)}, u32[]{:S(2)}, u32[]{:S(2)}) collective-permute-start(bf16[32,2048]{1,0:T(8,128)(2,1)} %bitcast.15), channel_id=1, source_target_pairs={{0,64},{16,80},{32,96},{48,112},{64,0},{80,16},{96,32},{112,48},{1... | collective-permute-start | bytes 393224 | tf_op jit(solution)/shard_map/ppermute | solution.py:388
  14.3 9.3 %collective-permute-start.5 = (bf16[32,2048]{1,0:T(8,128)(2,1)}, bf16[32,2048]{1,0:T(8,128)(2,1)S(1)}, u32[]{:S(2)}, u32[]{:S(2)}) collective-permute-start(bf16[32,2048]{1,0:T(8,128)(2,1)} %bitcast.16), channel_id=1, source_target_pairs={{0,32},{16,48},{32,64},{48,80},{64,96},{80,112},{96,0},{112,16},{1... | collective-permute-start | bytes 393224 | tf_op jit(solution)/shard_map/ppermute | solution.py:388
  25.5 5.5 %collective-permute-start.13 = (f32[872,128]{1,0:T(8,128)S(1)}, f32[872,128]{1,0:T(8,128)S(1)}, u32[]{:S(2)}, u32[]{:S(2)}) collective-permute-start(f32[872,128]{1,0:T(8,128)S(1)} %get-tuple-element.40), channel_id=1, source_target_pairs={{0,1},{1,0},{2,3},{3,2},{4,5},{5,4},{6,7},{7,6},{8,9},{9,8},{10,11... | collective-permute-start | bytes 1339400 | tf_op jit(solution)/shard_map/ppermute | solution.py:414
  26.5 7.7 %collective-permute-start.6 = (bf16[480,128]{1,0:T(8,128)(2,1)S(1)}, bf16[480,128]{1,0:T(8,128)(2,1)S(1)}, u32[]{:S(2)}, u32[]{:S(2)}) collective-permute-start(bf16[480,128]{1,0:T(8,128)(2,1)S(1)} %get-tuple-element.29), channel_id=1, source_target_pairs={{0,16},{16,0},{32,48},{48,32},{64,80},{80,64},{96,112},{112,96},{1... | collective-permute-start | bytes 368648 | tf_op jit(solution)/shard_map/ppermute | solution.py:396
  29.2 26.8 %collective-permute-start.10 = (bf16[128,2048]{1,0:T(8,128)(2,1)S(1)}, bf16[128,2048]{1,0:T(8,128)(2,1)S(1)}, u32[]{:S(2)}, u32[]{:S(2)}) collective-permute-start(bf16[128,2048]{1,0:T(8,128)(2,1)S(1)} %shard_map.83), channel_id=1, source_target_pairs={{0,1},{1,0},{2,3},{3,2},{4,5},{5,4},{6,7},{7,6},{8,9},{9,8},{10,11... | collective-permute-start | bytes 1572872 | tf_op jit(solution)/shard_map/ppermute | solution.py:434
  29.7 26.3 %collective-permute-start.11 = (bf16[128,2048]{1,0:T(8,128)(2,1)S(1)}, bf16[128,2048]{1,0:T(8,128)(2,1)S(1)}, u32[]{:S(2)}, u32[]{:S(2)}) collective-permute-start(bf16[128,2048]{1,0:T(8,128)(2,1)S(1)} %shard_map.83), channel_id=1, source_target_pairs={{0,32},{1,2},{2,1},{3,4},{4,3},{5,6},{6,5},{7,8},{8,7},{9,10},{10,... | collective-permute-start | bytes 1572872 | tf_op jit(solution)/shard_map/ppermute | solution.py:435
  31.4 6.1 %collective-permute-start.14 = (bf16[448,128]{1,0:T(8,128)(2,1)S(1)}, bf16[448,128]{1,0:T(8,128)(2,1)S(1)}, u32[]{:S(2)}, u32[]{:S(2)}) collective-permute-start(bf16[448,128]{1,0:T(8,128)(2,1)S(1)} %get-tuple-element.42), channel_id=1, source_target_pairs={{0,2},{1,17},{2,0},{3,19},{4,6},{5,21},{6,4},{7,23},{8,10},{9,25},... | collective-permute-start | bytes 344072 | tf_op jit(solution)/shard_map/ppermute | solution.py:433
  31.7 6.1 %collective-permute-start.15 = (bf16[448,128]{1,0:T(8,128)(2,1)S(1)}, bf16[448,128]{1,0:T(8,128)(2,1)S(1)}, u32[]{:S(2)}, u32[]{:S(2)}) collective-permute-start(bf16[448,128]{1,0:T(8,128)(2,1)S(1)} %get-tuple-element.43), channel_id=1, source_target_pairs={{0,8},{1,25},{2,10},{3,27},{4,12},{5,29},{6,14},{7,31},{8,0},{9,17... | collective-permute-start | bytes 344072 | tf_op jit(solution)/shard_map/ppermute | solution.py:432
  34.2 9.7 %collective-permute-start.7 = (bf16[480,128]{1,0:T(8,128)(2,1)S(1)}, bf16[480,128]{1,0:T(8,128)(2,1)S(1)}, u32[]{:S(2)}, u32[]{:S(2)}) collective-permute-start(bf16[480,128]{1,0:T(8,128)(2,1)S(1)} %collective-permute-done.6.near_ref), channel_id=1, source_target_pairs={{0,1},{1,0},{2,3},{3,2},{4,5},{5,4},{6,7},{7,6},{8,9},{9,8},{10,11... | collective-permute-start | bytes 368648 | tf_op jit(solution)/shard_map/ppermute | solution.py:397
  38.1 8.2 %collective-permute-start.16 = (bf16[448,128]{1,0:T(8,128)(2,1)S(1)}, bf16[448,128]{1,0:T(8,128)(2,1)S(1)}, u32[]{:S(2)}, u32[]{:S(2)}) collective-permute-start(bf16[448,128]{1,0:T(8,128)(2,1)S(1)} %shard_map.87.own_ref), channel_id=1, source_target_pairs={{0,6},{1,7},{2,0},{3,1},{4,2},{5,3},{6,4},{7,5},{8,14},{9,15},{10,... | collective-permute-start | bytes 344072 | tf_op jit(solution)/shard_map/ppermute | solution.py:438
  43.9 17.8 %copy-start = (bf16[32]{0:T(256)(128)(2,1)S(1)}, bf16[32]{0:T(256)(128)(2,1)}, u32[]{:S(2)}) copy-start(bf16[32]{0:T(256)(128)(2,1)} %param.6) | copy-start | bytes 196
  45.6 13.4 %collective-permute-start.8 = (bf16[64,2176]{1,0:T(8,128)(2,1)S(1)}, bf16[64,2176]{1,0:T(8,128)(2,1)S(1)}, u32[]{:S(2)}, u32[]{:S(2)}) collective-permute-start(bf16[64,2176]{1,0:T(8,128)(2,1)S(1)} %get-tuple-element.32), channel_id=1, source_target_pairs={{0,96},{16,112},{32,64},{48,80},{64,32},{80,48},{96,0},{112,16},{1... | collective-permute-start | bytes 835592 | tf_op jit(solution)/shard_map/ppermute | solution.py:422
  46.3 6.7 %collective-permute-start.17 = (bf16[448,128]{1,0:T(8,128)(2,1)S(1)}, bf16[448,128]{1,0:T(8,128)(2,1)S(1)}, u32[]{:S(2)}, u32[]{:S(2)}) collective-permute-start(bf16[448,128]{1,0:T(8,128)(2,1)S(1)} %shard_map.87.own_ref), channel_id=1, source_target_pairs={{0,4},{1,5},{2,6},{3,7},{4,0},{5,1},{6,2},{7,3},{8,12},{9,13},{10,... | collective-permute-start | bytes 344072 | tf_op jit(solution)/shard_map/ppermute | solution.py:438
  46.4 9.0 %collective-permute-start.18 = (bf16[448,128]{1,0:T(8,128)(2,1)S(1)}, bf16[448,128]{1,0:T(8,128)(2,1)S(1)}, u32[]{:S(2)}, u32[]{:S(2)}) collective-permute-start(bf16[448,128]{1,0:T(8,128)(2,1)S(1)} %shard_map.87.own_ref), channel_id=1, source_target_pairs={{0,2},{1,3},{2,4},{3,5},{4,6},{5,7},{6,0},{7,1},{8,10},{9,11},{10,... | collective-permute-start | bytes 344072 | tf_op jit(solution)/shard_map/ppermute | solution.py:438
  55.9 4.5 %collective-permute-start.19 = (bf16[448,128]{1,0:T(8,128)(2,1)S(1)}, bf16[448,128]{1,0:T(8,128)(2,1)S(1)}, u32[]{:S(2)}, u32[]{:S(2)}) collective-permute-start(bf16[448,128]{1,0:T(8,128)(2,1)S(1)} %shard_map.88.own_ref.piece_ref), channel_id=1, source_target_pairs={{0,8},{1,9},{2,10},{3,11},{4,12},{5,13},{6,14},{7,15},{8,0},{9,1},... | collective-permute-start | bytes 344072 | tf_op jit(solution)/shard_map/ppermute | solution.py:471
  57.7 6.5 %collective-permute-start.12 = (bf16[32,2176]{1,0:T(8,128)(2,1)S(1)}, bf16[32,2176]{1,0:T(8,128)(2,1)S(1)}, u32[]{:S(2)}, u32[]{:S(2)}) collective-permute-start(bf16[32,2176]{1,0:T(8,128)(2,1)S(1)} %get-tuple-element.36), channel_id=1, source_target_pairs={{0,16},{16,0},{32,48},{48,32},{64,80},{80,64},{96,112},{112,96},{1... | collective-permute-start | bytes 417800 | tf_op jit(solution)/shard_map/ppermute | solution.py:457
  59.4 4.8 %collective-permute-start.9 = (bf16[32,2176]{1,0:T(8,128)(2,1)S(1)}, bf16[32,2176]{1,0:T(8,128)(2,1)S(1)}, u32[]{:S(2)}, u32[]{:S(2)}) collective-permute-start(bf16[32,2176]{1,0:T(8,128)(2,1)S(1)} %get-tuple-element.34), channel_id=1, source_target_pairs={{0,32},{16,48},{32,0},{48,16},{64,96},{80,112},{96,64},{112,80},{1... | collective-permute-start | bytes 417800 | tf_op jit(solution)/shard_map/ppermute | solution.py:426
  59.5 6.4 %collective-permute-start.21 = (bf16[448,128]{1,0:T(8,128)(2,1)S(1)}, bf16[448,128]{1,0:T(8,128)(2,1)S(1)}, u32[]{:S(2)}, u32[]{:S(2)}) collective-permute-start(bf16[448,128]{1,0:T(8,128)(2,1)S(1)} %shard_map.88.own_ref.piece_ref), channel_id=1, source_target_pairs={{0,1},{1,0},{2,3},{3,2},{4,5},{5,4},{6,7},{7,6},{8,9},{9,8},{10,11... | collective-permute-start | bytes 344072 | tf_op jit(solution)/shard_map/ppermute | solution.py:472
  60.4 6.7 %collective-permute-start.20 = (bf16[448,128]{1,0:T(8,128)(2,1)S(1)}, bf16[448,128]{1,0:T(8,128)(2,1)S(1)}, u32[]{:S(2)}, u32[]{:S(2)}) collective-permute-start(bf16[448,128]{1,0:T(8,128)(2,1)S(1)} %collective-permute-done.19.own_ref), channel_id=1, source_target_pairs={{0,1},{1,0},{2,3},{3,2},{4,5},{5,4},{6,7},{7,6},{8,9},{9,8},{10,11... | collective-permute-start | bytes 344072 | tf_op jit(solution)/shard_map/ppermute | solution.py:473

commit v8 on v7

--- a/solution.py
+++ b/solution.py
@@ -101,21 +101,21 @@
 
 def forward_kernel(xs_ref, wa_ref, wb_ref, mine_ref, first_ref, send_ref):
     rhs = jnp.concatenate([xs_ref[0, :TAPS, :], xs_ref[1, :TAPS, :]], axis=0)
-    parts = []
-    for kh in range(3):
-        lhs = jnp.concatenate(
-            [w[(kd * 3 + kh) * 96 : (kd * 3 + kh) * 96 + 96, :] for w in (wa_ref, wb_ref) for kd in range(3)],
-            axis=0,
-        )
-        parts.append(
-            lax.dot_general(lhs, rhs, (((0,), (0,)), ((), ())), preferred_element_type=F32)
-        )
-    lane = lanes((128, PLANE))
-    total = (
-        parts[1]
-        + jnp.where(lane < WIDE, 0.0, pltpu.roll(parts[0], WIDE, 1))
-        + jnp.where(lane >= PLANE - WIDE, 0.0, pltpu.roll(parts[2], PLANE - WIDE, 1))
-    )
+    lhs = jnp.concatenate(
+        [
+            jnp.concatenate(
+                [w[(kd * 3 + kh) * 96 : (kd * 3 + kh) * 96 + 96, :] for w in (wa_ref, wb_ref) for kd in range(3)],
+                axis=0,
+            )
+            for kh in range(3)
+        ],
+        axis=1,
+    )
+    got = lax.dot_general(lhs, rhs, (((0,), (0,)), ((), ())), preferred_element_type=F32)
+    parts = [got[kh * 128 : kh * 128 + 128] for kh in range(3)]
+    high = (lanes((128, PLANE)) & 127) >= WIDE
+    later, earlier = beside_tiles(parts[0])[0], beside_tiles(parts[2])[1]
+    total = parts[1] + half_turn(jnp.where(high, later + parts[2], parts[0] + earlier))
     even = ((lax.axis_index("filt") // 2) & 1) == 0
     near, across, far = (total[r * 32 : r * 32 + 32] for r in (1, 2, 3))
     mine_ref[...] = total[:32]
@@ -123,12 +123,25 @@
     write_rows(send_ref, jnp.concatenate([jnp.where(even, far, near), across], axis=0))
 
 
+def half_turn(wide):
+    return jnp.concatenate(
+        [pltpu.roll(wide[:, at : at + 128], WIDE, 1) for at in range(0, PLANE, 128)], axis=1
+    )
+
+
+def beside_tiles(wide):
+    none = jnp.zeros((wide.shape[0], 128), wide.dtype)
+    return (
+        jnp.concatenate([none, wide[:, :-128]], axis=1),
+        jnp.concatenate([wide[:, 128:], none], axis=1),
+    )
+
+
 def row_shifts(wide):
-    lane = lanes(wide.shape)
-    turned = pltpu.roll(wide, PLANE - WIDE, 1)
-    up = jnp.where(lane >= PLANE - WIDE, 0.0, turned)
-    down = jnp.where(lane < WIDE, 0.0, pltpu.roll(wide, WIDE, 1))
-    return up.astype(BF), wide.astype(BF), down.astype(BF)
+    low = (lanes(wide.shape) & 127) < WIDE
+    turned = half_turn(wide)
+    later, earlier = beside_tiles(turned)
+    return jnp.where(low, turned, earlier), wide, jnp.where(low, later, turned)
 
 
 def beside():
@@ -138,13 +151,12 @@
 
 
 def kernel_grad_kernel(chip_ref, here_ref, far_ref, c0, c1, c2, c3, xs_ref, keep_ref, send_ref, cs_ref):
-    core = lax.axis_index("space") & 1
     col = columns((64, PLANE))
     inside, even = beside()
     for ref, kd in ((chip_ref, jnp.where(even, 2, 0)), (here_ref, 1), (far_ref, jnp.where(even, 0, 2))):
-        wide = ref[...].astype(F32)
+        wide = ref[...]
         if ref is far_ref:
-            wide = wide * inside
+            wide = wide * inside.astype(BF)
         left = jnp.where(col == 0, 0.0, pltpu.roll(wide, 1, 1))
         right = jnp.where(col == WIDE - 1, 0.0, pltpu.roll(wide, PLANE - 1, 1))
         for kw, part in enumerate((left, wide, right)):
@@ -154,15 +166,19 @@
             xs_ref[1, rows, :] = narrow[OWN:]
     xs_ref[:, TAPS:, :] = jnp.ones((2, 16, PLANE), BF)
     for r, ref in enumerate((c0, c1, c2, c3)):
-        for kh, part in enumerate(row_shifts(ref[...].astype(F32))):
+        for kh, part in enumerate(row_shifts(ref[...])):
             cs_ref[kh * 128 + r * 32 : kh * 128 + r * 32 + 32, :] = part
-    for slot, ref in enumerate((keep_ref, send_ref)):
-        got = lax.dot_general(
-            xs_ref[core ^ slot], cs_ref[...], (((1,), (1,)), ((), ())), preferred_element_type=F32
-        )
+    got = lax.dot_general(
+        xs_ref[...].reshape(2 * (TAPS + 16), PLANE),
+        cs_ref[...],
+        (((1,), (1,)), ((), ())),
+        preferred_element_type=F32,
+    )
+    first, second = got[: TAPS + 16], got[TAPS + 16 :]
+    for ref, half in ((keep_ref, jnp.where(even, first, second)), (send_ref, jnp.where(even, second, first))):
         for kh in range(3):
-            ref[kh * TAPS : (kh + 1) * TAPS, :] = got[:TAPS, kh * 128 : kh * 128 + 128]
-        ref[HALF:, :] = got[TAPS : TAPS + 8, 128:256]
+            ref[kh * TAPS : (kh + 1) * TAPS, :] = half[:TAPS, kh * 128 : kh * 128 + 128]
+        ref[HALF:, :] = half[TAPS : TAPS + 8, 128:256]
 
 
 def input_grad_kernel(chip_ref, far_ref, c0, c1, c2, c3, wa_ref, wb_ref, mine_ref, theirs_ref, cs_ref):
@@ -170,9 +186,9 @@
     for r, ref in enumerate((c0, c1, c2, c3)):
         rows = slice(r * 32, r * 32 + 32)
         planes = (
-            chip_ref[rows, :].astype(F32),
-            ref[...].astype(F32),
-            far_ref[rows, :].astype(F32) * inside,
+            chip_ref[rows, :],
+            ref[...],
+            far_ref[rows, :] * inside.astype(BF),
         )
         for kd, wide in enumerate(planes):
             for kh, part in enumerate(row_shifts(wide)):
@@ -211,7 +227,7 @@
 def encode(wide):
     size = jnp.abs(wide)
     scale = jnp.max(jnp.max(size, axis=1, keepdims=True), axis=0, keepdims=True)
-    scale = jnp.maximum(scale, 1e-30).astype(BF).astype(F32)
+    scale = jnp.maximum(scale, 1e-37).astype(BF).astype(F32)
     coded = jnp.exp2(jnp.log2(size * (1.0 / scale)) * POWER + TOP)
     return jnp.where(wide < 0, -coded, coded).astype(BF), scale
 
@@ -323,12 +339,21 @@
     return bias[:, :OWN], copies
 
 
-def first_kernel(own_ref, piece_ref, got_ref, grad_hbm, bias_hbm, rows_ref, sems, bias_ref, bias_sem):
+def first_kernel(
+    own_ref, piece_ref, got_ref, sum_ref, sum_got_ref, wide_ref, near_ref, theirs_ref,
+    grad_hbm, bias_hbm, out_hbm, gin_hbm, rows_ref, sems, bias_ref, out_ref, gin_ref, more,
+):
     bias, copies = write_half(0, own_ref, got_ref, grad_hbm, rows_ref, sems)
     core = lax.axis_index("space") & 1
     own_bias = read_tail(piece_ref[PIECE:CODED, :].astype(F32))[:, :OWN]
     bias_ref[...] = jnp.where(core == 0, own_bias, bias)
-    copies.append(pltpu.make_async_copy(bias_ref, bias_hbm, bias_sem))
+    copies.append(pltpu.make_async_copy(bias_ref, bias_hbm, more.at[0]))
+    copies[-1].start()
+    out_ref[...] = sum_ref[...] + read_rows(sum_got_ref[...]) + wide_ref[...]
+    copies.append(pltpu.make_async_copy(out_ref, out_hbm, more.at[1]))
+    copies[-1].start()
+    gin_ref[...] = near_ref[...] + read_rows(theirs_ref[...])
+    copies.append(pltpu.make_async_copy(gin_ref, gin_hbm, more.at[2]))
     copies[-1].start()
     for copy in copies:
         copy.wait()
@@ -353,19 +378,6 @@
     got = read_rows(got_ref[...])
     sum_ref[...] = mine_ref[...] + got[:OWN]
     write_rows(send_ref, first_ref[...] + got[OWN:])
-
-
-def sums_kernel(mine_ref, got_ref, bias_ref, near_ref, theirs_ref, out_hbm, grad_hbm, out_ref, grad_ref, sems):
-    copies = [
-        pltpu.make_async_copy(out_ref, out_hbm, sems.at[0]),
-        pltpu.make_async_copy(grad_ref, grad_hbm, sems.at[1]),
-    ]
-    out_ref[...] = mine_ref[...] + read_rows(got_ref[...]) + bias_ref[...]
-    copies[0].start()
-    grad_ref[...] = near_ref[...] + read_rows(theirs_ref[...])
-    copies[1].start()
-    for copy in copies:
-        copy.wait()
 
 
 def call(kernel, outs, *args, scratch=(), space=VM, out_space=VM, over=None):
@@ -455,19 +467,6 @@
         scratch=[pltpu.VMEM((9 * 128, PLANE), BF)],
     )
     g_other = lax.ppermute(g_theirs, "filt", ACROSS)
-    wide = [((OWN, PLANE), F32)] * 2
-    output, grad_inputs = call(
-        sums_kernel,
-        wide,
-        o_sum,
-        o_got,
-        wide_bias,
-        g_mine,
-        g_other,
-        scratch=[pltpu.VMEM(*v) for v in wide] + [pltpu.SemaphoreType.DMA((2,))],
-        out_space=pl.BlockSpec(memory_space=pltpu.HBM),
-    )
-
     piece_far = lax.ppermute(piece, "space", XLO)
     got_near = lax.ppermute(piece, "space", CORE)
     got_far = lax.ppermute(piece_far, "space", CORE)
@@ -477,13 +476,20 @@
     grad = ((9, 96, 256), F32)
     scratch = [pltpu.VMEM((PIECE, 256), F32), pltpu.SemaphoreType.DMA((5,))]
     hbm = pl.BlockSpec(memory_space=pltpu.HBM)
-    half_done, grad_bias = call(
+    half_done, grad_bias, output, grad_inputs = call(
         first_kernel,
-        [grad, ((1, OWN), F32)],
+        [grad, ((1, OWN), F32), ((OWN, PLANE), F32), ((OWN, PLANE), F32)],
         mine,
         piece,
         got_near,
-        scratch=scratch + [pltpu.VMEM((1, OWN), F32), pltpu.SemaphoreType.DMA],
+        o_sum,
+        o_got,
+        wide_bias,
+        g_mine,
+        g_other,
+        scratch=scratch
+        + [pltpu.VMEM(shape, F32) for shape in ((1, OWN), (OWN, PLANE), (OWN, PLANE))]
+        + [pltpu.SemaphoreType.DMA((3,))],
         out_space=hbm,
     )
     (grad_weight,) = call(

time: 68.7 us -> 66.6 us (0.969)
  waiting for transfers between devices: 24.7 us -> 23.4 us
  Pallas kernels: 12.5 us -> 11.5 us
    ppermute x1, waiting for transfers between devices: 2.48 us -> 1.34 us  [step(): g_other = lax.ppermute(g_theirs, 'filt', ACROSS)]
    pallas_call x18 -> x17, Pallas kernels: 12.5 us -> 11.5 us  [call(): pl.pallas_call(kernel, out_shape=[jax.ShapeDtypeStruct(s, d) for s, d in...]
  transfers between devices with their start and end apart: 22 -> 22, of which waited for: 9 -> 9; matrix products, arithmetic and copies ran while one was open for 0% -> 0% of each run, Pallas kernels for 14% -> 13%
where the time goes in v8:
time: 66.6 us; the launch traced here: 66.2 us
  starting transfers between devices  30.4 us (46%)
  waiting for transfers between devices  23.4 us (35%)
  Pallas kernels  11.5 us (17%)
  between operations  0.79 us (1%)
    pallas_call x17, Pallas kernels, call(): pl.pallas_call(kernel, out_shape=[jax.ShapeDtypeStruct(s, d) for s, d in...  11.5 us
    ppermute x3, waiting for transfers between devices, step(): c1, c3, c2 = (lax.ppermute(c_own, 'filt', along_z(-r)) for r in (1, 3, 2))  8.56 us
    ppermute x3, waiting for transfers between devices, step(): y1, y3, y2 = (lax.ppermute(mine_y, 'space', along_y(-r)) for r in (1, 3, 2))  8.29 us
    ppermute x3, starting transfers between devices, step(): y1, y3, y2 = (lax.ppermute(mine_y, 'space', along_y(-r)) for r in (1, 3, 2))  6.31 us
    ppermute x3, starting transfers between devices, step(): c1, c3, c2 = (lax.ppermute(c_own, 'filt', along_z(-r)) for r in (1, 3, 2))  4.46 us
    ppermute x1, starting transfers between devices, step(): x_other = lax.ppermute(x_own, 'filt', ACROSS)  3.64 us
    ppermute x1, waiting for transfers between devices, step(): r_near = lax.ppermute(r_cross, ('filt', 'space'), crossing(0, 2))  3.29 us
    ppermute x1, starting transfers between devices, step(): w_half = lax.ppermute(w_theirs, 'filt', ACROSS)  2.75 us
  transfers between devices with their start and end apart: 22, of which 9 were waited for; matrix products, arithmetic and copies ran while one was open for 0% of the time, Pallas kernels for 13%

profile of v8, /device:TPU:1, one launch (start us, length us, event | category | flops | bytes accessed | tf_op | source)
XLA Modules:
  0.0 66.2 jit_solution(10432679760939027896)
XLA Ops:
  0.6 3.6 %collective-permute-start = (bf16[32,2048]{1,0:T(8,128)(2,1)}, bf16[32,2048]{1,0:T(8,128)(2,1)S(1)}, u32[]{:S(2)}, u32[]{:S(2)}) collective-permute-start(bf16[32,2048]{1,0:T(8,128)(2,1)} %bitcast.11), channel_id=1, source_target_pairs={{0,16},{16,0},{32,48},{48,32},{64,80},{80,64},{96,112},{112,96},{1... | collective-permute-start | bytes 393224 | tf_op jit(solution)/shard_map/ppermute | solution.py:399
  4.3 1.4 %shard_map.75 = (bf16[864,128]{1,0:T(8,128)(2,1)S(1)}, bf16[480,128]{1,0:T(8,128)(2,1)S(1)}, bf16[32,2048]{1,0:T(8,128)(2,1)S(1)}, bf16[32,2048]{1,0:T(8,128)(2,1)S(1)}) custom-call(bf16[864,256]{1,0:T(8,128)(2,1)} %bitcast.10, bf16[32,2048]{1,0:T(8,128)(2,1)} %bitcast.12, bf16[32,2048]{1,0:T(8,128)(2,1)} %bitcast.13), custom_call_target="tpu_custom_call" | custom-call | tf_op jit(solution)/shard_map/pallas_call | solution.py:384
  5.7 1.6 %collective-permute-done.refs_1_ = bf16[32,2048]{1,0:T(8,128)(2,1)S(1)} collective-permute-done((bf16[32,2048]{1,0:T(8,128)(2,1)}, bf16[32,2048]{1,0:T(8,128)(2,1)S(1)}, u32[]{:S(2)}, u32[]{:S(2)}) %collective-permute-start) | collective-permute-done | bytes 131104 | tf_op jit(solution)/shard_map/ppermute | solution.py:399
  7.3 1.7 %collective-permute-start.1 = (bf16[64,2048]{1,0:T(8,128)(2,1)S(1)}, bf16[64,2048]{1,0:T(8,128)(2,1)S(1)}, u32[]{:S(2)}, u32[]{:S(2)}) collective-permute-start(bf16[64,2048]{1,0:T(8,128)(2,1)S(1)} %shard_map.76.here_ref), channel_id=1, source_target_pairs={{0,1},{1,0},{2,3},{3,2},{4,5},{5,4},{6,7},{7,6},{8,9},{9,8},{10,11... | collective-permute-start | bytes 786440 | tf_op jit(solution)/shard_map/ppermute | solution.py:414
  9.0 1.5 %collective-permute-start.2 = (bf16[64,2048]{1,0:T(8,128)(2,1)S(1)}, bf16[64,2048]{1,0:T(8,128)(2,1)S(1)}, u32[]{:S(2)}, u32[]{:S(2)}) collective-permute-start(bf16[64,2048]{1,0:T(8,128)(2,1)S(1)} %shard_map.76.here_ref), channel_id=1, source_target_pairs={{0,32},{1,2},{2,1},{3,4},{4,3},{5,6},{6,5},{7,8},{8,7},{9,10},{10,... | collective-permute-start | bytes 786440 | tf_op jit(solution)/shard_map/ppermute | solution.py:415
  10.5 3.8 %collective-permute-start.3 = (bf16[32,2048]{1,0:T(8,128)(2,1)}, bf16[32,2048]{1,0:T(8,128)(2,1)S(1)}, u32[]{:S(2)}, u32[]{:S(2)}) collective-permute-start(bf16[32,2048]{1,0:T(8,128)(2,1)} %bitcast.14), channel_id=1, source_target_pairs={{0,96},{16,112},{32,0},{48,16},{64,32},{80,48},{96,64},{112,80},{1... | collective-permute-start | bytes 393224 | tf_op jit(solution)/shard_map/ppermute | solution.py:400
  14.3 0.7 %collective-permute-start.5 = (bf16[32,2048]{1,0:T(8,128)(2,1)}, bf16[32,2048]{1,0:T(8,128)(2,1)S(1)}, u32[]{:S(2)}, u32[]{:S(2)}) collective-permute-start(bf16[32,2048]{1,0:T(8,128)(2,1)} %bitcast.16), channel_id=1, source_target_pairs={{0,32},{16,48},{32,64},{48,80},{64,96},{80,112},{96,0},{112,16},{1... | collective-permute-start | bytes 393224 | tf_op jit(solution)/shard_map/ppermute | solution.py:400
  15.0 5.5 %collective-permute-done.3.c1.refs_1_ = bf16[32,2048]{1,0:T(8,128)(2,1)S(1)} collective-permute-done((bf16[32,2048]{1,0:T(8,128)(2,1)}, bf16[32,2048]{1,0:T(8,128)(2,1)S(1)}, u32[]{:S(2)}, u32[]{:S(2)}) %collective-permute-start.3) | collective-permute-done | bytes 131104 | tf_op jit(solution)/shard_map/ppermute | solution.py:400
  20.4 1.1 %collective-permute-done.4.c2.refs_2_ = bf16[32,2048]{1,0:T(8,128)(2,1)S(1)} collective-permute-done((bf16[32,2048]{1,0:T(8,128)(2,1)}, bf16[32,2048]{1,0:T(8,128)(2,1)S(1)}, u32[]{:S(2)}, u32[]{:S(2)}) %collective-permute-start.4) | collective-permute-done | bytes 131104 | tf_op jit(solution)/shard_map/ppermute | solution.py:400
  21.6 2.0 %collective-permute-done.5.c3.refs_3_ = bf16[32,2048]{1,0:T(8,128)(2,1)S(1)} collective-permute-done((bf16[32,2048]{1,0:T(8,128)(2,1)}, bf16[32,2048]{1,0:T(8,128)(2,1)S(1)}, u32[]{:S(2)}, u32[]{:S(2)}) %collective-permute-start.5) | collective-permute-done | bytes 131104 | tf_op jit(solution)/shard_map/ppermute | solution.py:400
  23.6 1.8 %shard_map.77 = (bf16[2,304,2048]{2,1,0:T(8,128)(2,1)S(1)}, f32[872,128]{1,0:T(8,128)S(1)}, f32[872,128]{1,0:T(8,128)S(1)}) custom-call(bf16[64,2048]{1,0:T(8,128)(2,1)S(1)} %collective-permute-done.1.chip_ref, bf16[64,2048]{1,0:T(8,128)(2,1)S(1)} %shard_map.76.here_ref, bf16[64,2048]{1,0:T(8,128)(2,1)S(1)} %collective-permute-done.2.far_ref, ...), custom_call_target="tpu_custom_call" | custom-call | tf_op jit(solution)/shard_map/pallas_call | solution.py:384
  25.3 1.0 %collective-permute-start.6 = (f32[872,128]{1,0:T(8,128)S(1)}, f32[872,128]{1,0:T(8,128)S(1)}, u32[]{:S(2)}, u32[]{:S(2)}) collective-permute-start(f32[872,128]{1,0:T(8,128)S(1)} %get-tuple-element.28), channel_id=1, source_target_pairs={{0,1},{1,0},{2,3},{3,2},{4,5},{5,4},{6,7},{7,6},{8,9},{9,8},{10,11... | collective-permute-start | bytes 1339400 | tf_op jit(solution)/shard_map/ppermute | solution.py:426
  26.3 2.7 %collective-permute-start.13 = (bf16[480,128]{1,0:T(8,128)(2,1)S(1)}, bf16[480,128]{1,0:T(8,128)(2,1)S(1)}, u32[]{:S(2)}, u32[]{:S(2)}) collective-permute-start(bf16[480,128]{1,0:T(8,128)(2,1)S(1)} %get-tuple-element.34), channel_id=1, source_target_pairs={{0,16},{16,0},{32,48},{48,32},{64,80},{80,64},{96,112},{112,96},{1... | collective-permute-start | bytes 368648 | tf_op jit(solution)/shard_map/ppermute | solution.py:408
  29.1 0.5 collective-permute-start.17
  29.5 1.3 %collective-permute-start.18 = (bf16[128,2048]{1,0:T(8,128)(2,1)S(1)}, bf16[128,2048]{1,0:T(8,128)(2,1)S(1)}, u32[]{:S(2)}, u32[]{:S(2)}) collective-permute-start(bf16[128,2048]{1,0:T(8,128)(2,1)S(1)} %shard_map.87), channel_id=1, source_target_pairs={{0,32},{1,2},{2,1},{3,4},{4,3},{5,6},{6,5},{7,8},{8,7},{9,10},{10,... | collective-permute-start | bytes 1572872 | tf_op jit(solution)/shard_map/ppermute | solution.py:447
  31.5 2.5 %collective-permute-start.8 = (bf16[448,128]{1,0:T(8,128)(2,1)S(1)}, bf16[448,128]{1,0:T(8,128)(2,1)S(1)}, u32[]{:S(2)}, u32[]{:S(2)}) collective-permute-start(bf16[448,128]{1,0:T(8,128)(2,1)S(1)} %get-tuple-element.31), channel_id=1, source_target_pairs={{0,8},{1,25},{2,10},{3,27},{4,12},{5,29},{6,14},{7,31},{8,0},{9,17... | collective-permute-start | bytes 344072 | tf_op jit(solution)/shard_map/ppermute | solution.py:444
  34.0 3.3 %collective-permute-done.7.near_ref = bf16[448,128]{1,0:T(8,128)(2,1)S(1)} collective-permute-done((bf16[448,128]{1,0:T(8,128)(2,1)S(1)}, bf16[448,128]{1,0:T(8,128)(2,1)S(1)}, u32[]{:S(2)}, u32[]{:S(2)}) %collective-permute-start.7) | collective-permute-done | bytes 114720 | tf_op jit(solution)/shard_map/ppermute | solution.py:445
  38.0 5.7 %collective-permute-start.9 = (bf16[448,128]{1,0:T(8,128)(2,1)S(1)}, bf16[448,128]{1,0:T(8,128)(2,1)S(1)}, u32[]{:S(2)}, u32[]{:S(2)}) collective-permute-start(bf16[448,128]{1,0:T(8,128)(2,1)S(1)} %shard_map.79.own_ref), channel_id=1, source_target_pairs={{0,6},{1,7},{2,0},{3,1},{4,2},{5,3},{6,4},{7,5},{8,14},{9,15},{10,... | collective-permute-start | bytes 344072 | tf_op jit(solution)/shard_map/ppermute | solution.py:450
  43.7 1.8 %shard_map.83 = (f32[32,2048]{1,0:T(8,128)S(1)}, f32[32,2048]{1,0:T(8,128)S(1)}, bf16[64,2176]{1,0:T(8,128)(2,1)S(1)}) custom-call(bf16[2,304,2048]{2,1,0:T(8,128)(2,1)S(1)} %get-tuple-element.32.xs_ref, bf16[864,128]{1,0:T(8,128)(2,1)S(1)} %get-tuple-element.33.wa_ref, bf16[864,128]{1,0:T(8,128)(2,1)S(1)} %shard_map.82.wb_ref), custom_call_target="tpu_custom_call" | custom-call | tf_op jit(solution)/shard_map/pallas_call | solution.py:384
  45.6 0.7 %collective-permute-start.15 = (bf16[64,2176]{1,0:T(8,128)(2,1)S(1)}, bf16[64,2176]{1,0:T(8,128)(2,1)S(1)}, u32[]{:S(2)}, u32[]{:S(2)}) collective-permute-start(bf16[64,2176]{1,0:T(8,128)(2,1)S(1)} %get-tuple-element.37), channel_id=1, source_target_pairs={{0,96},{16,112},{32,64},{48,80},{64,32},{80,48},{96,0},{112,16},{1... | collective-permute-start | bytes 835592 | tf_op jit(solution)/shard_map/ppermute | solution.py:434
  46.3 0.6 collective-permute-start.11
  46.9 6.0 %collective-permute-done.10.y2_ref = bf16[448,128]{1,0:T(8,128)(2,1)S(1)} collective-permute-done((bf16[448,128]{1,0:T(8,128)(2,1)S(1)}, bf16[448,128]{1,0:T(8,128)(2,1)S(1)}, u32[]{:S(2)}, u32[]{:S(2)}) %collective-permute-start.10) | collective-permute-done | bytes 114720 | tf_op jit(solution)/shard_map/ppermute | solution.py:450
  52.9 2.2 %collective-permute-done.11.y3_ref = bf16[448,128]{1,0:T(8,128)(2,1)S(1)} collective-permute-done((bf16[448,128]{1,0:T(8,128)(2,1)S(1)}, bf16[448,128]{1,0:T(8,128)(2,1)S(1)}, u32[]{:S(2)}, u32[]{:S(2)}) %collective-permute-start.11) | collective-permute-done | bytes 114720 | tf_op jit(solution)/shard_map/ppermute | solution.py:450
  55.1 0.6 shard_map.80.own_ref.piece_ref
  55.8 1.6 %shard_map.88 = (f32[32,2048]{1,0:T(8,128)S(1)}, bf16[32,2176]{1,0:T(8,128)(2,1)S(1)}) custom-call(bf16[128,2048]{1,0:T(8,128)(2,1)S(1)} %collective-permute-done.17.chip_ref, bf16[128,2048]{1,0:T(8,128)(2,1)S(1)} %collective-permute-done.18.far_ref, bf16[32,2048]{1,0:T(8,128)(2,1)S(1)} %get-tuple-element.26.c0.refs_0_, ...), custom_call_target="tpu_custom_call" | custom-call | tf_op jit(solution)/shard_map/pallas_call | solution.py:384
  57.4 1.2 %collective-permute-start.19 = (bf16[32,2176]{1,0:T(8,128)(2,1)S(1)}, bf16[32,2176]{1,0:T(8,128)(2,1)S(1)}, u32[]{:S(2)}, u32[]{:S(2)}) collective-permute-start(bf16[32,2176]{1,0:T(8,128)(2,1)S(1)} %get-tuple-element.41), channel_id=1, source_target_pairs={{0,16},{16,0},{32,48},{48,32},{64,80},{80,64},{96,112},{112,96},{1... | collective-permute-start | bytes 417800 | tf_op jit(solution)/shard_map/ppermute | solution.py:469
  58.7 0.4 shard_map.84
  59.1 0.9 %collective-permute-start.12 = (bf16[448,128]{1,0:T(8,128)(2,1)S(1)}, bf16[448,128]{1,0:T(8,128)(2,1)S(1)}, u32[]{:S(2)}, u32[]{:S(2)}) collective-permute-start(bf16[448,128]{1,0:T(8,128)(2,1)S(1)} %shard_map.80.own_ref.piece_ref), channel_id=1, source_target_pairs={{0,1},{1,0},{2,3},{3,2},{4,5},{5,4},{6,7},{7,6},{8,9},{9,8},{10,11... | collective-permute-start | bytes 344072 | tf_op jit(solution)/shard_map/ppermute | solution.py:471
  60.1 1.5 %collective-permute-start.21 = (bf16[448,128]{1,0:T(8,128)(2,1)S(1)}, bf16[448,128]{1,0:T(8,128)(2,1)S(1)}, u32[]{:S(2)}, u32[]{:S(2)}) collective-permute-start(bf16[448,128]{1,0:T(8,128)(2,1)S(1)} %collective-permute-done.20.own_ref), channel_id=1, source_target_pairs={{0,1},{1,0},{2,3},{3,2},{4,5},{5,4},{6,7},{7,6},{8,9},{9,8},{10,11... | collective-permute-start | bytes 344072 | tf_op jit(solution)/shard_map/ppermute | solution.py:472
  62.4 1.3 %collective-permute-done.19.theirs_ref = bf16[32,2176]{1,0:T(8,128)(2,1)S(1)} collective-permute-done((bf16[32,2176]{1,0:T(8,128)(2,1)S(1)}, bf16[32,2176]{1,0:T(8,128)(2,1)S(1)}, u32[]{:S(2)}, u32[]{:S(2)}) %collective-permute-start.19) | collective-permute-done | bytes 139296 | tf_op jit(solution)/shard_map/ppermute | solution.py:469
  63.7 1.4 %shard_map.89 = (f32[9,96,256]{2,1,0:T(8,128)}, f32[1,32]{1,0:T(1,128)}, f32[32,2048]{1,0:T(8,128)}, f32[32,2048]{1,0:T(8,128)}) custom-call(f32[432,256]{1,0:T(8,128)S(1)} %shard_map.81.own_ref, bf16[448,128]{1,0:T(8,128)(2,1)S(1)} %shard_map.80.own_ref.piece_ref, bf16[448,128]{1,0:T(8,128)(2,1)S(1)} %collective-permute-done.12.got_ref, ...), custom_call_target="tpu_custom_call" | custom-call | tf_op jit(solution)/shard_map/pallas_call | solution.py:384
  65.1 1.1 %shard_map.91 = f32[9,96,256]{2,1,0:T(8,128)} custom-call(f32[432,256]{1,0:T(8,128)S(1)} %shard_map.90.own_ref, bf16[448,128]{1,0:T(8,128)(2,1)S(1)} %collective-permute-done.21.got_ref, f32[9,96,256]{2,1,0:T(8,128)} %get-tuple-element.44._), custom_call_target="tpu_custom_call", output_to_operand_aliasing={{}: (2, {})} | custom-call | tf_op jit(solution)/shard_map/pallas_call | solution.py:384
  (31 shorter events, 2.4 us)
Async XLA Ops:
  0.6 6.7 %collective-permute-start = (bf16[32,2048]{1,0:T(8,128)(2,1)}, bf16[32,2048]{1,0:T(8,128)(2,1)S(1)}, u32[]{:S(2)}, u32[]{:S(2)}) collective-permute-start(bf16[32,2048]{1,0:T(8,128)(2,1)} %bitcast.11), channel_id=1, source_target_pairs={{0,16},{16,0},{32,48},{48,32},{64,80},{80,64},{96,112},{112,96},{1... | collective-permute-start | bytes 393224 | tf_op jit(solution)/shard_map/ppermute | solution.py:399
  7.3 16.2 %collective-permute-start.1 = (bf16[64,2048]{1,0:T(8,128)(2,1)S(1)}, bf16[64,2048]{1,0:T(8,128)(2,1)S(1)}, u32[]{:S(2)}, u32[]{:S(2)}) collective-permute-start(bf16[64,2048]{1,0:T(8,128)(2,1)S(1)} %shard_map.76.here_ref), channel_id=1, source_target_pairs={{0,1},{1,0},{2,3},{3,2},{4,5},{5,4},{6,7},{7,6},{8,9},{9,8},{10,11... | collective-permute-start | bytes 786440 | tf_op jit(solution)/shard_map/ppermute | solution.py:414
  9.0 14.5 %collective-permute-start.2 = (bf16[64,2048]{1,0:T(8,128)(2,1)S(1)}, bf16[64,2048]{1,0:T(8,128)(2,1)S(1)}, u32[]{:S(2)}, u32[]{:S(2)}) collective-permute-start(bf16[64,2048]{1,0:T(8,128)(2,1)S(1)} %shard_map.76.here_ref), channel_id=1, source_target_pairs={{0,32},{1,2},{2,1},{3,4},{4,3},{5,6},{6,5},{7,8},{8,7},{9,10},{10,... | collective-permute-start | bytes 786440 | tf_op jit(solution)/shard_map/ppermute | solution.py:415
  10.5 9.9 %collective-permute-start.3 = (bf16[32,2048]{1,0:T(8,128)(2,1)}, bf16[32,2048]{1,0:T(8,128)(2,1)S(1)}, u32[]{:S(2)}, u32[]{:S(2)}) collective-permute-start(bf16[32,2048]{1,0:T(8,128)(2,1)} %bitcast.14), channel_id=1, source_target_pairs={{0,96},{16,112},{32,0},{48,16},{64,32},{80,48},{96,64},{112,80},{1... | collective-permute-start | bytes 393224 | tf_op jit(solution)/shard_map/ppermute | solution.py:400
  14.3 7.3 %collective-permute-start.4 = (bf16[32,2048]{1,0:T(8,128)(2,1)}, bf16[32,2048]{1,0:T(8,128)(2,1)S(1)}, u32[]{:S(2)}, u32[]{:S(2)}) collective-permute-start(bf16[32,2048]{1,0:T(8,128)(2,1)} %bitcast.15), channel_id=1, source_target_pairs={{0,64},{16,80},{32,96},{48,112},{64,0},{80,16},{96,32},{112,48},{1... | collective-permute-start | bytes 393224 | tf_op jit(solution)/shard_map/ppermute | solution.py:400
  14.3 9.3 %collective-permute-start.5 = (bf16[32,2048]{1,0:T(8,128)(2,1)}, bf16[32,2048]{1,0:T(8,128)(2,1)S(1)}, u32[]{:S(2)}, u32[]{:S(2)}) collective-permute-start(bf16[32,2048]{1,0:T(8,128)(2,1)} %bitcast.16), channel_id=1, source_target_pairs={{0,32},{16,48},{32,64},{48,80},{64,96},{80,112},{96,0},{112,16},{1... | collective-permute-start | bytes 393224 | tf_op jit(solution)/shard_map/ppermute | solution.py:400
  25.3 5.5 %collective-permute-start.6 = (f32[872,128]{1,0:T(8,128)S(1)}, f32[872,128]{1,0:T(8,128)S(1)}, u32[]{:S(2)}, u32[]{:S(2)}) collective-permute-start(f32[872,128]{1,0:T(8,128)S(1)} %get-tuple-element.28), channel_id=1, source_target_pairs={{0,1},{1,0},{2,3},{3,2},{4,5},{5,4},{6,7},{7,6},{8,9},{9,8},{10,11... | collective-permute-start | bytes 1339400 | tf_op jit(solution)/shard_map/ppermute | solution.py:426
  26.3 7.7 %collective-permute-start.13 = (bf16[480,128]{1,0:T(8,128)(2,1)S(1)}, bf16[480,128]{1,0:T(8,128)(2,1)S(1)}, u32[]{:S(2)}, u32[]{:S(2)}) collective-permute-start(bf16[480,128]{1,0:T(8,128)(2,1)S(1)} %get-tuple-element.34), channel_id=1, source_target_pairs={{0,16},{16,0},{32,48},{48,32},{64,80},{80,64},{96,112},{112,96},{1... | collective-permute-start | bytes 368648 | tf_op jit(solution)/shard_map/ppermute | solution.py:408
  29.1 26.7 %collective-permute-start.17 = (bf16[128,2048]{1,0:T(8,128)(2,1)S(1)}, bf16[128,2048]{1,0:T(8,128)(2,1)S(1)}, u32[]{:S(2)}, u32[]{:S(2)}) collective-permute-start(bf16[128,2048]{1,0:T(8,128)(2,1)S(1)} %shard_map.87), channel_id=1, source_target_pairs={{0,1},{1,0},{2,3},{3,2},{4,5},{5,4},{6,7},{7,6},{8,9},{9,8},{10,11... | collective-permute-start | bytes 1572872 | tf_op jit(solution)/shard_map/ppermute | solution.py:446
  29.5 26.3 %collective-permute-start.18 = (bf16[128,2048]{1,0:T(8,128)(2,1)S(1)}, bf16[128,2048]{1,0:T(8,128)(2,1)S(1)}, u32[]{:S(2)}, u32[]{:S(2)}) collective-permute-start(bf16[128,2048]{1,0:T(8,128)(2,1)S(1)} %shard_map.87), channel_id=1, source_target_pairs={{0,32},{1,2},{2,1},{3,4},{4,3},{5,6},{6,5},{7,8},{8,7},{9,10},{10,... | collective-permute-start | bytes 1572872 | tf_op jit(solution)/shard_map/ppermute | solution.py:447
  31.2 6.1 %collective-permute-start.7 = (bf16[448,128]{1,0:T(8,128)(2,1)S(1)}, bf16[448,128]{1,0:T(8,128)(2,1)S(1)}, u32[]{:S(2)}, u32[]{:S(2)}) collective-permute-start(bf16[448,128]{1,0:T(8,128)(2,1)S(1)} %get-tuple-element.30), channel_id=1, source_target_pairs={{0,2},{1,17},{2,0},{3,19},{4,6},{5,21},{6,4},{7,23},{8,10},{9,25},... | collective-permute-start | bytes 344072 | tf_op jit(solution)/shard_map/ppermute | solution.py:445
  31.5 6.1 %collective-permute-start.8 = (bf16[448,128]{1,0:T(8,128)(2,1)S(1)}, bf16[448,128]{1,0:T(8,128)(2,1)S(1)}, u32[]{:S(2)}, u32[]{:S(2)}) collective-permute-start(bf16[448,128]{1,0:T(8,128)(2,1)S(1)} %get-tuple-element.31), channel_id=1, source_target_pairs={{0,8},{1,25},{2,10},{3,27},{4,12},{5,29},{6,14},{7,31},{8,0},{9,17... | collective-permute-start | bytes 344072 | tf_op jit(solution)/shard_map/ppermute | solution.py:444
  34.0 9.7 %collective-permute-start.14 = (bf16[480,128]{1,0:T(8,128)(2,1)S(1)}, bf16[480,128]{1,0:T(8,128)(2,1)S(1)}, u32[]{:S(2)}, u32[]{:S(2)}) collective-permute-start(bf16[480,128]{1,0:T(8,128)(2,1)S(1)} %collective-permute-done.13.near_ref), channel_id=1, source_target_pairs={{0,1},{1,0},{2,3},{3,2},{4,5},{5,4},{6,7},{7,6},{8,9},{9,8},{10,11... | collective-permute-start | bytes 368648 | tf_op jit(solution)/shard_map/ppermute | solution.py:409
  38.0 8.3 %collective-permute-start.9 = (bf16[448,128]{1,0:T(8,128)(2,1)S(1)}, bf16[448,128]{1,0:T(8,128)(2,1)S(1)}, u32[]{:S(2)}, u32[]{:S(2)}) collective-permute-start(bf16[448,128]{1,0:T(8,128)(2,1)S(1)} %shard_map.79.own_ref), channel_id=1, source_target_pairs={{0,6},{1,7},{2,0},{3,1},{4,2},{5,3},{6,4},{7,5},{8,14},{9,15},{10,... | collective-permute-start | bytes 344072 | tf_op jit(solution)/shard_map/ppermute | solution.py:450
  43.7 17.9 %copy-start = (bf16[32]{0:T(256)(128)(2,1)S(1)}, bf16[32]{0:T(256)(128)(2,1)}, u32[]{:S(2)}) copy-start(bf16[32]{0:T(256)(128)(2,1)} %param.6) | copy-start | bytes 196
  45.6 13.1 %collective-permute-start.15 = (bf16[64,2176]{1,0:T(8,128)(2,1)S(1)}, bf16[64,2176]{1,0:T(8,128)(2,1)S(1)}, u32[]{:S(2)}, u32[]{:S(2)}) collective-permute-start(bf16[64,2176]{1,0:T(8,128)(2,1)S(1)} %get-tuple-element.37), channel_id=1, source_target_pairs={{0,96},{16,112},{32,64},{48,80},{64,32},{80,48},{96,0},{112,16},{1... | collective-permute-start | bytes 835592 | tf_op jit(solution)/shard_map/ppermute | solution.py:434
  46.3 6.6 %collective-permute-start.10 = (bf16[448,128]{1,0:T(8,128)(2,1)S(1)}, bf16[448,128]{1,0:T(8,128)(2,1)S(1)}, u32[]{:S(2)}, u32[]{:S(2)}) collective-permute-start(bf16[448,128]{1,0:T(8,128)(2,1)S(1)} %shard_map.79.own_ref), channel_id=1, source_target_pairs={{0,4},{1,5},{2,6},{3,7},{4,0},{5,1},{6,2},{7,3},{8,12},{9,13},{10,... | collective-permute-start | bytes 344072 | tf_op jit(solution)/shard_map/ppermute | solution.py:450
  46.3 8.9 %collective-permute-start.11 = (bf16[448,128]{1,0:T(8,128)(2,1)S(1)}, bf16[448,128]{1,0:T(8,128)(2,1)S(1)}, u32[]{:S(2)}, u32[]{:S(2)}) collective-permute-start(bf16[448,128]{1,0:T(8,128)(2,1)S(1)} %shard_map.79.own_ref), channel_id=1, source_target_pairs={{0,2},{1,3},{2,4},{3,5},{4,6},{5,7},{6,0},{7,1},{8,10},{9,11},{10,... | collective-permute-start | bytes 344072 | tf_op jit(solution)/shard_map/ppermute | solution.py:450
  55.7 4.3 %collective-permute-start.20 = (bf16[448,128]{1,0:T(8,128)(2,1)S(1)}, bf16[448,128]{1,0:T(8,128)(2,1)S(1)}, u32[]{:S(2)}, u32[]{:S(2)}) collective-permute-start(bf16[448,128]{1,0:T(8,128)(2,1)S(1)} %shard_map.80.own_ref.piece_ref), channel_id=1, source_target_pairs={{0,8},{1,9},{2,10},{3,11},{4,12},{5,13},{6,14},{7,15},{8,0},{9,1},... | collective-permute-start | bytes 344072 | tf_op jit(solution)/shard_map/ppermute | solution.py:470
  57.4 6.3 %collective-permute-start.19 = (bf16[32,2176]{1,0:T(8,128)(2,1)S(1)}, bf16[32,2176]{1,0:T(8,128)(2,1)S(1)}, u32[]{:S(2)}, u32[]{:S(2)}) collective-permute-start(bf16[32,2176]{1,0:T(8,128)(2,1)S(1)} %get-tuple-element.41), channel_id=1, source_target_pairs={{0,16},{16,0},{32,48},{48,32},{64,80},{80,64},{96,112},{112,96},{1... | collective-permute-start | bytes 417800 | tf_op jit(solution)/shard_map/ppermute | solution.py:469
  59.0 4.7 %collective-permute-start.16 = (bf16[32,2176]{1,0:T(8,128)(2,1)S(1)}, bf16[32,2176]{1,0:T(8,128)(2,1)S(1)}, u32[]{:S(2)}, u32[]{:S(2)}) collective-permute-start(bf16[32,2176]{1,0:T(8,128)(2,1)S(1)} %get-tuple-element.39), channel_id=1, source_target_pairs={{0,32},{16,48},{32,0},{48,16},{64,96},{80,112},{96,64},{112,80},{1... | collective-permute-start | bytes 417800 | tf_op jit(solution)/shard_map/ppermute | solution.py:438
  59.1 4.6 %collective-permute-start.12 = (bf16[448,128]{1,0:T(8,128)(2,1)S(1)}, bf16[448,128]{1,0:T(8,128)(2,1)S(1)}, u32[]{:S(2)}, u32[]{:S(2)}) collective-permute-start(bf16[448,128]{1,0:T(8,128)(2,1)S(1)} %shard_map.80.own_ref.piece_ref), channel_id=1, source_target_pairs={{0,1},{1,0},{2,3},{3,2},{4,5},{5,4},{6,7},{7,6},{8,9},{9,8},{10,11... | collective-permute-start | bytes 344072 | tf_op jit(solution)/shard_map/ppermute | solution.py:471
  60.1 5.0 %collective-permute-start.21 = (bf16[448,128]{1,0:T(8,128)(2,1)S(1)}, bf16[448,128]{1,0:T(8,128)(2,1)S(1)}, u32[]{:S(2)}, u32[]{:S(2)}) collective-permute-start(bf16[448,128]{1,0:T(8,128)(2,1)S(1)} %collective-permute-done.20.own_ref), channel_id=1, source_target_pairs={{0,1},{1,0},{2,3},{3,2},{4,5},{5,4},{6,7},{7,6},{8,9},{9,8},{10,11... | collective-permute-start | bytes 344072 | tf_op jit(solution)/shard_map/ppermute | solution.py:472
